TPU v7x, 128 devices: a whole 4x4x4 slice. The times are simulated.
128 devices in a mesh: seq: 16 (over z_hi, x, core), tensor: 2 (over z_lo), dp: 4 (over y).
Axes of the slice: x: 4, y: 4, z: 4 (z_hi: 2, z_lo: 2; z = z_hi * 2 + z_lo), core: 2. Of those that a mesh axis runs over, the one named last changes fastest.
Arguments:
- section_input: bfloat16 [4, 4096, 1280], P('dp', 'seq'), may hold values from -6 to 6
- conv_weight: bfloat16 [1280, 5, 1536], P('seq', None, 'tensor'), may hold values from -0.078125 to 0.078125
- head_weight: bfloat16 [1536, 3, 768], P('seq', None, 'tensor'), as said below
- output_weight: bfloat16 [1536, 768], P('seq', 'tensor'), may hold values from -0.21875 to 0.21875
- cotangent: bfloat16 [4, 2048, 1536], P('dp', 'seq', 'tensor'), may hold values from -6 to 6
Outputs:
- block_out: bfloat16 [4, 2048, 1536], P('dp', 'seq', 'tensor')
- conv_grad: float32 [1280, 5, 1536], P(('seq', 'dp'), None, 'tensor')
- head_grad: float32 [1536, 3, 768], P(('seq', 'dp'), None, 'tensor')
- output_grad: float32 [1536, 768], P(('seq', 'dp'), 'tensor')
Inputs may be any that keep to these rules, and one draw needn't show every extreme that they name: `head_weight`: finite projection weights whose deviation lies between about 1.7 and some 25 times 1536 to the minus one half.
All inputs are finite; a program needn't handle non-finite values.
Results may differ from a plain program's by a relative error of at most 0.023.
Values may be sent and summed in bfloat16 or wider, within the bound.
A program may use at most 128 MiB of HBM per device.

v0:
```python
import jax
import jax.numpy as jnp
from jax import lax
from jax.sharding import PartitionSpec as P

HEAD_DIM = 192


epsilon = 1e-06


def extended(block, sides, width):
    for axis, dim in sides:
        count = lax.axis_size(axis)
        forward = [(i, i + 1) for i in range(count - 1)]
        backward = [(target, source) for source, target in forward]
        low = lax.ppermute(
            lax.slice_in_dim(block, block.shape[dim] - width, None, axis=dim), axis, forward
        )
        high = lax.ppermute(lax.slice_in_dim(block, 0, width, axis=dim), axis, backward)
        block = jnp.concatenate([low, block, high], axis=dim)
    return block


def head_split(matrix):
    return matrix.reshape(matrix.shape[0], matrix.shape[1] // HEAD_DIM, HEAD_DIM)


def paired_product(window_rows, pool_rows):
    bins_here = pool_rows.shape[0]
    pairs = window_rows.reshape(bins_here, 2, window_rows.shape[1])
    even_part = jnp.einsum("bi,bo->io", pairs[:, 0], pool_rows, preferred_element_type=jnp.float32)
    odd_part = jnp.einsum("bi,bo->io", pairs[:, 1], pool_rows, preferred_element_type=jnp.float32)
    return even_part + odd_part


def local(section_input, conv_weight, head_weight, output_weight, cotangent):
    score_scale = HEAD_DIM ** (-0.5)
    activity = jax.nn.gelu(section_input[0].astype(jnp.float32), approximate=True).astype(
        jnp.bfloat16
    )
    positions = activity.shape[0]
    tap_count = conv_weight.shape[1]
    margin = tap_count // 2
    local_width = conv_weight.shape[2]
    padded = extended(activity, (("seq", 0),), margin)
    running = jnp.zeros((positions, local_width), jnp.float32)
    pieces = lax.all_gather(conv_weight, "seq", axis=0, tiled=True)
    for tap_index in range(tap_count):
        running = running + jnp.dot(
            padded[tap_index : tap_index + positions],
            pieces[:, tap_index],
            preferred_element_type=jnp.float32,
        )
    section_local = ((running[0::2] + running[1::2]) * 0.5).astype(jnp.bfloat16)
    section_full = lax.all_gather(section_local, "tensor", axis=1, tiled=True)
    section_float = section_full.astype(jnp.float32)
    inverse = lax.rsqrt(jnp.mean(section_float * section_float, axis=-1, keepdims=True) + epsilon)
    normed = (section_float * inverse).astype(jnp.bfloat16)
    head_full, output_full = (
        lax.all_gather(head_weight, "seq", axis=0, tiled=True),
        lax.all_gather(output_weight, "seq", axis=0, tiled=True),
    )
    projected = jnp.einsum(
        "bc,cje->bje", normed, head_full, preferred_element_type=jnp.float32
    ).astype(jnp.bfloat16)
    query_rows = projected[:, 0]
    key_local = projected[:, 1]
    value_local = projected[:, 2]
    key_all, value_all = (
        lax.all_gather(key_local, "seq", axis=0, tiled=True),
        lax.all_gather(value_local, "seq", axis=0, tiled=True),
    )
    query_heads = head_split(query_rows)
    key_heads = head_split(key_all)
    value_heads = head_split(value_all)
    scores = (
        jnp.einsum("qhd,khd->hqk", query_heads, key_heads, preferred_element_type=jnp.float32)
        * score_scale
    )
    highest = jnp.max(scores, axis=-1, keepdims=True)
    unnormed = jnp.exp(scores - highest)
    totals = jnp.sum(unnormed, axis=-1, keepdims=True)
    weights = unnormed / totals
    rounded = weights.astype(jnp.bfloat16)
    attended = jnp.einsum(
        "hqk,khd->qhd", rounded, value_heads, preferred_element_type=jnp.float32
    ).astype(jnp.bfloat16)
    rows_here = query_rows.shape[0]
    inner_local = query_rows.shape[1]
    attended = attended.reshape(rows_here, inner_local)
    partial_out = jnp.einsum("be,ce->bc", attended, output_full, preferred_element_type=jnp.float32)
    projected_out = lax.psum_scatter(
        partial_out.astype(jnp.bfloat16), "tensor", scatter_dimension=1, tiled=True
    ).astype(jnp.float32)
    block_out = (section_local.astype(jnp.float32) + projected_out).astype(jnp.bfloat16)
    grad_full = lax.all_gather(cotangent[0], "tensor", axis=1, tiled=True)
    grad_att = jnp.einsum(
        "bc,ce->be", grad_full, output_full, preferred_element_type=jnp.float32
    ).astype(jnp.bfloat16)
    grad_heads_att = head_split(grad_att)
    grad_prob = jnp.einsum(
        "qhd,khd->hqk", grad_heads_att, value_heads, preferred_element_type=jnp.float32
    )
    centre = jnp.sum(weights * grad_prob, axis=-1, keepdims=True)
    grad_score = (weights * (grad_prob - centre)).astype(jnp.bfloat16)
    grad_query = (
        jnp.einsum("hqk,khd->qhd", grad_score, key_heads, preferred_element_type=jnp.float32)
        * score_scale
    ).astype(jnp.bfloat16)
    key_part = (
        jnp.einsum("hqk,qhd->khd", grad_score, query_heads, preferred_element_type=jnp.float32)
        * score_scale
    )
    value_part = jnp.einsum(
        "hqk,qhd->khd", rounded, grad_heads_att, preferred_element_type=jnp.float32
    )
    summed = lax.psum_scatter(
        jnp.concatenate(
            [
                key_part.reshape(lax.axis_size("seq") * rows_here, inner_local),
                value_part.reshape(lax.axis_size("seq") * rows_here, inner_local),
            ],
            axis=1,
        ).astype(jnp.bfloat16),
        "seq",
        scatter_dimension=0,
        tiled=True,
    ).astype(jnp.float32)
    grad_key = summed[:, :inner_local].astype(jnp.bfloat16)
    grad_value = summed[:, inner_local:].astype(jnp.bfloat16)
    grad_proj = jnp.stack(
        [grad_query.reshape(rows_here, inner_local), grad_key, grad_value], axis=1
    )
    normed_partial = jnp.einsum(
        "bje,cje->bc", grad_proj, head_full, preferred_element_type=jnp.float32
    )
    grad_normed = lax.psum(normed_partial.astype(jnp.bfloat16), "tensor").astype(jnp.float32)
    spread = jnp.mean(grad_normed * section_float, axis=-1, keepdims=True)
    lower_edge = lax.axis_index("tensor") * local_width
    normed_slice = lax.dynamic_slice_in_dim(grad_normed, lower_edge, local_width, 1)
    grad_section = (
        cotangent[0].astype(jnp.float32)
        + inverse * normed_slice
        - inverse**3 * section_local.astype(jnp.float32) * spread
    )
    grad_pool = (0.5 * grad_section).astype(jnp.bfloat16)
    activity_part, normed_part, cotangent_part = (
        lax.all_to_all(activity, "seq", split_axis=1, concat_axis=0, tiled=True),
        lax.all_to_all(normed, "seq", split_axis=1, concat_axis=0, tiled=True),
        lax.all_to_all(grad_full, "seq", split_axis=1, concat_axis=0, tiled=True),
    )
    activity_padded = jnp.pad(activity_part, ((margin, margin), (0, 0)))
    pieces = lax.all_gather(grad_pool, "seq", axis=0, tiled=True)
    amount = pieces.shape[0]
    term_list = [
        paired_product(activity_padded[tap_index : tap_index + 2 * amount], pieces)
        for tap_index in range(tap_count)
    ]
    conv_rows_grad = jnp.stack(term_list, axis=1)
    pieces = (
        lax.all_gather(grad_proj, "seq", axis=0, tiled=True),
        lax.all_gather(attended, "seq", axis=0, tiled=True),
    )
    head_sum = jnp.einsum("bc,bje->cje", normed_part, pieces[0], preferred_element_type=jnp.float32)
    output_sum = jnp.einsum(
        "bc,be->ce", cotangent_part, pieces[1], preferred_element_type=jnp.float32
    )
    conv_grad, head_grad, output_grad = (
        lax.psum_scatter(
            conv_rows_grad.astype(jnp.bfloat16), "dp", scatter_dimension=0, tiled=True
        ).astype(jnp.float32),
        lax.psum_scatter(
            head_sum.astype(jnp.bfloat16), "dp", scatter_dimension=0, tiled=True
        ).astype(jnp.float32),
        lax.psum_scatter(
            output_sum.astype(jnp.bfloat16), "dp", scatter_dimension=0, tiled=True
        ).astype(jnp.float32),
    )
    return (block_out[None], conv_grad, head_grad, output_grad)


def solution(mesh):
    placed = (
        P("dp", "seq", None),
        P("seq", None, "tensor"),
        P("seq", None, "tensor"),
        P("seq", "tensor"),
        P("dp", "seq", "tensor"),
    )
    return jax.shard_map(
        local,
        mesh=mesh,
        in_specs=placed,
        out_specs=(
            P("dp", "seq", "tensor"),
            P(("seq", "dp"), None, "tensor"),
            P(("seq", "dp"), None, "tensor"),
            P(("seq", "dp"), "tensor"),
        ),
        check_vma=False,
    )
```

profile of v0, /device:TPU:1, one launch (start us, length us, event | category | flops | bytes accessed | tf_op | source)
XLA Modules:
  0.0 674.3 jit_solution(18366352381718251712)
XLA Ops:
  10.7 4.5 collective-permute-start
  17.2 76.9 %all-gather.12.cloned.1.call-done = bf16[1280,5,768]{2,0,1:T(8,128)(2,1)} async-done(((bf16[80,5,768]{2,0,1:T(8,128)(2,1)}), bf16[1280,5,768]{2,0,1:T(8,128)(2,1)}) %all-gather.12.cloned.1.call-update) | async-done | bytes 9830416 | tf_op jit(solution)/shard_map/all_gather | solution.py:48
  96.6 3.1 fusion.5
  103.6 9.9 %all_gather.31 = bf16[128,1536]{1,0:T(8,128)(2,1)S(1)} all-gather(bf16[128,768]{1,0:T(8,128)(2,1)S(1)} %multiply_convert_fusion.2), channel_id=1, replica_groups=mesh['seq'=16,'tensor'=2,'dp'=4] {'tensor'}, dimensions={1}, use_global_device_ids=true | all-gather | bytes 589824 | tf_op jit(solution)/shard_map/all_gather | solution.py:56
  114.4 35.1 %all-gather.14.cloned.1.call-done = bf16[1536,3,384]{2,0,1:T(8,128)(2,1)} async-done(((bf16[96,3,384]{2,0,1:T(8,128)(2,1)}), bf16[1536,3,384]{2,0,1:T(8,128)(2,1)}) %all-gather.14.cloned.1.call-update) | async-done | bytes 3538960 | tf_op jit(solution)/shard_map/all_gather | solution.py:61
  149.5 2.7 convolution_convert_fusion.2
  153.8 7.2 %all-gather.2 = bf16[1,128,1536]{1,2,0:T(8,128)(2,1)} all-gather(bf16[1,128,768]{1,2,0:T(8,128)(2,1)S(1)} %copy.80), channel_id=4, replica_groups=mesh['seq'=16,'tensor'=2,'dp'=4] {'tensor'}, dimensions={2}, use_global_device_ids=true | all-gather | bytes 589824 | tf_op jit(solution)/shard_map/all_gather | solution.py:97
  161.0 35.2 %all-gather.16.cloned.1.call-done = bf16[1536,384]{1,0:T(8,128)(2,1)} async-done(((bf16[96,384]{1,0:T(8,128)(2,1)}), bf16[1536,384]{1,0:T(8,128)(2,1)}) %all-gather.16.cloned.1.call-update) | async-done | bytes 1179664 | tf_op jit(solution)/shard_map/all_gather | solution.py:62
  198.3 46.3 %all-gather.26.cloned.1.call-done = bf16[2048,1,384]{2,0,1:T(8,128)(2,1)} async-done(((bf16[128,1,384]{2,0,1:T(8,128)(2,1)}), bf16[2048,1,384]{2,0,1:T(8,128)(2,1)}) %all-gather.26.cloned.1.call-update) | async-done | bytes 1572880 | tf_op jit(solution)/shard_map/all_gather | solution.py:71
  244.5 2.7 copy.76
  251.4 41.5 %all-gather.24.cloned.1.call-done = bf16[2048,1,384]{2,0,1:T(8,128)(2,1)} async-done(((bf16[128,1,384]{2,0,1:T(8,128)(2,1)}), bf16[2048,1,384]{2,0,1:T(8,128)(2,1)}) %all-gather.24.cloned.1.call-update) | async-done | bytes 1572880 | tf_op jit(solution)/shard_map/all_gather | solution.py:72
  292.9 2.6 copy.74
  303.6 3.1 fusion.42
  308.3 67.8 %reduce-scatter.10.cloned.1.call-done = bf16[128,768]{1,0:T(8,128)(2,1)} async-done(((bf16[2048,768]{1,0:T(8,128)(2,1)}), bf16[128,768]{1,0:T(8,128)(2,1)}) %reduce-scatter.10.cloned.1.call-update) | async-done | bytes 196624 | tf_op jit(solution)/shard_map/reduce_scatter | solution.py:118
  377.7 2.9 fusion.3
  380.8 2.8 convolution_convert_fusion.5
  385.7 27.4 %all-reduce.8.cloned.1.call-done = bf16[128,1536]{1,0:T(8,128)(2,1)} async-done(((bf16[128,1536]{1,0:T(8,128)(2,1)}), bf16[128,1536]{1,0:T(8,128)(2,1)}) %all-reduce.8.cloned.1.call-update) | async-done | bytes 393232 | tf_op jit(solution)/shard_map/psum | solution.py:138
  415.4 16.9 %reduce-scatter.8.cloned.1.call-done = bf16[128,768]{1,0:T(8,128)(2,1)} async-done(((bf16[128,1536]{1,0:T(8,128)(2,1)}), bf16[128,768]{1,0:T(8,128)(2,1)}) %reduce-scatter.8.cloned.1.call-update) | async-done | bytes 196624 | tf_op jit(solution)/shard_map/reduce_scatter | solution.py:93
  435.5 21.2 %all_to_all.54 = bf16[256,16,80]{0,2,1:T(8,128)(2,1)S(1)} all-to-all(bf16[256,16,80]{0,2,1:T(8,128)(2,1)S(1)} %fusion.32), channel_id=1, replica_groups=mesh['seq'=16,'tensor'=2,'dp'=4] {'seq'}, dimensions={1} | all-to-all | bytes 1310720 | tf_op jit(solution)/shard_map/all_to_all | solution.py:149
  461.6 3.4 copy.79
  469.8 3.4 copy.87
  483.0 3.9 all-to-all-start.1
  493.5 3.3 all-to-all-done.1
  496.9 5.0 all-to-all-start.2
  506.1 6.0 all-to-all-done.2
  512.1 2.7 fusion.53
  515.1 23.7 %all-gather.18.cloned.1.call-done = bf16[2048,768]{1,0:T(8,128)(2,1)} async-done(((bf16[128,768]{1,0:T(8,128)(2,1)}), bf16[2048,768]{1,0:T(8,128)(2,1)}) %all-gather.18.cloned.1.call-update) | async-done | bytes 3145744 | tf_op jit(solution)/shard_map/all_gather | solution.py:154
  538.8 2.7 fusion.93
  549.8 48.1 %all-gather.20.cloned.1.call-done = bf16[2048,3,384]{2,0,1:T(8,128)(2,1)} async-done(((bf16[128,3,384]{2,0,1:T(8,128)(2,1)}), bf16[2048,3,384]{2,0,1:T(8,128)(2,1)}) %all-gather.20.cloned.1.call-update) | async-done | bytes 4718608 | tf_op jit(solution)/shard_map/all_gather | solution.py:162
  597.9 3.9 convolution_convert_fusion.3
  603.7 13.1 %reduce-scatter.12.cloned.1.call-done = bf16[24,384]{1,0:T(8,128)(2,1)} async-done(((bf16[96,384]{1,0:T(8,128)(2,1)}), bf16[24,384]{1,0:T(8,128)(2,1)}) %reduce-scatter.12.cloned.1.call-update) | async-done | bytes 18448
  618.2 46.4 %all-reduce.10.cloned.1.call-done = (bf16[80,5,768]{2,0,1:T(8,128)(2,1)}, bf16[96,3,384]{2,0,1:T(8,128)(2,1)}) async-done(((bf16[80,5,768]{2,0,1:T(8,128)(2,1)}, bf16[96,3,384]{2,0,1:T(8,128)(2,1)}), (bf16[80,5,768]{2,0,1:T(8,128)(2,1)}, bf16[96,3,384]{2,0,1:T(8,128)(2,1)})) %all-reduce.10.cloned.1.call-update) | async-done | bytes 835600
  (167 shorter events, 83.0 us)
Async XLA Ops:
  7.2 86.9 %all-gather.12.cloned.1.call-start = ((), (), s32[]{:S(2)}) async-start(), calls=%async_computation.6 | async-start | bytes 10444800 | tf_op jit(solution)/shard_map/all_gather | solution.py:48
  7.9 141.7 %all-gather.14.cloned.1.call-start = ((), (), s32[]{:S(2)}) async-start(), calls=%async_computation.7 | async-start | bytes 3760128 | tf_op jit(solution)/shard_map/all_gather | solution.py:61
  8.6 187.6 %all-gather.16.cloned.1.call-start = ((), (), s32[]{:S(2)}) async-start(), calls=%async_computation.8 | async-start | bytes 1253376 | tf_op jit(solution)/shard_map/all_gather | solution.py:62
  10.0 86.6 %copy-start.5 = (bf16[1,256,1280]{1,2,0:T(8,128)(2,1)}, bf16[1,256,1280]{1,2,0:T(8,128)(2,1)S(1)}, u32[]{:S(2)}) copy-start(bf16[1,256,1280]{1,2,0:T(8,128)(2,1)S(1)} %copy.73) | copy-start | bytes 1966084
  10.7 90.1 %collective-permute-start = (bf16[2,1280]{0,1:T(8,128)(2,1)S(1)}, bf16[2,1280]{0,1:T(8,128)(2,1)S(1)}, u32[]{:S(2)}, u32[]{:S(2)}) collective-permute-start(bf16[2,1280]{0,1:T(8,128)(2,1)S(1)} %get-tuple-element.20), channel_id=1, source_target_pairs={{0,8},{8,16},{16,24},{24,32},{32,40},{40,48},{48,56},{56,64},{64,7... | collective-permute-start | bytes 15368 | tf_op jit(solution)/shard_map/ppermute | solution.py:17
  15.2 81.4 %collective-permute-start.1 = (bf16[2,1280]{0,1:T(8,128)(2,1)S(1)}, bf16[2,1280]{0,1:T(8,128)(2,1)S(1)}, u32[]{:S(2)}, u32[]{:S(2)}) collective-permute-start(bf16[2,1280]{0,1:T(8,128)(2,1)S(1)} %get-tuple-element.21), channel_id=1, source_target_pairs={{8,0},{16,8},{24,16},{32,24},{40,32},{48,40},{56,48},{64,56},{72,6... | collective-permute-start | bytes 15368 | tf_op jit(solution)/shard_map/ppermute | solution.py:20
  17.1 227.4 %all-gather.26.cloned.1.call-start = ((), (), s32[]{:S(2)}) async-start(), calls=%async_computation.16 | async-start | bytes 1671168 | tf_op jit(solution)/shard_map/all_gather | solution.py:71
  114.4 37.8 %copy-start.9 = (bf16[128,1536]{1,0:T(8,128)(2,1)}, bf16[128,1536]{1,0:T(8,128)(2,1)S(1)}, u32[]{:S(2)}) copy-start(bf16[128,1536]{1,0:T(8,128)(2,1)S(1)} %fusion.55) | copy-start | bytes 1179652
  114.4 39.2 %copy-start.29 = (bf16[1,128,768]{2,1,0:T(8,128)(2,1)S(1)}, bf16[1,128,768]{2,1,0:T(8,128)(2,1)}, u32[]{:S(2)}) copy-start(bf16[1,128,768]{2,1,0:T(8,128)(2,1)} %param.9) | copy-start | bytes 589828
  153.0 139.9 %all-gather.24.cloned.1.call-start = ((), (), s32[]{:S(2)}) async-start(), calls=%async_computation.15 | async-start | bytes 1671168 | tf_op jit(solution)/shard_map/all_gather | solution.py:72
  153.6 222.5 %reduce-scatter.10.cloned.1.call-start = ((), (), s32[]{:S(2)}) async-start(), calls=%async_computation.10 | async-start | bytes 3342336 | tf_op jit(solution)/shard_map/reduce_scatter | solution.py:118
  249.5 48.1 %copy-start.2 = (f32[2,128,2048]{2,1,0:T(8,128)}, f32[2,128,2048]{2,1,0:T(8,128)S(1)}, u32[]{:S(2)}) copy-start(f32[2,128,2048]{2,1,0:T(8,128)S(1)} %get-tuple-element.32) | copy-start | bytes 6291460
  303.5 74.2 %copy-start.1 = (bf16[1536,3,384]{2,0,1:T(8,128)(2,1)S(1)}, bf16[1536,3,384]{2,0,1:T(8,128)(2,1)}, u32[]{:S(2)}) copy-start(bf16[1536,3,384]{2,0,1:T(8,128)(2,1)} %all-gather.14.cloned.1.call-done) | copy-start | bytes 10616836
  303.6 109.6 %all-reduce.8.cloned.1.call-start = ((), (), s32[]{:S(2)}) async-start(), calls=%async_computation.11 | async-start | bytes 786432 | tf_op jit(solution)/shard_map/psum | solution.py:138
  380.7 51.6 %reduce-scatter.8.cloned.1.call-start = ((), (), s32[]{:S(2)}) async-start(), calls=%async_computation.9 | async-start | bytes 589824 | tf_op jit(solution)/shard_map/reduce_scatter | solution.py:93
  383.6 30.7 %copy-start.4 = (bf16[128,1536]{1,0:T(8,128)(2,1)S(1)}, bf16[128,1536]{1,0:T(8,128)(2,1)}, u32[]{:S(2)}) copy-start(bf16[128,1536]{1,0:T(8,128)(2,1)} %copy-done.3) | copy-start | bytes 1179652
  383.6 48.7 %copy-start.13 = (bf16[128,768]{1,0:T(8,128)(2,1)S(1)}, bf16[128,768]{1,0:T(8,128)(2,1)}, u32[]{:S(2)}) copy-start(bf16[128,768]{1,0:T(8,128)(2,1)} %copy-done.12) | copy-start | bytes 589828
  383.6 48.7 %copy-start.30 = (bf16[1,128,768]{2,1,0:T(8,128)(2,1)S(1)}, bf16[1,128,768]{2,1,0:T(8,128)(2,1)}, u32[]{:S(2)}) copy-start(bf16[1,128,768]{2,1,0:T(8,128)(2,1)} %param.9) | copy-start | bytes 589828
  384.9 49.4 %copy-start.23 = (bf16[128,1,384]{2,0,1:T(8,128)(2,1)S(1)}, bf16[128,1,384]{2,0,1:T(8,128)(2,1)}, u32[]{:S(2)}) copy-start(bf16[128,1,384]{2,0,1:T(8,128)(2,1)} %copy.84) | copy-start | bytes 294916
  384.9 49.4 %copy-start.25 = (bf16[128,1,384]{2,0,1:T(8,128)(2,1)S(1)}, bf16[128,1,384]{2,0,1:T(8,128)(2,1)}, u32[]{:S(2)}) copy-start(bf16[128,1,384]{2,0,1:T(8,128)(2,1)} %copy-done.24) | copy-start | bytes 294916
  384.9 49.4 %copy-start.27 = (bf16[128,1,384]{2,0,1:T(8,128)(2,1)S(1)}, bf16[128,1,384]{2,0,1:T(8,128)(2,1)}, u32[]{:S(2)}) copy-start(bf16[128,1,384]{2,0,1:T(8,128)(2,1)} %copy-done.26) | copy-start | bytes 294916
  384.9 127.1 %all-gather.22.cloned.1.call-start = ((), (), s32[]{:S(2)}) async-start(), calls=%async_computation.14 | async-start | bytes 1671168 | tf_op jit(solution)/shard_map/all_gather | solution.py:163
  385.7 153.2 %all-gather.18.cloned.1.call-start = ((), (), s32[]{:S(2)}) async-start(), calls=%async_computation.12 | async-start | bytes 3342336 | tf_op jit(solution)/shard_map/all_gather | solution.py:154
  385.7 49.4 %copy-start.6 = (bf16[1,256,1280]{1,2,0:T(8,128)(2,1)S(1)}, bf16[1,256,1280]{1,2,0:T(8,128)(2,1)}, u32[]{:S(2)}) copy-start(bf16[1,256,1280]{1,2,0:T(8,128)(2,1)} %copy-done.5) | copy-start | bytes 1966084
  434.2 163.7 %all-gather.20.cloned.1.call-start = ((), (), s32[]{:S(2)}) async-start(), calls=%async_computation.13 | async-start | bytes 5013504 | tf_op jit(solution)/shard_map/all_gather | solution.py:162
  483.0 13.8 %all-to-all-start.1 = ((bf16[128,16,96]{0,2,1:T(8,128)(2,1)}), bf16[128,16,96]{0,2,1:T(8,128)(2,1)S(1)}, u32[]{:S(2)}, u32[]{:S(2)}) async-start(bf16[128,16,96]{0,2,1:T(8,128)(2,1)} %bitcast.48), calls=%async_computation.3 | async-start | bytes 786432 | tf_op jit(solution)/shard_map/all_to_all | solution.py:150
  496.9 15.2 %all-to-all-start.2 = ((bf16[128,16,96]{0,2,1:T(8,128)(2,1)}), bf16[128,16,96]{0,2,1:T(8,128)(2,1)}, u32[]{:S(2)}, u32[]{:S(2)}) async-start(bf16[128,16,96]{0,2,1:T(8,128)(2,1)} %bitcast.51), calls=%async_computation.4 | async-start | bytes 786432 | tf_op jit(solution)/shard_map/all_to_all | solution.py:151
  501.8 115.0 %reduce-scatter.12.cloned.1.call-start = ((), (), s32[]{:S(2)}) async-start(), calls=%async_computation.17 | async-start | bytes 92160
  505.7 33.1 %copy-start.14 = (bf16[2048,1,80]{0,2,1:T(8,128)(2,1)S(1)}, bf16[2048,1,80]{0,2,1:T(8,128)(2,1)}, u32[]{:S(2)}) copy-start(bf16[2048,1,80]{0,2,1:T(8,128)(2,1)} %copy.79) | copy-start | bytes 983044
  514.8 149.8 %all-reduce.10.cloned.1.call-start = ((), (), s32[]{:S(2)}) async-start(), calls=%async_computation.18 | async-start | bytes 1671168
  549.8 52.0 %copy-start.28 = (bf16[80,5,768]{2,0,1:T(8,128)(2,1)}, bf16[80,5,768]{2,0,1:T(8,128)(2,1)S(1)}, u32[]{:S(2)}) copy-start(bf16[80,5,768]{2,0,1:T(8,128)(2,1)S(1)} %fusion.44) | copy-start | bytes 1843204
  549.8 52.1 %copy-start.32 = (u32[128]{0:T(128)S(1)}, u32[128]{0:T(128)}, u32[]{:S(2)}) copy-start(u32[128]{0:T(128)} %constant.43) | copy-start | bytes 1540
  (18 other events, 64.5 us)
Sparse Core Ops, SparseCore 0:
  10.5 83.5 all-gather.11
  96.6 52.9 all-gather.13
  152.0 44.1 all-gather.15
  199.1 45.3 all-gather.25
  247.4 45.4 all-gather.23
  303.7 72.3 reduce-scatter.9
  380.8 32.2 all-reduce.7
  415.6 16.6 reduce-scatter.7
  434.6 50.0 all-gather.21
  487.0 51.7 all-gather.17
  541.3 56.5 all-gather.19
  600.7 16.1 reduce-scatter.11
  620.0 44.5 all-reduce.9
where the time goes:
time: 677 us; the launch traced here: 674 us
  waiting for transfers between devices  491 us (73%)
  local copies, waits for them, and re-layouts  55.7 us (8%)
  matrix products  45 us (7%)
  blocking collectives  38.3 us (6%)
  starting transfers between devices  16.1 us (2%)
  between operations  15.8 us (2%)
  other arithmetic  12.9 us (2%)
    all_gather x1, waiting for transfers between devices, local(): pieces = lax.all_gather(conv_weight, 'seq', axis=0, tiled=True)  76.9 us
    reduce_scatter x1, waiting for transfers between devices, local(): lax.psum_scatter(jnp.concatenate([key_part.reshape(lax.axis_size('seq') *...  67.8 us
    unnamed x15, waiting for transfers between devices  62.3 us
    all_gather x1, waiting for transfers between devices, local(): lax.all_gather(grad_proj, 'seq', axis=0, tiled=True)  48.1 us
    all_gather x1, waiting for transfers between devices, local(): lax.all_gather(key_local, 'seq', axis=0, tiled=True)  46.3 us
    all_gather x1, waiting for transfers between devices, local(): lax.all_gather(value_local, 'seq', axis=0, tiled=True)  41.5 us
    all_gather x1, waiting for transfers between devices, local(): lax.all_gather(output_weight, 'seq', axis=0, tiled=True)  35.2 us
    all_gather x1, waiting for transfers between devices, local(): lax.all_gather(head_weight, 'seq', axis=0, tiled=True)  35.1 us
  transfers between devices with their start and end apart: 17, of which 14 were waited for; matrix products, arithmetic and copies ran while one was open for 14% of the time, Pallas kernels for 0%

commit v1 on v0

v1 whole, which is shorter than its diff:
```python
import functools

import jax
import jax.numpy as jnp
from jax import lax
from jax.experimental import pallas as pl
from jax.experimental.pallas import tpu as pltpu
from jax.sharding import PartitionSpec as P

HEAD_DIM = 192
EPSILON = 1e-06
MESH = pl.DeviceIdType.MESH
BF16 = jnp.bfloat16
F32 = jnp.float32


def place():
    seq = lax.axis_index("seq")
    return seq, lax.div(seq, 2), lax.rem(seq, 2), lax.axis_index("tensor"), lax.axis_index("dp")


def device(seq, tensor, dp):
    return {"seq": seq, "tensor": tensor, "dp": dp}


def remote(src, dst, send, recv, target):
    return pltpu.make_async_remote_copy(
        src_ref=src, dst_ref=dst, send_sem=send, recv_sem=recv, device_id=target, device_id_type=MESH
    )


def greet(targets):
    barrier = pltpu.get_barrier_semaphore()
    for condition, target in targets:
        if condition is None:
            pl.semaphore_signal(barrier, inc=1, device_id=target, device_id_type=MESH)
        else:

            @pl.when(condition)
            def _(target=target):
                pl.semaphore_signal(barrier, inc=1, device_id=target, device_id_type=MESH)

    return barrier


def under(condition, action):
    if condition is None:
        action()
    else:

        @pl.when(condition)
        def _():
            action()


def communicate(kernel, collective, outputs, semaphores, *operands):
    anywhere = pl.BlockSpec(memory_space=pl.ANY)
    return pl.pallas_call(
        kernel,
        out_shape=outputs,
        in_specs=[anywhere] * len(operands),
        out_specs=tuple([anywhere] * len(outputs)),
        scratch_shapes=[pltpu.SemaphoreType.DMA((count,)) for count in semaphores],
        compiler_params=pltpu.CompilerParams(collective_id=collective, has_side_effects=True),
    )(*operands)


def half_sends(items, s, j, c, t, d, src_of, dst, send, recv, local):
    zh, m = lax.div(s, 8), lax.rem(s, 8)
    for k in range(8):
        chip = lax.rem(j + k, 8)
        target = 2 * chip + zh
        src = src_of(chip)
        copy = remote(src, dst(m), send.at[k], recv.at[m], device(target, t, d))
        if k == 0:
            items.append((c != zh, copy.start, copy.wait_send))
            own = pltpu.make_async_copy(src, dst(m), local)
            items.append((c == zh, own.start, own.wait))
        else:
            items.append((None, copy.start, copy.wait_send))
    waits = []
    for n in range(8):
        copy = remote(dst(n), dst(n), send.at[0], recv.at[n], device(s, t, d))
        waits.append((8 * c + n != s, copy.wait_recv))
    return waits


def start_kernel(at_ref, cw_ref, wp_ref, cot_ref, xt_ref, halo_ref, cwf_ref, wq_ref, cots_ref,
                 at_send, at_recv, halo_send, halo_recv, w_send, w_recv, q_send, q_recv, c_send, c_recv, local):
    s, j, c, t, d = place()
    zh = lax.div(s, 8)
    peers = [(None, device(lax.rem(s + k, 16), t, d)) for k in range(1, 16)]
    peers += [(None, device(2 * j + other, 1 - t, d)) for other in range(2)]
    barrier = greet(peers)
    items, waits = [], []
    pl.semaphore_wait(barrier, 17)

    waits += half_sends(
        items, s, j, c, t, d,
        lambda chip: at_ref.at[chip],
        lambda slot: xt_ref.at[:, :, pl.ds(pl.multiple_of(slot * 128, 128), 128)],
        at_send, at_recv, local.at[0],
    )
    edge = jnp.logical_or(s == 7, s == 8)
    for k in range(8):
        chip = lax.rem(j + k, 8)
        target = 2 * chip + 1 - zh
        copy = remote(at_ref.at[chip], halo_ref, halo_send.at[k], halo_recv.at[0], device(target, t, d))
        if k == 0:
            alone = c == 1 - zh
            own = pltpu.make_async_copy(at_ref.at[chip], halo_ref, local.at[1])
            items.append((jnp.logical_and(edge, jnp.logical_not(alone)), copy.start, copy.wait_send))
            items.append((jnp.logical_and(edge, alone), own.start, own.wait))
        else:
            items.append((edge, copy.start, copy.wait_send))
    halo_source = 8 - c
    halo_copy = remote(halo_ref, halo_ref, halo_send.at[0], halo_recv.at[0], device(s, t, d))
    waits.append((halo_source != s, halo_copy.wait_recv))
    mine = cwf_ref.at[:, pl.ds(pl.multiple_of(c * 80, 16), 80), :]
    copy = remote(cw_ref, mine, c_send.at[0], c_recv.at[0], device(2 * j + 1 - c, t, d))
    items.append((None, copy.start, copy.wait_send))
    waits.append((None, copy.wait_recv))
    own = pltpu.make_async_copy(cw_ref, mine, local.at[2])
    items.append((None, own.start, own.wait))
    for k in range(16):
        target = lax.rem(s + k, 16)
        src = wp_ref.at[lax.rem(target, 2), d]
        if k == 0:
            own = pltpu.make_async_copy(src, wq_ref.at[s], local.at[3])
            items.append((None, own.start, own.wait))
        else:
            copy = remote(src, wq_ref.at[s], w_send.at[k], w_recv.at[k], device(target, t, d))
            items.append((None, copy.start, copy.wait_send))
            waits.append((None, copy.wait_recv))
    quad_sends(items, waits, j, c, t, d, lambda cc, tt: cot_ref, cots_ref, q_send, q_recv, local.at[4])
    for condition, start, _ in items:
        under(condition, start)
    for condition, wait in waits:
        under(condition, wait)
    for condition, _, wait in items:
        under(condition, wait)


def quad_peers(j, c, t, d):
    index = 2 * c + t
    found = []
    for k in range(1, 4):
        other = lax.rem(index + k, 4)
        found.append((None, device(2 * j + lax.div(other, 2), lax.rem(other, 2), d)))
    return found


def quad_sends(items, waits, j, c, t, d, src_of, dst_ref, send, recv, local):
    index = 2 * c + t
    for k in range(4):
        other = lax.rem(index + k, 4)
        cc, tt = lax.div(other, 2), lax.rem(other, 2)
        src = src_of(cc, tt)
        if k == 0:
            own = pltpu.make_async_copy(src, dst_ref.at[c, t], local)
            items.append((None, own.start, own.wait))
        else:
            copy = remote(src, dst_ref.at[c, t], send.at[k], recv.at[k], device(2 * j + cc, tt, d))
            items.append((None, copy.start, copy.wait_send))
            waits.append((None, copy.wait_recv))


def settle(items, waits):
    for condition, start, _ in items:
        under(condition, start)
    for condition, wait in waits:
        under(condition, wait)
    for condition, _, wait in items:
        under(condition, wait)


def section_kernel(part_ref, wq_ref, rs_ref, wf_ref, send, recv, y_send, y_recv, local):
    s, j, c, t, d = place()
    zh = lax.div(s, 8)
    senders = []
    for k in range(8):
        target = device(2 * lax.rem(j + k, 8) + zh, t, d)
        senders.append((c != zh if k == 0 else None, target))
    senders += [(None, device(s, t, lax.rem(d + k, 4))) for k in range(1, 4)]
    barrier = greet(senders)
    pl.semaphore_wait(barrier, 11 - jnp.where(c == zh, 1, 0))
    items, waits = [], []
    m = lax.rem(s, 8)
    for k in range(8):
        slot = lax.rem(m + k, 8)
        target = 8 * c + slot
        copy = remote(part_ref.at[slot], rs_ref.at[j], send.at[k], recv.at[j], device(target, t, d))
        if k == 0:
            items.append((c != zh, copy.start, copy.wait_send))
            own = pltpu.make_async_copy(part_ref.at[slot], rs_ref.at[j], local.at[0])
            items.append((c == zh, own.start, own.wait))
        else:
            items.append((None, copy.start, copy.wait_send))
    for n in range(8):
        copy = remote(rs_ref.at[n], rs_ref.at[n], send.at[0], recv.at[n], device(s, t, d))
        waits.append((2 * n + zh != s, copy.wait_recv))
    own = pltpu.make_async_copy(wq_ref, wf_ref.at[:, d], local.at[1])
    items.append((None, own.start, own.wait))
    for k in range(1, 4):
        copy = remote(wq_ref, wf_ref.at[:, d], y_send.at[k], y_recv.at[k], device(s, t, lax.rem(d + k, 4)))
        items.append((None, copy.start, copy.wait_send))
        waits.append((None, copy.wait_recv))
    settle(items, waits)


def quad_kernel(count, *refs):
    s, j, c, t, d = place()
    ins, outs, sems = refs[:count], refs[count : 2 * count], refs[2 * count :]
    barrier = greet(quad_peers(j, c, t, d))
    pl.semaphore_wait(barrier, 3)
    items, waits = [], []
    for n in range(count):
        if len(ins[n].shape) == len(outs[n].shape):
            src_of = lambda cc, tt, n=n: ins[n].at[cc, tt]
        else:
            src_of = lambda cc, tt, n=n: ins[n]
        quad_sends(items, waits, j, c, t, d, src_of, outs[n], sems[3 * n], sems[3 * n + 1], sems[3 * n + 2].at[0])
    settle(items, waits)


def head_group_sends(items, waits, j, c, t, d, src_of, dst_ref, send, recv, local):
    for k in range(8):
        chip = lax.rem(j + k, 8)
        src = src_of(chip)
        if k == 0:
            own = pltpu.make_async_copy(src, dst_ref.at[j], local)
            items.append((None, own.start, own.wait))
        else:
            copy = remote(src, dst_ref.at[j], send.at[k], recv.at[k], device(2 * chip + c, t, d))
            items.append((None, copy.start, copy.wait_send))
            waits.append((None, copy.wait_recv))


def keys_kernel(kv_ref, all_ref, send, recv, local):
    s, j, c, t, d = place()
    barrier = greet([(None, device(2 * lax.rem(j + k, 8) + c, t, d)) for k in range(1, 8)])
    pl.semaphore_wait(barrier, 7)
    items, waits = [], []
    head_group_sends(items, waits, j, c, t, d, lambda chip: kv_ref, all_ref, send, recv, local.at[0])
    settle(items, waits)


def key_grads_kernel(dkv_ref, bo_ref, all_ref, bos_ref, send, recv, q_send, q_recv, local):
    s, j, c, t, d = place()
    peers = [(None, device(2 * lax.rem(j + k, 8) + c, t, d)) for k in range(1, 8)]
    barrier = greet(peers + quad_peers(j, c, t, d))
    pl.semaphore_wait(barrier, 10)
    items, waits = [], []
    head_group_sends(items, waits, j, c, t, d, lambda chip: dkv_ref.at[chip], all_ref, send, recv, local.at[0])
    quad_sends(items, waits, j, c, t, d, lambda cc, tt: bo_ref.at[cc, tt], bos_ref, q_send, q_recv, local.at[1])
    settle(items, waits)


def pool_kernel(gp_ref, hg_ref, gps_ref, hgs_ref, send, recv, y_send, y_recv, local):
    s, j, c, t, d = place()
    zh = lax.div(s, 8)
    m = lax.rem(s, 8)
    senders = []
    for k in range(8):
        n = lax.rem(m + k, 8)
        senders.append((c != zh if k == 0 else None, device(8 * c + n, t, d)))
    senders += [(None, device(s, t, lax.rem(d + k, 4))) for k in range(1, 4)]
    barrier = greet(senders)
    pl.semaphore_wait(barrier, 11 - jnp.where(c == zh, 1, 0))
    items = []
    waits = half_sends(items, s, j, c, t, d, lambda chip: gp_ref, lambda slot: gps_ref.at[slot], send, recv, local.at[0])
    own = pltpu.make_async_copy(hg_ref.at[d], hgs_ref.at[d], local.at[1])
    items.append((None, own.start, own.wait))
    for k in range(1, 4):
        other = lax.rem(d + k, 4)
        copy = remote(hg_ref.at[other], hgs_ref.at[d], y_send.at[k], y_recv.at[k], device(s, t, other))
        items.append((None, copy.start, copy.wait_send))
        waits.append((None, copy.wait_recv))
    settle(items, waits)


def last_kernel(hg_ref, cg_ref, hgs_ref, cgs_ref, send, recv, y_send, y_recv, local):
    s, j, c, t, d = place()
    peers = [(None, device(lax.rem(s + k, 16), t, d)) for k in range(1, 16)]
    index = 4 * c + d
    others = []
    for k in range(8):
        other = lax.rem(index + k, 8)
        others.append((lax.div(other, 4), lax.rem(other, 4)))
    for cc, dd in others[1:]:
        peers.append((dd != d, device(2 * j + cc, t, dd)))
    barrier = greet(peers)
    pl.semaphore_wait(barrier, 21)
    items, waits = [], []
    for k in range(16):
        target = lax.rem(s + k, 16)
        if k == 0:
            own = pltpu.make_async_copy(hg_ref.at[target], hgs_ref.at[s], local.at[0])
            items.append((None, own.start, own.wait))
        else:
            copy = remote(hg_ref.at[target], hgs_ref.at[s], send.at[k], recv.at[k], device(target, t, d))
            items.append((None, copy.start, copy.wait_send))
            waits.append((None, copy.wait_recv))
    for k in range(8):
        cc, dd = others[k]
        if k == 0:
            own = pltpu.make_async_copy(cg_ref.at[cc, dd], cgs_ref.at[c, d], local.at[1])
            items.append((None, own.start, own.wait))
        else:
            copy = remote(cg_ref.at[cc, dd], cgs_ref.at[c, d], y_send.at[k], y_recv.at[k], device(2 * j + cc, t, dd))
            items.append((None, copy.start, copy.wait_send))
            waits.append((None, copy.wait_recv))
    settle(items, waits)


def dot(a, b, dims):
    return lax.dot_general(a, b, (dims, ((), ())), preferred_element_type=F32)


def attention_kernel(q_ref, kv_ref, g_ref, att_ref, dq_ref, dkv_ref):
    scale = HEAD_DIM ** (-0.5)
    query = q_ref[...]
    grad = g_ref[...]
    keys = kv_ref[:, :HEAD_DIM]
    values = kv_ref[:, HEAD_DIM:]
    scores = dot(keys, query, ((1,), (1,))) * scale
    highest = jnp.max(scores, axis=0, keepdims=True)
    unnormed = jnp.exp(scores - highest)
    weights = unnormed / jnp.sum(unnormed, axis=0, keepdims=True)
    rounded = weights.astype(BF16)
    att_ref[...] = dot(rounded, values, ((0,), (0,))).astype(BF16)
    grad_prob = dot(values, grad, ((1,), (1,)))
    centre = jnp.sum(weights * grad_prob, axis=0, keepdims=True)
    grad_score = (weights * (grad_prob - centre)).astype(BF16)
    dq_ref[...] = (dot(grad_score, keys, ((0,), (0,))) * scale).astype(BF16)
    dkv_ref[:, :HEAD_DIM] = (dot(grad_score, query, ((1,), (0,))) * scale).astype(BF16)
    dkv_ref[:, HEAD_DIM:] = dot(rounded, grad, ((1,), (0,))).astype(BF16)


def attention(query, kv, grad):
    rows, keys = query.shape[0], kv.shape[0]
    vmem = pl.BlockSpec(memory_space=pltpu.VMEM)
    return pl.pallas_call(
        attention_kernel,
        out_shape=(
            jax.ShapeDtypeStruct((rows, HEAD_DIM), BF16),
            jax.ShapeDtypeStruct((rows, HEAD_DIM), BF16),
            jax.ShapeDtypeStruct((keys, 2 * HEAD_DIM), BF16),
        ),
        in_specs=[vmem] * 3,
        out_specs=(vmem,) * 3,
        compiler_params=pltpu.CompilerParams(vmem_limit_bytes=48 * 1024 * 1024),
    )(query, kv, grad)


def shape(*dims):
    return jax.ShapeDtypeStruct(dims, BF16)


def local(section_input, conv_weight, head_weight, output_weight, cotangent):
    s, j, c, t, d = place()
    activity = jax.nn.gelu(section_input[0].astype(F32), approximate=True).astype(BF16)
    at = activity.reshape(128, 2, 8, 160).transpose(2, 1, 3, 0)
    taps = conv_weight.transpose(1, 0, 2).astype(F32) * 0.5
    zero = jnp.zeros((1,) + taps.shape[1:], F32)
    cw = (jnp.concatenate([taps, zero]) + jnp.concatenate([zero, taps])).astype(BF16)
    wp = jnp.concatenate(
        [head_weight.reshape(96, 3, 2, 192), output_weight.reshape(96, 1, 2, 192)], axis=1
    )
    wp = wp.transpose(2, 0, 1, 3).reshape(2, 4, 24, 768)
    cot = cotangent[0]
    xt, halo, cwf, wq, cots = communicate(
        start_kernel, 1,
        (shape(2, 160, 1024), shape(2, 160, 128), shape(6, 160, 768), shape(16, 24, 768), shape(2, 2, 128, 768)),
        (8, 8, 8, 1, 16, 16, 4, 4, 1, 1, 5),
        at, cw, wp, cot,
    )
    low = jnp.where(c == 1, halo[:, :, 127:], 0)
    high = jnp.where(c == 0, halo[:, :, :1], 0)
    before = jnp.concatenate([low, xt[:, :, :-1]], axis=2)
    after = jnp.concatenate([xt[:, :, 1:], high], axis=2)
    taken = jnp.concatenate([before, xt, after], axis=0).reshape(960, 1024)
    part = dot(taken, cwf.reshape(960, 768), ((0,), (0,))).astype(BF16).reshape(8, 128, 768)
    rs, wf = communicate(
        section_kernel, 2, (shape(8, 128, 768), shape(16, 4, 24, 768)), (8, 8, 4, 4, 2), part, wq
    )
    section_local = jnp.sum(rs.astype(F32), axis=0).astype(BF16)
    (sections,) = communicate(
        functools.partial(quad_kernel, 1), 3, (shape(2, 2, 128, 768),), (4, 4, 1), section_local
    )
    weights = wf.reshape(1536, 768)
    head_full, output_full = weights[:, :576], weights[:, 576:]
    section = sections.transpose(0, 2, 1, 3).reshape(256, 1536).astype(F32)
    inverse = lax.rsqrt(jnp.mean(section * section, axis=-1, keepdims=True) + EPSILON)
    normed = (section * inverse).astype(BF16)
    projected = dot(normed, head_full, ((1,), (0,))).astype(BF16)
    cot_full = cots.transpose(0, 2, 1, 3).reshape(256, 1536)
    grad_att = dot(cot_full, output_full, ((1,), (0,))).astype(BF16)
    (kv,) = communicate(keys_kernel, 4, (shape(8, 256, 384),), (8, 8, 1), projected[:, 192:])
    attended, grad_query, dkv = attention(projected[:, :192], kv.reshape(2048, 384), grad_att)
    out_part = dot(attended, output_full, ((1,), (1,))).astype(BF16)
    out_part = out_part.reshape(2, 128, 2, 768).transpose(0, 2, 1, 3)
    dkvs, outs = communicate(
        key_grads_kernel, 5, (shape(8, 256, 384), shape(2, 2, 128, 768)), (8, 8, 4, 4, 2),
        dkv.reshape(8, 256, 384), out_part,
    )
    block_out = (
        section_local.astype(F32) + jnp.sum(outs.astype(F32), axis=(0, 1))
    ).astype(BF16)
    grad_kv = jnp.sum(dkvs.astype(F32), axis=0).astype(BF16)
    grad_proj = jnp.concatenate([grad_query, grad_kv], axis=1)
    normed_part = dot(grad_proj, head_full, ((1,), (1,)))
    spread_part = jnp.sum(normed_part * section, axis=-1) * (1.0 / 1536)
    spread_high = spread_part.astype(BF16)
    spread_low = (spread_part - spread_high.astype(F32)).astype(BF16)
    spread_pair = jnp.stack([spread_high, spread_low], axis=-1).reshape(2, 128, 2)
    spread_pair = jnp.broadcast_to(
        jnp.pad(spread_pair, ((0, 0), (0, 0), (0, 126)))[:, None], (2, 2, 128, 128)
    )
    norm_part = normed_part.astype(BF16).reshape(2, 128, 2, 768).transpose(0, 2, 1, 3)
    norms, spreads = communicate(
        functools.partial(quad_kernel, 2), 6,
        (shape(2, 2, 128, 768), shape(2, 2, 128, 128)), (4, 4, 1, 4, 4, 1), norm_part, spread_pair,
    )
    grad_normed = jnp.sum(norms.astype(F32), axis=(0, 1))
    spread = jnp.sum(spreads.astype(F32), axis=(0, 1, 3))[:, None]
    inverse_here = lax.dynamic_slice_in_dim(inverse, 128 * c, 128, 0)
    grad_section = (
        cot.astype(F32)
        + inverse_here * grad_normed
        - inverse_here**3 * section_local.astype(F32) * spread
    )
    grad_pool = (0.5 * grad_section).astype(BF16)
    head_part = dot(normed, grad_proj, ((0,), (0,)))
    output_part = dot(cot_full, attended, ((0,), (0,)))
    hg = jnp.concatenate([head_part, output_part], axis=1).astype(BF16)
    hg = hg.reshape(16, 4, 24, 768).transpose(1, 0, 2, 3)
    gps, hgs = communicate(
        pool_kernel, 7, (shape(8, 128, 768), shape(4, 16, 24, 768)), (8, 8, 4, 4, 2), grad_pool, hg
    )
    hg_sum = jnp.sum(hgs.astype(F32), axis=0).astype(BF16)
    products = dot(taken, gps.reshape(1024, 768), ((1,), (0,))).reshape(6, 160, 768)
    cg = (products[:5] + products[1:]).astype(BF16)
    cg = cg.reshape(5, 2, 4, 20, 768).transpose(1, 2, 0, 3, 4).reshape(2, 4, 100, 768)
    hgl, cgl = communicate(
        last_kernel, 8, (shape(16, 24, 768), shape(2, 4, 100, 768)), (16, 16, 8, 8, 2), hg_sum, cg
    )
    conv_grad = jnp.sum(cgl.astype(F32), axis=(0, 1)).reshape(5, 20, 768).transpose(1, 0, 2)
    both = jnp.sum(hgl.astype(F32).reshape(8, 2, 24, 4, 192), axis=0)
    both = both.transpose(1, 2, 0, 3).reshape(24, 4, 384)
    return (block_out[None], conv_grad, both[:, :3], both[:, 3])


def solution(mesh):
    placed = (
        P("dp", "seq", None),
        P("seq", None, "tensor"),
        P("seq", None, "tensor"),
        P("seq", "tensor"),
        P("dp", "seq", "tensor"),
    )
    return jax.shard_map(
        local,
        mesh=mesh,
        in_specs=placed,
        out_specs=(
            P("dp", "seq", "tensor"),
            P(("seq", "dp"), None, "tensor"),
            P(("seq", "dp"), None, "tensor"),
            P(("seq", "dp"), "tensor"),
        ),
        check_vma=False,
    )
```

time: 677 us -> 274 us (0.40)
  waiting for transfers between devices: 491 us -> 0 us
  Pallas kernels: 0 us -> 210 us
  blocking collectives: 38.3 us -> 0 us
  local copies, waits for them, and re-layouts: 55.7 us -> 25.7 us
  matrix products: 45 us -> 15.2 us
  starting transfers between devices: 16.1 us -> 0 us
  between operations: 15.8 us -> 1.13 us
  other arithmetic: 12.9 us -> 20.7 us
    all_gather x8 -> x0, waiting for transfers between devices: 307 us -> none  [the longest x1 76.9 us: local(): pieces = lax.all_gather(conv_weight, 'seq', axis=0, tiled=True)]
    pallas_call x0 -> x9, Pallas kernels: none -> 210 us  [the longest x8 206 us: communicate(): pl.pallas_call(kernel, out_shape=outputs, in_specs=[anywhere] * len(opera...]
    reduce_scatter x2 -> x0, waiting for transfers between devices: 84.7 us -> none  [the longest x1 67.8 us: local(): lax.psum_scatter(jnp.concatenate([key_part.reshape(lax.axis_size('seq') *...]
    unnamed x15 -> x0, waiting for transfers between devices: 62.3 us -> none
    slice x25 -> x4, local copies, waits for them, and re-layouts: 36.7 us -> 1.77 us  [the longest x1 0.8 us: local(): projected[:, 192:]]
    dot_general x26 -> x8, matrix products: 42.7 us -> 15.2 us  [dot(): return lax.dot_general(a, b, (dims, ((), ())), preferred_element_type=F32)]
    psum x1 -> x0, waiting for transfers between devices: 27.4 us -> none  [local(): lax.psum(normed_partial.astype(jnp.bfloat16), 'tensor').astype(jnp.float32)]
    all_to_all x1 -> x0, blocking collectives: 21.2 us -> none  [local(): lax.all_to_all(activity, 'seq', split_axis=1, concat_axis=0, tiled=True)]
  transfers between devices with their start and end apart: 17 -> 0, of which waited for: 14 -> 0; matrix products, arithmetic and copies ran while one was open for 14% -> 0% of each run, Pallas kernels for 0% -> 0%
where the time goes in v1:
time: 274 us; the launch traced here: 273 us
  Pallas kernels  210 us (77%)
  local copies, waits for them, and re-layouts  25.7 us (9%)
  other arithmetic  20.7 us (8%)
  matrix products  15.2 us (6%)
    pallas_call x8, Pallas kernels, communicate(): pl.pallas_call(kernel, out_shape=outputs, in_specs=[anywhere] * len(opera...  206 us
    dot_general x8, matrix products, dot(): return lax.dot_general(a, b, (dims, ((), ())), preferred_element_type=F32)  15.2 us
    unnamed x33, local copies, waits for them, and re-layouts  6.29 us

profile of v1, /device:TPU:1, one launch (start us, length us, event | category | flops | bytes accessed | tf_op | source)
XLA Modules:
  0.0 273.0 jit_solution(16417498453345330339)
XLA Ops:
  1.8 1.2 reshape.167
  5.9 1.2 reshape.184
  8.0 1.3 fusion.21.at_ref
  9.3 38.6 %shard_map.84 = (bf16[2,160,1024]{2,1,0:T(8,128)(2,1)}, bf16[2,160,128]{2,1,0:T(8,128)(2,1)}, bf16[6,160,768]{2,1,0:T(8,128)(2,1)}, bf16[16,24,768]{2,1,0:T(8,128)(2,1)}, bf16[2,2,128,768]{3,2,1,0:T(8,128)(2,1)}) custom-call(bf16[8,2,160,128]{3,2,1,0:T(8,128)(2,1)} %fusion.21.at_ref, bf16[6,80,768]{2,1,0:T(8,128)(2,1)} %add_convert_fusion.cw_ref, ...), custom_call_target="tpu_custom_call" | custom-call | tf_op jit(solution)/shard_map/pallas_call | solution.py:58
  49.0 1.9 copy.119
  53.7 3.0 %bitcast_convert_fusion = bf16[1024,768]{1,0:T(8,128)(2,1)} fusion(bf16[6,160,1024]{2,1,0:T(8,128)(2,1)S(1)} %maximum_maximum_fusion, bf16[6,160,768]{2,1,0:T(8,128)(2,1)S(1)} %copy-done.14), kind=kOutput, calls=%fused_computation | convolution fusion | flops 1510735872 | bytes 5013504 | tf_op jit(solution)/shard_map/dot_general | solution.py:317
  56.8 33.4 %shard_map.85 = (bf16[8,128,768]{2,1,0:T(8,128)(2,1)}, bf16[16,4,24,768]{3,2,1,0:T(8,128)(2,1)}) custom-call(bf16[8,128,768]{2,1,0:T(8,128)(2,1)} %bitcast.98, bf16[16,24,768]{2,1,0:T(8,128)(2,1)} %get-tuple-element.25.wq_ref), custom_call_target="tpu_custom_call" | custom-call | tf_op jit(solution)/shard_map/pallas_call | solution.py:58
  90.2 2.4 reduce_sum.99.refs_0_
  92.6 2.0 convolution_convert_fusion.3
  94.6 11.9 %shard_map.86 = bf16[2,2,128,768]{3,2,1,0:T(8,128)(2,1)} custom-call(bf16[128,768]{1,0:T(8,128)(2,1)} %reduce_sum.99.refs_0_), custom_call_target="tpu_custom_call" | custom-call | tf_op jit(solution)/shard_map/pallas_call | solution.py:58
  106.5 1.4 fusion.5
  107.9 1.3 convert_bitcast_fusion
  109.2 1.2 copy.117
  110.5 1.5 copy-done.3
  113.7 22.6 %shard_map.87 = bf16[8,256,384]{2,1,0:T(8,128)(2,1)} custom-call(bf16[256,384]{1,0:T(8,128)(2,1)} %slice.52.kv_ref), custom_call_target="tpu_custom_call" | custom-call | tf_op jit(solution)/shard_map/pallas_call | solution.py:58
  136.3 1.4 copy-done
  137.7 4.0 %shard_map.88 = (bf16[256,192]{1,0:T(8,128)(2,1)S(1)}, bf16[256,192]{1,0:T(8,128)(2,1)S(1)}, bf16[2048,384]{1,0:T(8,128)(2,1)S(1)}) custom-call(bf16[256,192]{1,0:T(8,128)(2,1)S(1)} %slice.51.q_ref, bf16[2048,384]{1,0:T(8,128)(2,1)S(1)} %bitcast.79, bf16[256,192]{1,0:T(8,128)(2,1)S(1)} %copy.120.g_ref), custom_call_target="tpu_custom_call" | custom-call | tf_op jit(solution)/shard_map/pallas_call | solution.py:343
  141.8 1.2 copy-done.1
  142.9 1.3 convolution_convert_fusion.2
  144.3 1.6 convolution_convert_fusion
  147.1 33.4 %shard_map.89 = (bf16[8,256,384]{2,1,0:T(8,128)(2,1)}, bf16[2,2,128,768]{3,2,1,0:T(8,128)(2,1)}) custom-call(bf16[8,256,384]{2,1,0:T(8,128)(2,1)} %bitcast.80, bf16[2,2,128,768]{3,2,1,0:T(8,128)(2,1)} %bitcast.96), custom_call_target="tpu_custom_call" | custom-call | tf_op jit(solution)/shard_map/pallas_call | solution.py:58
  180.6 1.7 reduce_sum.102
  182.4 2.5 fusion.36
  187.2 13.7 %shard_map.90 = (bf16[2,2,128,768]{3,2,1,0:T(8,128)(2,1)}, bf16[2,2,128,128]{3,2,1,0:T(8,128)(2,1)}) custom-call(bf16[2,2,128,768]{3,2,1,0:T(8,128)(2,1)} %bitcast.92, bf16[2,2,128,128]{3,2,1,0:T(8,128)(2,1)} %broadcast_in_dim.8.refs_1_), custom_call_target="tpu_custom_call" | custom-call | tf_op jit(solution)/shard_map/pallas_call | solution.py:58
  200.9 1.4 convert_reduce_fusion.1
  204.5 1.9 maximum_bitcast_fusion.hg_ref
  206.4 32.9 %shard_map.91 = (bf16[8,128,768]{2,1,0:T(8,128)(2,1)}, bf16[4,16,24,768]{3,2,1,0:T(8,128)(2,1)}) custom-call(bf16[128,768]{1,0:T(8,128)(2,1)} %get-tuple-element.45.gp_ref, bf16[4,16,24,768]{3,2,1,0:T(8,128)(2,1)} %maximum_bitcast_fusion.hg_ref), custom_call_target="tpu_custom_call" | custom-call | tf_op jit(solution)/shard_map/pallas_call | solution.py:58
  239.3 3.1 %reduce_sum.106.hg_ref = bf16[16,24,768]{2,1,0:T(8,128)(2,1)} reduce(bf16[4,16,24,768]{3,2,1,0:T(8,128)(2,1)} %get-tuple-element.36, bf16[]{:T(256)} %constant.36.clone.1), dimensions={0}, to_apply=%region_7.8 | reduce | flops 884736 | bytes 2949122 | tf_op jit(solution)/shard_map/reduce_sum | solution.py:441
  242.4 3.1 %fusion.40 = f32[960,768]{1,0:T(8,128)S(1)} fusion(bf16[960,1024]{1,0:T(8,128)(2,1)S(1)} %bitcast.97, bf16[1024,768]{1,0:T(8,128)(2,1)} %bitcast.104), kind=kOutput, calls=%fused_computation.70 | convolution fusion | flops 1509949440 | bytes 6488064 | tf_op jit(solution)/shard_map/dot_general | solution.py:317
  246.5 1.2 copy.132.cg_ref
  247.7 19.8 %shard_map.92 = (bf16[16,24,768]{2,1,0:T(8,128)(2,1)}, bf16[2,4,100,768]{3,2,1,0:T(8,128)(2,1)}) custom-call(bf16[16,24,768]{2,1,0:T(8,128)(2,1)} %reduce_sum.106.hg_ref, bf16[2,4,100,768]{3,2,1,0:T(8,128)(2,1)} %copy.132.cg_ref), custom_call_target="tpu_custom_call" | custom-call | tf_op jit(solution)/shard_map/pallas_call | solution.py:58
  267.5 1.6 convert_reduce_fusion
  (73 shorter events, 21.4 us)
Async XLA Ops:
  1.6 3.2 %copy-start.11 = (bf16[80,5,768]{2,0,1:T(8,128)(2,1)S(1)}, bf16[80,5,768]{2,0,1:T(8,128)(2,1)}, u32[]{:S(2)}) copy-start(bf16[80,5,768]{2,0,1:T(8,128)(2,1)} %param.6) | copy-start | bytes 1843204
  4.8 1.1 copy-start.10
  51.0 1.1 copy-start.2
  52.4 1.4 copy-start.14
  52.8 4.0 %copy-start.5 = (bf16[6,160,1024]{2,1,0:T(8,128)(2,1)}, bf16[6,160,1024]{2,1,0:T(8,128)(2,1)S(1)}, u32[]{:S(2)}) copy-start(bf16[6,160,1024]{2,1,0:T(8,128)(2,1)S(1)} %maximum_maximum_fusion) | copy-start | bytes 5898244
  110.4 1.7 copy-start.3
  136.3 1.4 copy-start
  141.8 1.2 copy-start.1
  186.2 14.7 %copy-start.9 = (bf16[2,2,128,768]{3,2,1,0:T(8,128)(2,1)S(1)}, bf16[2,2,128,768]{3,2,1,0:T(8,128)(2,1)}, u32[]{:S(2)}) copy-start(bf16[2,2,128,768]{3,2,1,0:T(8,128)(2,1)} %get-tuple-element.31) | copy-start | bytes 2359300
  187.2 15.3 %copy-start.7 = (bf16[128,768]{1,0:T(8,128)(2,1)S(1)}, bf16[128,768]{1,0:T(8,128)(2,1)}, u32[]{:S(2)}) copy-start(bf16[128,768]{1,0:T(8,128)(2,1)} %reduce_sum.99.refs_0_) | copy-start | bytes 589828
  187.2 15.3 %copy-start.8 = (bf16[1,128,768]{2,1,0:T(8,128)(2,1)S(1)}, bf16[1,128,768]{2,1,0:T(8,128)(2,1)}, u32[]{:S(2)}) copy-start(bf16[1,128,768]{2,1,0:T(8,128)(2,1)} %param.9) | copy-start | bytes 589828
  200.8 1.5 copy-start.13
  203.4 1.1 copy-start.4
  239.3 3.1 %copy-start.6 = (bf16[6,160,1024]{2,1,0:T(8,128)(2,1)S(1)}, bf16[6,160,1024]{2,1,0:T(8,128)(2,1)}, u32[]{:S(2)}) copy-start(bf16[6,160,1024]{2,1,0:T(8,128)(2,1)} %copy-done.5) | copy-start | bytes 5898244
  267.5 2.4 copy-start.12

commit v2 on v0

v2 whole, which is shorter than its diff:
```python
import functools

import jax
import jax.numpy as jnp
from jax import lax
from jax.experimental import pallas as pl
from jax.experimental.pallas import tpu as pltpu
from jax.sharding import PartitionSpec as P

HEAD_DIM = 192
EPSILON = 1e-06
MESH = pl.DeviceIdType.MESH
BF16 = jnp.bfloat16
F32 = jnp.float32


class Place:
    def __init__(self):
        self.s = lax.axis_index("seq")
        self.zh = lax.div(self.s, 8)
        self.x = lax.rem(lax.div(self.s, 2), 4)
        self.c = lax.rem(self.s, 2)
        self.t = lax.axis_index("tensor")
        self.d = lax.axis_index("dp")
        self.z = 2 * self.zh + self.t

    def at(self, x=None, zh=None, c=None, t=None, d=None):
        x = self.x if x is None else x
        zh = self.zh if zh is None else zh
        c = self.c if c is None else c
        return {
            "seq": zh * 8 + x * 2 + c,
            "tensor": self.t if t is None else t,
            "dp": self.d if d is None else d,
        }

    def along_x(self, k):
        return lax.rem(self.x + k, 4)

    def along_y(self, k):
        return lax.rem(self.d + k, 4)

    def along_z(self, k):
        return lax.rem(self.z + k, 4)

    def at_z(self, z):
        return self.at(zh=lax.div(z, 2), t=lax.rem(z, 2))

    @property
    def sibling(self):
        return self.at(c=1 - self.c)


def remote(src, dst, send, recv, target):
    return pltpu.make_async_remote_copy(
        src_ref=src, dst_ref=dst, send_sem=send, recv_sem=recv, device_id=target, device_id_type=MESH
    )


def greet(targets):
    barrier = pltpu.get_barrier_semaphore()
    for condition, target in targets:
        if condition is None:
            pl.semaphore_signal(barrier, inc=1, device_id=target, device_id_type=MESH)
        else:

            @pl.when(condition)
            def _(target=target):
                pl.semaphore_signal(barrier, inc=1, device_id=target, device_id_type=MESH)

    return barrier


def under(condition, action):
    if condition is None:
        action()
    else:

        @pl.when(condition)
        def _():
            action()


def communicate(kernel, name, collective, outputs, remotes, locals_, *operands, aliases=None, vmem=(), scratch=()):
    anywhere = pl.BlockSpec(memory_space=pl.ANY)
    inside = pl.BlockSpec(memory_space=pltpu.VMEM)
    return pl.pallas_call(
        kernel,
        name=name,
        out_shape=outputs,
        in_specs=[inside if n in vmem else anywhere for n in range(len(operands))],
        out_specs=tuple([anywhere] * len(outputs)),
        scratch_shapes=list(scratch)
        + [
            pltpu.SemaphoreType.DMA((remotes,)),
            pltpu.SemaphoreType.DMA((remotes,)),
            pltpu.SemaphoreType.DMA((locals_,)),
        ],
        input_output_aliases=aliases or {},
        compiler_params=pltpu.CompilerParams(
            collective_id=collective, has_side_effects=True, vmem_limit_bytes=16 * 1024 * 1024 if vmem else None
        ),
    )(*operands)


class Moves:
    def __init__(self, place, send, recv, local):
        self.place, self.send, self.recv, self.local = place, send, recv, local
        self.sends, self.receives, self.locals = [], [], []
        self.used = 0
        self.used_local = 0

    def slots(self, count):
        first = self.used
        self.used += count
        return first

    def push(self, src, dst, target, slot, recv_slot=None, when=None):
        recv_slot = slot if recv_slot is None else recv_slot
        copy = remote(src, dst, self.send.at[slot], self.recv.at[recv_slot], target)
        under(when, copy.start)
        self.sends.append((when, copy.wait_send))

    def keep(self, src, dst, when=None):
        copy = pltpu.make_async_copy(src, dst, self.local.at[self.used_local])
        self.used_local += 1
        under(when, copy.start)
        self.locals.append((when, copy.wait))

    def arrival(self, dst, slot, when=None):
        place = self.place
        copy = remote(dst, dst, self.send.at[0], self.recv.at[slot], place.at())
        return lambda: under(when, copy.wait_recv)

    def expect(self, dst, slot, when=None):
        self.receives.append(self.arrival(dst, slot, when))

    def settle(self):
        for wait in self.receives:
            wait()
        for when, wait in self.locals + self.sends:
            under(when, wait)


def z_gather(moves, src, dst_ref):
    p = moves.place
    first = moves.slots(4)
    moves.keep(src, dst_ref.at[p.z])
    for k in (2, 1, 3):
        moves.push(src, dst_ref.at[p.z], p.at_z(p.along_z(k)), first + k)
        moves.expect(dst_ref.at[p.along_z(4 - k)], first + k)


def z_scatter(moves, src_ref, dst_ref):
    p = moves.place
    first = moves.slots(4)
    moves.keep(src_ref.at[p.z], dst_ref.at[p.z])
    for k in (2, 1, 3):
        z = p.along_z(k)
        moves.push(src_ref.at[z], dst_ref.at[p.z], p.at_z(z), first + k)
        moves.expect(dst_ref.at[p.along_z(4 - k)], first + k)


def z_ring(p):
    return [(None, p.at_z(p.along_z(k))) for k in range(1, 4)]


def y_ring(p):
    return [(None, p.at(d=p.along_y(k))) for k in range(1, 4)]


def x_ring(p):
    return [(None, p.at(x=p.along_x(k))) for k in range(1, 4)]


def start_kernel(at_ref, edge_ref, cw_ref, wp_ref, xt_ref, low_ref, high_ref, cwf_ref, wq_ref, send, recv, local):
    p = Place()
    peers = []
    for k in range(1, 16):
        peers.append((None, {"seq": lax.rem(p.s + k, 16), "tensor": p.t, "dp": p.d}))
    barrier = greet(peers)
    pl.semaphore_wait(barrier, 15)
    moves = Moves(p, send, recv, local)

    first = moves.slots(4)
    mine = cwf_ref.at[:, 2 * p.zh + p.c]
    moves.push(cw_ref, mine, p.at(zh=1 - p.zh), first)
    moves.push(cw_ref, mine, p.sibling, first + 1)
    moves.keep(cw_ref, mine)
    from_z = cwf_ref.at[:, 2 * (1 - p.zh) + p.c]
    conv_arrival = moves.arrival(from_z, first)
    moves.expect(cwf_ref.at[:, 2 * p.zh + 1 - p.c], first + 1)

    a = moves.slots(4)
    core = lax.div(p.x, 2)
    slot = 2 * lax.rem(p.x, 2) + p.c
    spot = xt_ref.at[:, :, pl.ds(pl.multiple_of(slot * 128, 128), 128)]
    for k in (2, 1, 3, 0):
        x = p.along_x(k)
        if k == 0:
            moves.push(at_ref.at[x], spot, p.at(c=core), a, a + slot, core != p.c)
            moves.keep(at_ref.at[x], spot, core == p.c)
        else:
            moves.push(at_ref.at[x], spot, p.at(x=x, c=core), a + k, a + slot)
    for n in range(4):
        x, c = 2 * p.c + n // 2, n % 2
        here = xt_ref.at[:, :, pl.ds(n * 128, 128)]
        moves.expect(here, a + n, jnp.logical_or(x != p.x, c != p.c))
    for up, out_ref in ((True, low_ref), (False, high_ref)):
        e = moves.slots(4)
        if up:
            sends = jnp.logical_and(lax.rem(p.s, 4) == 3, p.s != 15)
            block = lax.rem(p.s + 1, 16)
        else:
            sends = jnp.logical_and(lax.rem(p.s, 4) == 0, p.s != 0)
            block = lax.rem(p.s + 15, 16)
        zh, c = lax.div(block, 8), lax.div(lax.rem(block, 8), 4)
        for k in range(4):
            x = p.along_x(k)
            src = edge_ref.at[1 if up else 0, x]
            target = p.at(x=x, zh=zh, c=c)
            if k == 0:
                alone = jnp.logical_and(zh == p.zh, c == p.c)
                moves.push(src, out_ref, target, e, e, jnp.logical_and(sends, jnp.logical_not(alone)))
                moves.keep(src, out_ref, jnp.logical_and(sends, alone))
            else:
                moves.push(src, out_ref, target, e + k, e, sends)
        base = 8 * p.zh + 4 * p.c
        if up:
            moves.expect(out_ref, e, jnp.logical_and(base != 0, base - 1 != p.s))
        else:
            moves.expect(out_ref, e, jnp.logical_and(base != 12, base + 4 != p.s))
    w = moves.slots(8)
    shard = 4 * p.zh + p.x
    for k in range(8):
        other = lax.rem(shard + k, 8)
        zh, x = lax.div(other, 4), lax.rem(other, 4)
        src = wp_ref.at[zh, p.d]
        if k == 0:
            moves.keep(src, wq_ref.at[shard])
        else:
            moves.push(src, wq_ref.at[shard], p.at(x=x, zh=zh), w + k)
            moves.expect(wq_ref.at[lax.rem(shard + 8 - k, 8)], w + k)
    conv_arrival()
    moves.push(from_z, from_z, p.sibling, first + 2)
    moves.expect(cwf_ref.at[:, 2 * (1 - p.zh) + 1 - p.c], first + 2)
    moves.settle()


def weight_rows(moves, wq_ref, wf_ref, lower, wait_now):
    p = moves.place
    y = moves.slots(8)
    src = wq_ref.at[pl.ds(lower, 4)]

    def rows(c, d):
        return wf_ref.at[lower // 4, :, c, d]

    moves.keep(src, rows(p.c, p.d))
    moves.push(src, rows(p.c, p.d), p.sibling, y)
    moves.expect(rows(1 - p.c, p.d), y)
    for k in (2, 1, 3):
        moves.push(src, rows(p.c, p.d), p.at(d=p.along_y(k)), y + k)

    def forward():
        for k in (1, 3, 2):
            d = p.along_y(4 - k)
            moves.arrival(rows(p.c, d), y + k)()
            moves.push(rows(p.c, d), rows(p.c, d), p.sibling, y + 3 + k)
            moves.expect(rows(1 - p.c, d), y + 3 + k)

    wait_now.append(forward)


def section_kernel(part_ref, cot_ref, x5_ref, wq_ref, rs_ref, cots_ref, x5s_ref, wa_ref, send, recv, local):
    p = Place()
    core = lax.div(p.x, 2)
    senders = []
    for k in range(4):
        senders.append((core != p.c if k == 0 else None, p.at(x=p.along_x(k), c=core)))
    barrier = greet(senders + [(None, p.sibling)] + z_ring(p) + y_ring(p))
    pl.semaphore_wait(barrier, 3 + jnp.where(core != p.c, 1, 0) + 1 + 3 + 3)
    moves = Moves(p, send, recv, local)
    a = moves.slots(4)
    for k in (2, 1, 3, 0):
        slot = lax.rem(2 * lax.rem(p.x, 2) + p.c + k, 4)
        x, c = 2 * p.c + lax.div(slot, 2), lax.rem(slot, 2)
        alone = jnp.logical_and(x == p.x, c == p.c)
        moves.push(part_ref.at[slot], rs_ref.at[p.x], p.at(x=x, c=c), a + k, a + p.x, jnp.logical_not(alone))
        moves.keep(part_ref.at[slot], rs_ref.at[p.x], alone)
    for x in range(4):
        moves.expect(rs_ref.at[x], a + x, jnp.logical_or(p.x != x, core != p.c))
    later = []
    weight_rows(moves, wq_ref, wa_ref, 0, later)
    z_gather(moves, cot_ref, cots_ref)
    b = moves.slots(1)
    moves.push(x5_ref, x5s_ref, p.sibling, b)
    moves.expect(x5s_ref, b)
    for action in later:
        action()
    moves.settle()


def channels_kernel(sec_ref, wq_ref, wa_ref, secs_ref, wf_ref, send, recv, local):
    p = Place()
    barrier = greet(z_ring(p) + y_ring(p) + [(None, p.sibling)])
    pl.semaphore_wait(barrier, 7)
    moves = Moves(p, send, recv, local)
    z_gather(moves, sec_ref, secs_ref)
    later = []
    weight_rows(moves, wq_ref, wf_ref, 4, later)
    for action in later:
        action()
    moves.settle()


def keys_kernel(kv_ref, all_ref, send, recv, local):
    p = Place()
    barrier = greet(x_ring(p) + [(None, p.sibling)])
    pl.semaphore_wait(barrier, 4)
    moves = Moves(p, send, recv, local)
    a = moves.slots(8)
    mine = all_ref.at[p.c, p.x]
    for k in (2, 1, 3):
        moves.push(kv_ref, mine, p.at(x=p.along_x(k)), a + k)
    moves.push(kv_ref, mine, p.sibling, a)
    moves.keep(kv_ref, mine)
    moves.expect(all_ref.at[1 - p.c, p.x], a)
    for k in (1, 3, 2):
        x = p.along_x(4 - k)
        moves.arrival(all_ref.at[p.c, x], a + k)()
        moves.push(all_ref.at[p.c, x], all_ref.at[p.c, x], p.sibling, a + 3 + k)
        moves.expect(all_ref.at[1 - p.c, x], a + 3 + k)
    moves.settle()


def key_grads_kernel(dkv_ref, bo_ref, all_ref, bos_ref, buf_ref, sum_ref, send, recv, local):
    p = Place()
    barrier = greet(x_ring(p) + [(None, p.sibling)] + z_ring(p))
    pl.semaphore_wait(barrier, 7)
    moves = Moves(p, send, recv, local)
    a = moves.slots(8)
    for k in (2, 1, 3, 0):
        x = p.along_x(k)
        moves.push(dkv_ref.at[1 - p.c, x], buf_ref.at[k], p.sibling, a + k)
    z_scatter(moves, bo_ref, bos_ref)
    for k in (2, 1, 3, 0):
        x = p.along_x(k)
        moves.arrival(buf_ref.at[k], a + k)()
        total = (dkv_ref[p.c, x].astype(F32) + buf_ref[k].astype(F32)).astype(BF16)
        if k == 0:
            sum_ref[0] = total
            moves.keep(sum_ref.at[0], all_ref.at[p.x])
        else:
            sum_ref[k] = total
            moves.push(sum_ref.at[k], all_ref.at[p.x], p.at(x=x), a + 4 + k)
            moves.expect(all_ref.at[p.along_x(4 - k)], a + 4 + k)
    moves.settle()


def norm_kernel(norm_ref, spread_ref, nh_ref, ch_ref, gpa_ref, norms_ref, spreads_ref, nhs_ref, chs_ref, gpas_ref,
                send, recv, local):
    p = Place()
    barrier = greet(z_ring(p) + [(None, p.sibling)])
    pl.semaphore_wait(barrier, 4)
    moves = Moves(p, send, recv, local)
    z_scatter(moves, norm_ref, norms_ref)
    z_scatter(moves, spread_ref, spreads_ref)
    b = moves.slots(3)
    for n, (src, dst) in enumerate(((nh_ref.at[1 - p.c], nhs_ref), (ch_ref.at[1 - p.c], chs_ref), (gpa_ref, gpas_ref))):
        moves.push(src, dst, p.sibling, b + n)
        moves.expect(dst, b + n)
    moves.settle()


def pool_kernel(gp_ref, hg_ref, gps_ref, hgs_ref, send, recv, local):
    p = Place()
    barrier = greet(
        [(None, p.at(x=p.along_x(k), c=c)) for k in range(1, 4) for c in range(2)] + [(None, p.sibling)] + y_ring(p)
    )
    pl.semaphore_wait(barrier, 10)
    moves = Moves(p, send, recv, local)
    y = moves.slots(4)
    moves.keep(hg_ref.at[p.d], hgs_ref.at[p.d])
    for k in (2, 1, 3):
        d = p.along_y(k)
        moves.push(hg_ref.at[d], hgs_ref.at[p.d], p.at(d=d), y + k)
        moves.expect(hgs_ref.at[p.along_y(4 - k)], y + k)
    a = moves.slots(8)
    block = 2 * p.x + p.c
    for k in (4, 5, 2, 3, 6, 7, 1, 0):
        other = lax.rem(block + k, 8)
        x, c = lax.div(other, 2), lax.rem(other, 2)
        if k == 0:
            moves.keep(gp_ref.at[c], gps_ref.at[block])
        else:
            moves.push(gp_ref.at[c], gps_ref.at[block], p.at(x=x, c=c), a + k)
            moves.expect(gps_ref.at[lax.rem(block + 8 - k, 8)], a + k)
    moves.settle()


def last_kernel(hg_ref, cg_ref, hgs_ref, cgs_ref, send, recv, local):
    p = Place()
    peers = []
    for zh in range(2):
        for c in range(2):
            for k in range(4):
                here = k == 0
                target = p.at(zh=zh, c=c, d=p.along_y(k))
                peers.append((jnp.logical_or(zh != p.zh, c != p.c) if here else None, target))
    for zh in range(2):
        for k in range(1, 4):
            peers.append((None, p.at(zh=zh, x=p.along_x(k), c=p.zh)))
    barrier = greet(peers)
    pl.semaphore_wait(barrier, 15 + 6)
    moves = Moves(p, send, recv, local)
    b = moves.slots(16)
    me = 8 * p.zh + 4 * p.c + p.d
    for k in (8, 12, 4, 2, 10, 14, 6, 1, 3, 9, 11, 13, 15, 5, 7, 0):
        other = lax.rem(me + k, 16)
        zh, c, d = lax.div(other, 8), lax.rem(lax.div(other, 4), 2), lax.rem(other, 4)
        src = cg_ref.at[zh, c, d]
        if k == 0:
            moves.keep(src, cgs_ref.at[me])
        else:
            moves.push(src, cgs_ref.at[me], p.at(zh=zh, c=c, d=d), b + k)
            moves.expect(cgs_ref.at[lax.rem(me + 16 - k, 16)], b + k)
    a = moves.slots(8)
    for k in range(8):
        other = lax.rem(2 * p.x + k, 8)
        x, c = lax.div(other, 2), lax.rem(other, 2)
        src, dst = hg_ref.at[x, c], hgs_ref.at[p.zh, p.x]
        alone = jnp.logical_and(jnp.logical_and(x == p.x, c == p.c), p.zh == p.c)
        if k < 2:
            moves.push(src, dst, p.at(x=x, zh=p.c, c=c), a + k, a + 4 * p.zh + p.x, jnp.logical_not(alone))
            moves.keep(src, dst, alone)
        else:
            moves.push(src, dst, p.at(x=x, zh=p.c, c=c), a + k, a + 4 * p.zh + p.x)
    for zh in range(2):
        for x in range(4):
            alone = jnp.logical_and(jnp.logical_and(x == p.x, zh == p.zh), p.zh == p.c)
            moves.expect(hgs_ref.at[zh, x], a + 4 * zh + x, jnp.logical_not(alone))
    moves.settle()

def dot(a, b, dims):
    return lax.dot_general(a, b, (dims, ((), ())), preferred_element_type=F32)


def attention_kernel(q_ref, kv_ref, g_ref, att_ref, dq_ref, dkv_ref):
    scale = HEAD_DIM ** (-0.5)
    query = q_ref[...]
    grad = g_ref[...]
    keys = kv_ref[:, :HEAD_DIM]
    values = kv_ref[:, HEAD_DIM:]
    scores = dot(keys, query, ((1,), (1,))) * scale
    highest = jnp.max(scores, axis=0, keepdims=True)
    unnormed = jnp.exp(scores - highest)
    weights = unnormed / jnp.sum(unnormed, axis=0, keepdims=True)
    rounded = weights.astype(BF16)
    att_ref[...] = dot(rounded, values, ((0,), (0,))).astype(BF16)
    grad_prob = dot(values, grad, ((1,), (1,)))
    centre = jnp.sum(weights * grad_prob, axis=0, keepdims=True)
    grad_score = (weights * (grad_prob - centre)).astype(BF16)
    dq_ref[...] = (dot(grad_score, keys, ((0,), (0,))) * scale).astype(BF16)
    dkv_ref[:, :HEAD_DIM] = (dot(grad_score, query, ((1,), (0,))) * scale).astype(BF16)
    dkv_ref[:, HEAD_DIM:] = dot(rounded, grad, ((1,), (0,))).astype(BF16)


def attention(query, kv, grad):
    rows, keys = query.shape[0], kv.shape[0]
    vmem = pl.BlockSpec(memory_space=pltpu.VMEM)
    return pl.pallas_call(
        attention_kernel,
        out_shape=(
            jax.ShapeDtypeStruct((rows, HEAD_DIM), BF16),
            jax.ShapeDtypeStruct((rows, HEAD_DIM), BF16),
            jax.ShapeDtypeStruct((keys, 2 * HEAD_DIM), BF16),
        ),
        in_specs=[vmem] * 3,
        out_specs=(vmem,) * 3,
        compiler_params=pltpu.CompilerParams(vmem_limit_bytes=48 * 1024 * 1024),
    )(query, kv, grad)


def shape(*dims):
    return jax.ShapeDtypeStruct(dims, BF16)


def local(section_input, conv_weight, head_weight, output_weight, cotangent):
    p = Place()
    activity = jax.nn.gelu(section_input[0].astype(F32), approximate=True).astype(BF16)
    bins = activity.reshape(128, 2, 2, 4, 160)
    at = bins.transpose(3, 1, 2, 4, 0).reshape(4, 2, 320, 128)
    edges = jnp.stack([bins[0], bins[127]]).transpose(0, 3, 1, 2, 4).reshape(2, 4, 2, 320)
    edges = jnp.pad(edges, ((0, 0), (0, 0), (0, 6), (0, 0)))
    cw = conv_weight.transpose(1, 0, 2)
    wp = jnp.concatenate(
        [head_weight.reshape(96, 3, 2, 192), output_weight.reshape(96, 1, 2, 192)], axis=1
    )
    wp = wp.transpose(2, 0, 1, 3).reshape(2, 4, 24, 768)
    cot = cotangent[0]
    xt, low, high, cwf, wq = communicate(
        start_kernel, "start", 1,
        (shape(2, 320, 512), shape(8, 320), shape(8, 320), shape(5, 4, 80, 768), shape(8, 24, 768)),
        24, 8, at, edges, cw, wp,
    )
    base = 8 * p.zh + 4 * p.c
    low = jnp.where(base != 0, low[:2], 0)[:, :, None]
    high = jnp.where(base != 12, high[:2], 0)[:, :, None]
    wide = jnp.concatenate([low, xt, high], axis=2).astype(F32)
    even, odd = wide[0], wide[1]
    same = (even + odd).astype(BF16)
    cross = (odd[:, :-1] + even[:, 1:]).astype(BF16)
    x5 = jnp.stack([same[:, :512], cross[:, :512], same[:, 1:513], cross[:, 1:513], same[:, 2:514]])
    x5 = x5.reshape(1600, 512)
    part = (dot(x5, cwf.reshape(1600, 768), ((0,), (0,))) * 0.5).astype(BF16).reshape(4, 128, 768)
    rs, cots, x5s, wa = communicate(
        section_kernel, "section", 2,
        (shape(4, 128, 768), shape(4, 128, 768), shape(1600, 512), shape(2, 4, 2, 4, 24, 768)),
        20, 8, part, cot, x5, wq,
    )
    section_local = jnp.sum(rs.astype(F32), axis=0).astype(BF16)
    sections, wf = communicate(
        channels_kernel, "channels", 3, (shape(4, 128, 768), shape(2, 4, 2, 4, 24, 768)), 16, 4,
        section_local, wq, wa, aliases={2: 1},
    )
    weights = wf.reshape(1536, 768)
    head_full, output_full = weights[:, :576], weights[:, 576:]

    def whole(blocks):
        return blocks.reshape(2, 2, 128, 768).transpose(0, 2, 1, 3).reshape(256, 1536)

    section = whole(sections).astype(F32)
    inverse = lax.rsqrt(jnp.mean(section * section, axis=-1, keepdims=True) + EPSILON)
    normed = (section * inverse).astype(BF16)
    projected = dot(normed, head_full, ((1,), (0,))).astype(BF16)
    cot_full = whole(cots)
    grad_att = dot(cot_full, output_full, ((1,), (0,))).astype(BF16)
    (kv,) = communicate(keys_kernel, "keys", 4, (shape(2, 4, 256, 384),), 8, 1, projected[:, 192:])
    attended, grad_query, dkv = attention(projected[:, :192], kv.reshape(2048, 384), grad_att)

    def blocks(full):
        return full.reshape(2, 128, 2, 768).transpose(0, 2, 1, 3).reshape(4, 128, 768)

    out_part = blocks(dot(attended, output_full, ((1,), (1,))).astype(BF16))
    dkvs, outs, = communicate(
        key_grads_kernel, "key_grads", 5, (shape(4, 256, 384), shape(4, 128, 768)), 12, 2,
        dkv.reshape(2, 4, 256, 384), out_part, vmem=(0,),
        scratch=(pltpu.VMEM((4, 256, 384), BF16), pltpu.VMEM((4, 256, 384), BF16)),
    )
    block_out = (section_local.astype(F32) + jnp.sum(outs.astype(F32), axis=0)).astype(BF16)
    grad_kv = jnp.sum(dkvs.astype(F32), axis=0).astype(BF16)
    grad_proj = jnp.concatenate([grad_query, grad_kv], axis=1)
    normed_part = dot(grad_proj, head_full, ((1,), (1,)))
    spread_part = jnp.sum(normed_part * section, axis=-1) * (1.0 / 1536)
    spread_high = spread_part.astype(BF16)
    spread_low = (spread_part - spread_high.astype(F32)).astype(BF16)
    spread_pair = jnp.stack([spread_high, spread_low], axis=-1).reshape(2, 128, 2)
    spread_pair = jnp.broadcast_to(
        jnp.pad(spread_pair, ((0, 0), (0, 0), (0, 126)))[:, None], (2, 2, 128, 128)
    ).reshape(4, 128, 128)
    normed_halves = normed.reshape(256, 2, 768).transpose(1, 0, 2)
    cot_halves = cot_full.reshape(256, 2, 768).transpose(1, 0, 2)
    gpa = jnp.concatenate([grad_proj, attended], axis=1)
    norms, spreads, normed_other, cot_other, gpa_other = communicate(
        norm_kernel, "norm", 6,
        (shape(4, 128, 768), shape(4, 128, 128), shape(256, 768), shape(256, 768), shape(256, 768)), 12, 2,
        blocks(normed_part.astype(BF16)), spread_pair, normed_halves, cot_halves, gpa,
    )
    grad_normed = jnp.sum(norms.astype(F32), axis=0)
    spread = jnp.sum(spreads.astype(F32), axis=(0, 2))[:, None]
    inverse_here = lax.dynamic_slice_in_dim(inverse, 128 * p.zh, 128, 0)
    grad_section = (
        cot.astype(F32)
        + inverse_here * grad_normed
        - inverse_here**3 * section_local.astype(F32) * spread
    )
    grad_pool = (0.5 * grad_section).astype(BF16)
    normed_mine = lax.dynamic_index_in_dim(normed_halves, p.c, 0, False)
    cot_mine = lax.dynamic_index_in_dim(cot_halves, p.c, 0, False)
    rows = ((0,), (0,))
    head_part = dot(normed_mine, gpa[:, :576], rows) + dot(normed_other, gpa_other[:, :576], rows)
    output_part = dot(cot_mine, gpa[:, 576:], rows) + dot(cot_other, gpa_other[:, 576:], rows)
    hg = jnp.concatenate([head_part, output_part], axis=1).astype(BF16)
    hg = hg.reshape(8, 4, 24, 768).transpose(1, 0, 2, 3)
    gps, hgs = communicate(
        pool_kernel, "pool", 7, (shape(8, 128, 384), shape(4, 8, 24, 768)), 12, 2,
        grad_pool.reshape(128, 2, 384).transpose(1, 0, 2), hg,
    )
    hg_sum = jnp.sum(hgs.astype(F32), axis=0).astype(BF16)
    pool_mine = lax.dynamic_slice_in_dim(gps, 4 * p.c, 4, 0).reshape(512, 384)
    pool_other = lax.dynamic_slice_in_dim(gps, 4 - 4 * p.c, 4, 0).reshape(512, 384)
    across = ((1,), (0,))
    cg = (dot(x5, pool_mine, across) + dot(x5s, pool_other, across)).astype(BF16)
    cg = cg.reshape(5, 2, 2, 4, 20, 384).transpose(1, 2, 3, 0, 4, 5).reshape(2, 2, 4, 100, 384)
    hgl, cgl = communicate(
        last_kernel, "last", 8, (shape(2, 4, 24, 768), shape(16, 100, 384)), 24, 4,
        hg_sum.reshape(4, 2, 24, 768), cg,
    )
    conv_grad = jnp.sum(cgl.astype(F32).reshape(2, 2, 4, 5, 20, 384), axis=(0, 2))
    conv_grad = conv_grad.transpose(2, 1, 0, 3).reshape(20, 5, 768)
    both = jnp.sum(hgl.astype(F32), axis=1).reshape(2, 24, 4, 192)
    both = both.transpose(1, 2, 0, 3).reshape(24, 4, 384)
    return (block_out[None], conv_grad, both[:, :3], both[:, 3])


def solution(mesh):
    placed = (
        P("dp", "seq", None),
        P("seq", None, "tensor"),
        P("seq", None, "tensor"),
        P("seq", "tensor"),
        P("dp", "seq", "tensor"),
    )
    return jax.shard_map(
        local,
        mesh=mesh,
        in_specs=placed,
        out_specs=(
            P("dp", "seq", "tensor"),
            P(("seq", "dp"), None, "tensor"),
            P(("seq", "dp"), None, "tensor"),
            P(("seq", "dp"), "tensor"),
        ),
        check_vma=False,
    )
```

time: 677 us -> 231 us (0.34)
  waiting for transfers between devices: 491 us -> 0 us
  Pallas kernels: 0 us -> 156 us
  blocking collectives: 38.3 us -> 0 us
  matrix products: 45 us -> 20.1 us
  local copies, waits for them, and re-layouts: 55.7 us -> 35.9 us
  starting transfers between devices: 16.1 us -> 0 us
  between operations: 15.8 us -> 1.34 us
    all_gather x8 -> x0, waiting for transfers between devices: 307 us -> none  [the longest x1 76.9 us: local(): pieces = lax.all_gather(conv_weight, 'seq', axis=0, tiled=True)]
    pallas_call x0 -> x9, Pallas kernels: none -> 156 us  [the longest x8 152 us: communicate(): pl.pallas_call(kernel, name=name, out_shape=outputs, in_specs=[inside if...]
    reduce_scatter x2 -> x0, waiting for transfers between devices: 84.7 us -> none  [the longest x1 67.8 us: local(): lax.psum_scatter(jnp.concatenate([key_part.reshape(lax.axis_size('seq') *...]
    unnamed x15 -> x0, waiting for transfers between devices: 62.3 us -> none
    slice x25 -> x8, local copies, waits for them, and re-layouts: 36.7 us -> 1.68 us  [the longest x1 0.8 us: local(): projected[:, 192:]]
    psum x1 -> x0, waiting for transfers between devices: 27.4 us -> none  [local(): lax.psum(normed_partial.astype(jnp.bfloat16), 'tensor').astype(jnp.float32)]
    dot_general x26 -> x11, matrix products: 42.7 us -> 20.1 us  [dot(): return lax.dot_general(a, b, (dims, ((), ())), preferred_element_type=F32)]
    all_to_all x1 -> x0, blocking collectives: 21.2 us -> none  [local(): lax.all_to_all(activity, 'seq', split_axis=1, concat_axis=0, tiled=True)]
  transfers between devices with their start and end apart: 17 -> 0, of which waited for: 14 -> 0; matrix products, arithmetic and copies ran while one was open for 14% -> 0% of each run, Pallas kernels for 0% -> 0%
where the time goes in v2:
time: 231 us; the launch traced here: 230 us
  Pallas kernels  156 us (68%)
  local copies, waits for them, and re-layouts  35.9 us (16%)
  matrix products  20.1 us (9%)
  other arithmetic  16.9 us (7%)
    pallas_call x8, Pallas kernels, communicate(): pl.pallas_call(kernel, name=name, out_shape=outputs, in_specs=[inside if...  152 us
    dot_general x11, matrix products, dot(): return lax.dot_general(a, b, (dims, ((), ())), preferred_element_type=F32)  20.1 us
    unnamed x53, local copies, waits for them, and re-layouts  9.26 us

profile of v2, /device:TPU:1, one launch (start us, length us, event | category | flops | bytes accessed | tf_op | source)
XLA Modules:
  0.0 230.1 jit_solution(11034974361937719821)
XLA Ops:
  0.7 1.6 fusion.21
  3.3 2.0 reshape.267
  9.8 28.8 %start.1 = (bf16[2,320,512]{2,1,0:T(8,128)(2,1)}, bf16[8,320]{1,0:T(8,128)(2,1)}, bf16[8,320]{1,0:T(8,128)(2,1)}, bf16[5,4,80,768]{3,2,1,0:T(8,128)(2,1)}, bf16[8,24,768]{2,1,0:T(8,128)(2,1)}) custom-call(bf16[4,2,320,128]{3,2,1,0:T(8,128)(2,1)} %bitcast.164, bf16[2,4,8,320]{3,2,1,0:T(8,128)(2,1)} %pad.8.edge_ref, bf16[5,80,768]{2,1,0:T(8,128)(2,1)} %bitcast.179, ...), custom_call_target="tpu_custom_call" | custom-call | tf_op jit(solution)/shard_map/start/pallas_call | solution.py:87
  39.7 1.5 maximum_convert_fusion
  42.2 1.5 copy-done.11
  43.7 2.5 %multiply_convert_fusion.1 = bf16[512,768]{1,0:T(8,128)(2,1)} fusion(bf16[1600,512]{1,0:T(8,128)(2,1)S(1)} %bitcast.143, bf16[1600,768]{1,0:T(8,128)(2,1)S(1)} %bitcast.165), kind=kOutput, calls=%fused_computation.17 | convolution fusion | flops 1259077632 | bytes 4882432 | tf_op jit(solution)/shard_map/dot_general | solution.py:445
  46.2 19.0 %section.1 = (bf16[4,128,768]{2,1,0:T(8,128)(2,1)}, bf16[4,128,768]{2,1,0:T(8,128)(2,1)}, bf16[1600,512]{1,0:T(8,128)(2,1)}, bf16[2,4,2,4,24,768]{5,4,3,2,1,0:T(8,128)(2,1)}) custom-call(bf16[4,128,768]{2,1,0:T(8,128)(2,1)} %bitcast.161, bf16[128,768]{1,0:T(8,128)(2,1)} %bitcast.175, bf16[1600,512]{1,0:T(8,128)(2,1)} %bitcast.144, ...), custom_call_target="tpu_custom_call" | custom-call | tf_op jit(solution)/shard_map/section/pallas_call | solution.py:87
  65.2 2.0 reduce_sum.108.sec_ref
  67.2 19.3 %channels.1 = (bf16[4,128,768]{2,1,0:T(8,128)(2,1)}, bf16[2,4,2,4,24,768]{5,4,3,2,1,0:T(8,128)(2,1)}) custom-call(bf16[128,768]{1,0:T(8,128)(2,1)} %reduce_sum.108.sec_ref, bf16[8,24,768]{2,1,0:T(8,128)(2,1)} %get-tuple-element.33.wq_ref, bf16[2,4,2,4,24,768]{5,4,3,2,1,0:T(8,128)(2,1)} %get-tuple-element.35.wa_ref), custom_call_target="tpu_custom_call", output_to_operand_aliasing={{1}: (2, {})} | custom-call | tf_op jit(solution)/shard_map/channels/pallas_call | solution.py:87
  86.5 1.3 convert_element_type.231
  92.1 2.0 convolution_convert_fusion.1
  94.2 1.2 copy.159
  95.5 2.1 copy-done.5
  99.3 15.1 %keys.1 = bf16[2,4,256,384]{3,2,1,0:T(8,128)(2,1)} custom-call(bf16[256,384]{1,0:T(8,128)(2,1)} %slice.105.kv_ref), custom_call_target="tpu_custom_call" | custom-call | tf_op jit(solution)/shard_map/keys/pallas_call | solution.py:87
  114.4 1.4 copy-done
  115.8 4.0 %shard_map.84 = (bf16[256,192]{1,0:T(8,128)(2,1)S(1)}, bf16[256,192]{1,0:T(8,128)(2,1)S(1)}, bf16[2048,384]{1,0:T(8,128)(2,1)S(1)}) custom-call(bf16[256,192]{1,0:T(8,128)(2,1)S(1)} %slice.104.q_ref, bf16[2048,384]{1,0:T(8,128)(2,1)S(1)} %bitcast.140, bf16[256,192]{1,0:T(8,128)(2,1)S(1)} %copy.162.g_ref), custom_call_target="tpu_custom_call" | custom-call | tf_op jit(solution)/shard_map/pallas_call | solution.py:471
  119.8 1.6 convolution_convert_fusion
  121.7 14.5 %key_grads.1 = (bf16[4,256,384]{2,1,0:T(8,128)(2,1)S(1)}, bf16[4,128,768]{2,1,0:T(8,128)(2,1)S(1)}) custom-call(bf16[2,4,256,384]{3,2,1,0:T(8,128)(2,1)S(1)} %bitcast.142, bf16[4,128,768]{2,1,0:T(8,128)(2,1)S(1)} %bitcast.141), custom_call_target="tpu_custom_call" | custom-call | tf_op jit(solution)/shard_map/key_grads/pallas_call | solution.py:87
  136.4 3.0 %fusion.33 = f32[768,576]{0,1:T(8,128)} fusion(bf16[256,2,768]{2,0,1:T(8,128)(2,1)} %fusion.5, s32[]{:T(128)S(6)} %select_n.33, bf16[256,384]{1,0:T(8,128)(2,1)S(1)} %reduce_sum.113, bf16[256,192]{1,0:T(8,128)(2,1)S(1)} %get-tuple-element.42), kind=kOutput, calls=%fused_computation.55 | convolution fusion | flops 227082240 | bytes 2457604 | tf_op jit(solution)/shard_map/dot_general | solution.py:445
  140.3 2.4 %multiply_reduce_fusion = (f32[256]{0:T(256)S(1)}, bf16[256,1536]{1,0:T(8,128)(2,1)S(1)}) fusion(f32[256,1536]{1,0:T(8,128)} %bitcast.168, bf16[1536,768]{1,0:T(8,128)(2,1)S(1)} %bitcast.153, bf16[256,384]{1,0:T(8,128)(2,1)S(1)} %reduce_sum.113, bf16[256,192]{1,0:T(8,128)(2,1)S(1)} %get-tuple-element.42), kind=kOutput, calls=%fused_computation.13 | convolution fusion | flops 454754048 | bytes 4654080 | tf_op jit(solution)/shard_map/dot_general | solution.py:445
  145.8 14.5 %norm.1 = (bf16[4,128,768]{2,1,0:T(8,128)(2,1)}, bf16[4,128,128]{2,1,0:T(8,128)(2,1)}, bf16[256,768]{1,0:T(8,128)(2,1)}, bf16[256,768]{1,0:T(8,128)(2,1)}, bf16[256,768]{1,0:T(8,128)(2,1)}) custom-call(bf16[4,128,768]{2,1,0:T(8,128)(2,1)} %bitcast.163, bf16[4,128,128]{2,1,0:T(8,128)(2,1)} %bitcast.180, bf16[2,256,768]{2,1,0:T(8,128)(2,1)} %bitcast.159, ...), custom_call_target="tpu_custom_call" | custom-call | tf_op jit(solution)/shard_map/norm/pallas_call | solution.py:87
  160.3 3.1 %add_convert_fusion = bf16[768,576]{0,1:T(8,128)(2,1)} fusion(f32[768,576]{0,1:T(8,128)} %fusion.33, bf16[256,768]{1,0:T(8,128)(2,1)} %get-tuple-element.46, bf16[256,768]{1,0:T(8,128)(2,1)} %get-tuple-element.47), kind=kOutput, calls=%fused_computation.5 | convolution fusion | flops 227377152 | bytes 3375104 | tf_op jit(solution)/shard_map/dot_general | solution.py:445
  163.4 1.6 copy.173
  165.3 1.4 fusion.25
  166.8 1.2 copy_bitcast_fusion.hg_ref
  170.6 17.5 %pool.1 = (bf16[8,128,384]{2,1,0:T(8,128)(2,1)}, bf16[4,8,24,768]{3,2,1,0:T(8,128)(2,1)}) custom-call(bf16[2,128,384]{2,1,0:T(8,128)(2,1)} %fusion.44.gp_ref, bf16[4,8,24,768]{3,2,1,0:T(8,128)(2,1)} %copy_bitcast_fusion.hg_ref), custom_call_target="tpu_custom_call" | custom-call | tf_op jit(solution)/shard_map/pool/pallas_call | solution.py:87
  190.7 2.1 fusion
  192.8 2.2 reshape.260
  195.5 1.2 copy.178.cg_ref
  198.1 23.1 %last.1 = (bf16[2,4,24,768]{3,2,1,0:T(8,128)(2,1)}, bf16[16,100,384]{2,1,0:T(8,128)(2,1)}) custom-call(bf16[4,2,24,768]{3,2,1,0:T(8,128)(2,1)} %bitcast.174, bf16[2,2,4,100,384]{4,3,2,1,0:T(8,128)(2,1)} %copy.178.cg_ref), custom_call_target="tpu_custom_call" | custom-call | tf_op jit(solution)/shard_map/last/pallas_call | solution.py:87
  221.2 3.0 %reshape.277 = f32[2,2,4,5,20,384]{5,4,3,2,1,0:T(8,128)} reshape(bf16[16,100,384]{2,1,0:T(8,128)(2,1)} %get-tuple-element.52) | data formatting | bytes 3686400 | tf_op jit(solution)/shard_map/reshape | solution.py:599
  224.2 2.1 reduce_sum.119
  (120 shorter events, 29.2 us)
Async XLA Ops:
  0.6 2.6 %copy-start.10 = (bf16[1,256,1280]{2,1,0:T(8,128)(2,1)S(1)}, bf16[1,256,1280]{2,1,0:T(8,128)(2,1)}, u32[]{:S(2)}) copy-start(bf16[1,256,1280]{2,1,0:T(8,128)(2,1)} %param.5) | copy-start | bytes 1966084
  6.2 1.4 copy-start.19
  6.6 1.4 copy-start.21
  41.6 2.0 copy-start.11
  42.2 4.0 %copy-start.1 = (bf16[5,320,512]{2,1,0:T(8,128)(2,1)}, bf16[5,320,512]{2,1,0:T(8,128)(2,1)S(1)}, u32[]{:S(2)}) copy-start(bf16[5,320,512]{2,1,0:T(8,128)(2,1)S(1)} %fusion.37) | copy-start | bytes 4915204
  87.8 1.1 copy-start.9
  89.2 1.3 copy-start.17
  91.2 0.9 copy-start.3
  95.4 2.2 copy-start.5
  95.5 2.9 %copy-start.13 = (f32[32,8,2,768]{3,1,2,0:T(8,128)}, f32[32,8,2,768]{3,1,2,0:T(8,128)S(1)}, u32[]{:S(2)}) copy-start(f32[32,8,2,768]{3,1,2,0:T(8,128)S(1)} %copy.187) | copy-start | bytes 4718596
  114.4 1.4 copy-start
  136.4 3.9 %copy-start.6 = (bf16[2,4,2,4,24,768]{5,4,3,2,1,0:T(8,128)(2,1)S(1)}, bf16[2,4,2,4,24,768]{5,4,3,2,1,0:T(8,128)(2,1)}, u32[]{:S(2)}) copy-start(bf16[2,4,2,4,24,768]{5,4,3,2,1,0:T(8,128)(2,1)} %get-tuple-element.37) | copy-start | bytes 7077892
  142.9 1.9 copy-start.4
  163.4 1.6 copy-start.7
  166.8 1.2 copy-start.16
  168.1 0.9 copy-start.20
  168.1 1.0 copy-start.8
  168.2 1.2 copy-start.15
  170.6 18.7 %copy-start.2 = (bf16[5,320,512]{2,1,0:T(8,128)(2,1)S(1)}, bf16[5,320,512]{2,1,0:T(8,128)(2,1)}, u32[]{:S(2)}) copy-start(bf16[5,320,512]{2,1,0:T(8,128)(2,1)} %copy-done.1) | copy-start | bytes 4915204
  189.3 1.4 copy-start.12
  195.5 1.7 copy-start.14
  224.2 3.2 %copy-start.18 = (bf16[2,4,24,768]{3,2,1,0:T(8,128)(2,1)S(1)}, bf16[2,4,24,768]{3,2,1,0:T(8,128)(2,1)}, u32[]{:S(2)}) copy-start(bf16[2,4,24,768]{3,2,1,0:T(8,128)(2,1)} %get-tuple-element.53) | copy-start | bytes 884740

commit v3 on v0

v3 whole, which is shorter than its diff:
```python
import jax
import jax.numpy as jnp
from jax import lax
from jax.experimental import pallas as pl
from jax.experimental.pallas import tpu as pltpu
from jax.sharding import PartitionSpec as P

HEAD_DIM = 192
EPSILON = 1e-06
MESH = pl.DeviceIdType.MESH
BF16 = jnp.bfloat16
F32 = jnp.float32


class Place:
    def __init__(self):
        self.s = lax.axis_index("seq")
        self.zh = lax.div(self.s, 8)
        self.x = lax.rem(lax.div(self.s, 2), 4)
        self.c = lax.rem(self.s, 2)
        self.t = lax.axis_index("tensor")
        self.d = lax.axis_index("dp")
        self.z = 2 * self.zh + self.t

    def at(self, x=None, zh=None, c=None, t=None, d=None):
        x = self.x if x is None else x
        zh = self.zh if zh is None else zh
        c = self.c if c is None else c
        return {
            "seq": zh * 8 + x * 2 + c,
            "tensor": self.t if t is None else t,
            "dp": self.d if d is None else d,
        }

    def along_x(self, k):
        return lax.rem(self.x + k, 4)

    def along_y(self, k):
        return lax.rem(self.d + k, 4)

    def along_z(self, k):
        return lax.rem(self.z + k, 4)

    def at_z(self, z):
        return self.at(zh=lax.div(z, 2), t=lax.rem(z, 2))

    @property
    def sibling(self):
        return self.at(c=1 - self.c)


def remote(src, dst, send, recv, target):
    return pltpu.make_async_remote_copy(
        src_ref=src, dst_ref=dst, send_sem=send, recv_sem=recv, device_id=target, device_id_type=MESH
    )


def greet(targets):
    barrier = pltpu.get_barrier_semaphore()
    for condition, target in targets:
        if condition is None:
            pl.semaphore_signal(barrier, inc=1, device_id=target, device_id_type=MESH)
        else:

            @pl.when(condition)
            def _(target=target):
                pl.semaphore_signal(barrier, inc=1, device_id=target, device_id_type=MESH)

    return barrier


def under(condition, action):
    if condition is None:
        action()
    else:

        @pl.when(condition)
        def _():
            action()


def communicate(kernel, name, collective, outputs, remotes, locals_, *operands, aliases=None, vmem=(), scratch=()):
    anywhere = pl.BlockSpec(memory_space=pl.ANY)
    inside = pl.BlockSpec(memory_space=pltpu.VMEM)
    return pl.pallas_call(
        kernel,
        name=name,
        out_shape=outputs,
        in_specs=[inside if n in vmem else anywhere for n in range(len(operands))],
        out_specs=tuple([anywhere] * len(outputs)),
        scratch_shapes=list(scratch)
        + [
            pltpu.SemaphoreType.DMA((remotes,)),
            pltpu.SemaphoreType.DMA((remotes,)),
            pltpu.SemaphoreType.DMA((locals_,)),
        ],
        input_output_aliases=aliases or {},
        compiler_params=pltpu.CompilerParams(
            collective_id=collective, has_side_effects=True, vmem_limit_bytes=16 * 1024 * 1024 if vmem else None
        ),
    )(*operands)


class Moves:
    def __init__(self, place, send, recv, local):
        self.place, self.send, self.recv, self.local = place, send, recv, local
        self.sends, self.receives, self.locals = [], [], []
        self.used = 0
        self.used_local = 0

    def slots(self, count):
        first = self.used
        self.used += count
        return first

    def push(self, src, dst, target, slot, recv_slot=None, when=None):
        recv_slot = slot if recv_slot is None else recv_slot
        copy = remote(src, dst, self.send.at[slot], self.recv.at[recv_slot], target)
        under(when, copy.start)
        self.sends.append((when, copy.wait_send))

    def keep(self, src, dst, when=None):
        copy = pltpu.make_async_copy(src, dst, self.local.at[self.used_local])
        self.used_local += 1
        under(when, copy.start)
        self.locals.append((when, copy.wait))

    def arrival(self, dst, slot, when=None):
        place = self.place
        copy = remote(dst, dst, self.send.at[0], self.recv.at[slot], place.at())
        return lambda: under(when, copy.wait_recv)

    def expect(self, dst, slot, when=None):
        self.receives.append(self.arrival(dst, slot, when))

    def settle(self):
        for wait in self.receives:
            wait()
        for when, wait in self.locals + self.sends:
            under(when, wait)


def z_ring(p):
    return [(None, p.at_z(p.along_z(k))) for k in range(1, 4)]


def y_ring(p):
    return [(None, p.at(d=p.along_y(k))) for k in range(1, 4)]


def last_kernel(hg_ref, cg_ref, hgs_ref, cgs_ref, send, recv, local):
    p = Place()
    peers = []
    for zh in range(2):
        for c in range(2):
            for k in range(4):
                here = k == 0
                target = p.at(zh=zh, c=c, d=p.along_y(k))
                peers.append((jnp.logical_or(zh != p.zh, c != p.c) if here else None, target))
    for zh in range(2):
        for k in range(1, 4):
            peers.append((None, p.at(zh=zh, x=p.along_x(k), c=p.zh)))
    barrier = greet(peers)
    pl.semaphore_wait(barrier, 15 + 6)
    moves = Moves(p, send, recv, local)
    b = moves.slots(16)
    me = 8 * p.zh + 4 * p.c + p.d
    for k in (8, 12, 4, 2, 10, 14, 6, 1, 3, 9, 11, 13, 15, 5, 7, 0):
        other = lax.rem(me + k, 16)
        zh, c, d = lax.div(other, 8), lax.rem(lax.div(other, 4), 2), lax.rem(other, 4)
        src = cg_ref.at[zh, c, d]
        if k == 0:
            moves.keep(src, cgs_ref.at[me])
        else:
            moves.push(src, cgs_ref.at[me], p.at(zh=zh, c=c, d=d), b + k)
            moves.expect(cgs_ref.at[lax.rem(me + 16 - k, 16)], b + k)
    a = moves.slots(8)
    for k in range(8):
        other = lax.rem(2 * p.x + k, 8)
        x, c = lax.div(other, 2), lax.rem(other, 2)
        src, dst = hg_ref.at[x, c], hgs_ref.at[p.zh, p.x]
        alone = jnp.logical_and(jnp.logical_and(x == p.x, c == p.c), p.zh == p.c)
        if k < 2:
            moves.push(src, dst, p.at(x=x, zh=p.c, c=c), a + k, a + 4 * p.zh + p.x, jnp.logical_not(alone))
            moves.keep(src, dst, alone)
        else:
            moves.push(src, dst, p.at(x=x, zh=p.c, c=c), a + k, a + 4 * p.zh + p.x)
    for zh in range(2):
        for x in range(4):
            alone = jnp.logical_and(jnp.logical_and(x == p.x, zh == p.zh), p.zh == p.c)
            moves.expect(hgs_ref.at[zh, x], a + 4 * zh + x, jnp.logical_not(alone))
    moves.settle()

def dot(a, b, dims):
    return lax.dot_general(a, b, (dims, ((), ())), preferred_element_type=F32)


NN = ((1,), (0,))
NT = ((1,), (1,))
TN = ((0,), (0,))


def main_kernel(
    at_ref, edge_ref, cw_ref, wp_ref, cot_ref,
    out_ref, hgo_ref, cg_ref,
    xt_ref, low_ref, high_ref, cwf_ref, wf_ref, cots_ref, x5_ref, x5s_ref, part_ref, rs_ref, sec_ref, secs_ref,
    inv_ref, nb_ref, nl_ref, cl_ref, kv_ref, st_ref, dp_ref, p16_ref, ds_ref, dkv_ref, buf_ref, sum_ref, dkvs_ref,
    bo_ref, bos_ref, gpa_ref, gpas_ref, norm_ref, norms_ref, spread_ref, spreads_ref, hg_ref, hgs_ref, gp_ref, gps_ref,
    send, recv, local,
):
    p = Place()
    scale = HEAD_DIM ** (-0.5)
    peers = [(None, {"seq": lax.rem(p.s + k, 16), "tensor": p.t, "dp": p.d}) for k in range(1, 16)]
    peers += [(None, p.at(t=1 - p.t)), (None, p.at(zh=1 - p.zh, t=1 - p.t))] + y_ring(p)
    barrier = greet(peers)
    pl.semaphore_wait(barrier, 20)
    moves = Moves(p, send, recv, local)
    arrival = moves.arrival

    first = moves.slots(4)
    mine = cwf_ref.at[:, 2 * p.zh + p.c]
    moves.push(cw_ref, mine, p.at(zh=1 - p.zh), first)
    moves.push(cw_ref, mine, p.sibling, first + 1)
    moves.keep(cw_ref, mine)
    from_z = cwf_ref.at[:, 2 * (1 - p.zh) + p.c]

    a = moves.slots(4)
    core = lax.div(p.x, 2)
    slot = 2 * lax.rem(p.x, 2) + p.c
    spot = xt_ref.at[slot]
    for k in (2, 1, 3, 0):
        x = p.along_x(k)
        if k == 0:
            moves.push(at_ref.at[x], spot, p.at(c=core), a, a + slot, core != p.c)
            moves.keep(at_ref.at[x], spot, core == p.c)
        else:
            moves.push(at_ref.at[x], spot, p.at(x=x, c=core), a + k, a + slot)
    base = 8 * p.zh + 4 * p.c
    halo = []
    for up, end_ref in ((True, low_ref), (False, high_ref)):
        e = moves.slots(4)
        if up:
            sends = jnp.logical_and(lax.rem(p.s, 4) == 3, p.s != 15)
            block = lax.rem(p.s + 1, 16)
        else:
            sends = jnp.logical_and(lax.rem(p.s, 4) == 0, p.s != 0)
            block = lax.rem(p.s + 15, 16)
        zh, c = lax.div(block, 8), lax.div(lax.rem(block, 8), 4)
        for k in range(4):
            x = p.along_x(k)
            src = edge_ref.at[1 if up else 0, x]
            target = p.at(x=x, zh=zh, c=c)
            if k == 0:
                alone = jnp.logical_and(zh == p.zh, c == p.c)
                moves.push(src, end_ref, target, e, e, jnp.logical_and(sends, jnp.logical_not(alone)))
                moves.keep(src, end_ref, jnp.logical_and(sends, alone))
            else:
                moves.push(src, end_ref, target, e + k, e, sends)
        if up:
            halo.append(arrival(end_ref, e, jnp.logical_and(base != 0, base - 1 != p.s)))
        else:
            halo.append(arrival(end_ref, e, jnp.logical_and(base != 12, base + 4 != p.s)))

    def quarter(zh, x, c, d):
        rows = pl.ds(pl.multiple_of(48 * lax.div(d, 2), 16), 48)
        columns = pl.ds(pl.multiple_of(384 * lax.rem(d, 2), 128), 384)
        return wf_ref.at[zh, x, c, rows, columns]

    def quarters(c, d):
        rows = pl.ds(pl.multiple_of(48 * lax.div(d, 2), 16), 48)
        columns = pl.ds(pl.multiple_of(384 * lax.rem(d, 2), 128), 384)
        return wf_ref.at[:, :, c, rows, columns]

    w = moves.slots(8)
    shard = 4 * p.zh + p.x
    own_quarter = quarter(p.zh, p.x, p.c, p.d)
    quarter_arrivals = []
    for k in range(8):
        other = lax.rem(shard + k, 8)
        zh, x = lax.div(other, 4), lax.rem(other, 4)
        src = wp_ref.at[zh, p.d]
        if k == 0:
            copy = pltpu.make_async_copy(src, own_quarter, local.at[moves.used_local])
            moves.used_local += 1
            copy.start()
            quarter_arrivals.append(copy.wait)
        else:
            moves.push(src, own_quarter, p.at(x=x, zh=zh), w + k)
            other = lax.rem(shard + 8 - k, 8)
            quarter_arrivals.append(arrival(quarter(lax.div(other, 4), lax.rem(other, 4), p.c, p.d), w + k))

    cot_first = moves.slots(4)
    cot_own = pltpu.make_async_copy(cot_ref, cots_ref.at[p.z], local.at[moves.used_local])
    moves.used_local += 1
    cot_own.start()
    cot_arrivals = [cot_own.wait]
    for k in (2, 1, 3):
        moves.push(cot_ref, cots_ref.at[p.z], p.at_z(p.along_z(k)), cot_first + k)
        cot_arrivals.append(arrival(cots_ref.at[p.along_z(4 - k)], cot_first + k))

    arrival(from_z, first)()
    moves.push(from_z, from_z, p.sibling, first + 2)
    for wait in quarter_arrivals:
        wait()
    y = moves.slots(8)
    moves.push(quarters(p.c, p.d), quarters(p.c, p.d), p.sibling, y)
    for k in (2, 1, 3):
        moves.push(quarters(p.c, p.d), quarters(p.c, p.d), p.at(d=p.along_y(k)), y + k)

    for n in range(4):
        x, c = 2 * p.c + n // 2, n % 2
        arrival(xt_ref.at[n], a + n, jnp.logical_or(x != p.x, c != p.c))()
    for wait in halo:
        wait()
    for when, wait in moves.locals:
        under(when, wait)
    moves.locals = []
    pick = (lax.broadcasted_iota(jnp.int32, (16, 128), 0) == lax.broadcasted_iota(jnp.int32, (16, 128), 1)).astype(BF16)
    zero_rows = jnp.zeros((16, 384), BF16)
    low = dot(jnp.where(base != 0, low_ref[...], zero_rows), pick, TN)[:320]
    high = dot(jnp.where(base != 12, high_ref[...], zero_rows), pick, TN)[:320]
    even = jnp.concatenate([xt_ref[n, 0] for n in range(4)], axis=1).astype(F32)
    odd = jnp.concatenate([xt_ref[n, 1] for n in range(4)], axis=1).astype(F32)
    lane = lax.broadcasted_iota(jnp.int32, (320, 512), 1)
    both = even + odd
    x5_ref[pl.ds(640, 320), :] = both.astype(BF16)
    x5_ref[pl.ds(0, 320), :] = jnp.where(lane == 0, low[:, 0:1] + low[:, 1:2], pltpu.roll(both, 1, 1)).astype(BF16)
    x5_ref[pl.ds(1280, 320), :] = jnp.where(
        lane == 511, high[:, 0:1] + high[:, 1:2], pltpu.roll(both, 511, 1)
    ).astype(BF16)
    x5_ref[pl.ds(320, 320), :] = (even + jnp.where(lane == 0, low[:, 1:2], pltpu.roll(odd, 1, 1))).astype(BF16)
    x5_ref[pl.ds(960, 320), :] = (odd + jnp.where(lane == 511, high[:, 0:1], pltpu.roll(even, 511, 1))).astype(BF16)
    arrival(cwf_ref.at[:, 2 * p.zh + 1 - p.c], first + 1)()
    arrival(cwf_ref.at[:, 2 * (1 - p.zh) + 1 - p.c], first + 2)()
    b = moves.slots(4)
    for half in range(2):
        conv = dot(x5_ref[:, 256 * half : 256 * half + 256], cwf_ref[...].reshape(1600, 768), TN) * 0.5
        for n in range(2):
            slot = 2 * half + n
            part_ref[slot] = conv[128 * n : 128 * n + 128].astype(BF16)
            x = 2 * p.c + half
            alone = jnp.logical_and(x == p.x, n == p.c)
            moves.push(part_ref.at[slot], rs_ref.at[p.x], p.at(x=x, c=n), b + slot, b + p.x, jnp.logical_not(alone))
            moves.keep(part_ref.at[slot], rs_ref.at[p.x], alone)
    other_x5 = moves.slots(1)
    moves.push(x5_ref, x5s_ref, p.sibling, other_x5)
    for x in range(4):
        arrival(rs_ref.at[x], b + x, jnp.logical_or(p.x != x, core != p.c))()
    for when, wait in moves.locals:
        under(when, wait)
    moves.locals = []
    total = rs_ref[0].astype(F32)
    for x in range(1, 4):
        total = total + rs_ref[x].astype(F32)
    sec_ref[...] = total.astype(BF16)
    secs_ref[p.z] = total.astype(BF16)
    g = moves.slots(4)
    for k in (2, 1, 3):
        moves.push(sec_ref, secs_ref.at[p.z], p.at_z(p.along_z(k)), g + k)

    for k in (1, 3, 2):
        d = p.along_y(4 - k)
        arrival(quarters(p.c, d), y + k)()
        moves.push(quarters(p.c, d), quarters(p.c, d), p.sibling, y + 3 + k)
    for wait in cot_arrivals:
        wait()
    o = moves.slots(4)
    for zh in range(2):
        cl_ref[zh] = cots_ref[2 * zh + p.c]
        moves.push(cots_ref.at[2 * zh + 1 - p.c], cl_ref.at[2 + zh], p.sibling, o + zh)
    arrival(quarters(1 - p.c, p.d), y)()
    for k in (1, 3, 2):
        arrival(quarters(1 - p.c, p.along_y(4 - k)), y + 3 + k)()

    def kv_rows(zh):
        return wf_ref[zh, :, :, :, :640].reshape(768, 640)

    def output_rows(zh):
        return wf_ref[zh, :, :, :, 512:].reshape(768, 256)

    def channels(ref, t):
        return jnp.concatenate([ref[t], ref[2 + t]], axis=0)

    wide_lane = lax.broadcasted_iota(jnp.int32, (256, 256), 1)
    grad_att = dot(channels(cots_ref, 0), output_rows(0), NN) + dot(channels(cots_ref, 1), output_rows(1), NN)
    grad_att = jnp.where(wide_lane < 64, 0.0, grad_att).astype(BF16)

    for k in (2, 1, 3):
        arrival(secs_ref.at[p.along_z(4 - k)], g + k)()
    for zh in range(2):
        left, right = secs_ref[2 * zh].astype(F32), secs_ref[2 * zh + 1].astype(F32)
        squares = jnp.sum(left * left, axis=1, keepdims=True) + jnp.sum(right * right, axis=1, keepdims=True)
        inverse = lax.rsqrt(squares * (1.0 / 1536) + EPSILON)
        inv_ref[zh] = jnp.broadcast_to(inverse, (128, 128))
        nb_ref[2 * zh] = (left * inverse).astype(BF16)
        nb_ref[2 * zh + 1] = (right * inverse).astype(BF16)
    projected = dot(channels(nb_ref, 0), kv_rows(0), NN) + dot(channels(nb_ref, 1), kv_rows(1), NN)
    kv_ref[p.c, p.x] = projected[:, :384].astype(BF16)
    query = jnp.where(wide_lane < 192, projected[:, 384:], 0.0).astype(BF16)
    q = moves.slots(8)
    mine = kv_ref.at[p.c, p.x]
    for k in (2, 1, 3):
        moves.push(mine, mine, p.at(x=p.along_x(k)), q + k)
    moves.push(mine, mine, p.sibling, q)
    for zh in range(2):
        nl_ref[zh] = nb_ref[2 * zh + p.c]
        moves.push(nb_ref.at[2 * zh + 1 - p.c], nl_ref.at[2 + zh], p.sibling, o + 2 + zh)
    for k in (1, 3, 2):
        spot = kv_ref.at[p.c, p.along_x(4 - k)]
        arrival(spot, q + k)()
        moves.push(spot, spot, p.sibling, q + 3 + k)
    arrival(kv_ref.at[1 - p.c, p.x], q)()
    for k in (1, 3, 2):
        arrival(kv_ref.at[1 - p.c, p.along_x(4 - k)], q + 3 + k)()

    highest = None
    for n in range(8):
        scores = dot(kv_ref[n // 4, n % 4, :, :256], query, NT) * scale
        st_ref[n] = scores
        top = jnp.max(scores, axis=0, keepdims=True)
        highest = top if highest is None else jnp.maximum(highest, top)
    sums = jnp.zeros((1, 256), F32)
    for n in range(8):
        unnormed = jnp.exp(st_ref[n] - highest)
        st_ref[n] = unnormed
        sums = sums + jnp.sum(unnormed, axis=0, keepdims=True)
    share = 1.0 / sums
    centre = jnp.zeros((1, 256), F32)
    for n in range(8):
        weights = st_ref[n] * share
        grad_prob = dot(kv_ref[n // 4, n % 4, :, 128:], grad_att, NT)
        centre = centre + jnp.sum(weights * grad_prob, axis=0, keepdims=True)
        st_ref[n] = weights
        dp_ref[n] = grad_prob
        p16_ref[n] = weights.astype(BF16)
    r = moves.slots(8)

    def key_grads(c, x):
        n = 4 * c + x
        grad_score = (st_ref[n] * (dp_ref[n] - centre)).astype(BF16)
        ds_ref[n] = grad_score
        keys = dot(grad_score, query, NN) * scale
        values = dot(p16_ref[n], grad_att, NN)
        return jnp.concatenate([keys[:, :128], keys[:, 128:] + values[:, :128], values[:, 128:]], axis=1)

    for k in (2, 1, 3, 0):
        dkv_ref[k] = key_grads(1 - p.c, p.along_x(k)).astype(BF16)
        moves.push(dkv_ref.at[k], buf_ref.at[k], p.sibling, r + k)
    for k in (2, 1, 3, 0):
        x = p.along_x(k)
        here = key_grads(p.c, x)
        arrival(buf_ref.at[k], r + k)()
        sum_ref[k] = (here + buf_ref[k].astype(F32)).astype(BF16)
        if k:
            moves.push(sum_ref.at[k], dkvs_ref.at[p.x], p.at(x=x), r + 4 + k)
    dkvs_ref[p.x] = sum_ref[0]

    def rows8(ref, first, last):
        return ref[:, :, :, first:last].reshape(2048, last - first)

    attended = dot(p16_ref[...].reshape(2048, 256), rows8(kv_ref, 128, 384), TN)
    attended = jnp.where(wide_lane < 64, 0.0, attended).astype(BF16)
    grad_query = dot(ds_ref[...].reshape(2048, 256), rows8(kv_ref, 0, 256), TN) * scale
    grad_query = jnp.where(wide_lane < 192, grad_query, 0.0).astype(BF16)
    gpa_ref[:, 384:512] = grad_query[:, :128]
    gpa_ref[:, 512:640] = grad_query[:, 128:] + attended[:, :128]
    gpa_ref[:, 640:] = attended[:, 128:]
    u = moves.slots(4)
    for t in range(2):
        block = dot(attended, output_rows(t), NT).astype(BF16)
        bo_ref[t] = block[:128]
        bo_ref[2 + t] = block[128:]
    for k in (2, 1, 3):
        z = p.along_z(k)
        moves.push(bo_ref.at[z], bos_ref.at[p.z], p.at_z(z), u + k)
    bos_ref[p.z] = bo_ref[p.z]

    for k in (1, 3, 2):
        arrival(dkvs_ref.at[p.along_x(4 - k)], r + 4 + k)()
    total = dkvs_ref[0].astype(F32)
    for x in range(1, 4):
        total = total + dkvs_ref[x].astype(F32)
    grad_kv = total.astype(BF16)
    gpa_ref[:, :384] = grad_kv
    h = moves.slots(5)
    moves.push(gpa_ref, gpas_ref, p.sibling, h)
    grad_proj = jnp.concatenate([grad_kv, grad_query], axis=1)
    spread = jnp.zeros((256, 1), F32)
    for t in range(2):
        block = dot(grad_proj, kv_rows(t), NT)
        spread = spread + jnp.sum(block * channels(secs_ref, t).astype(F32), axis=1, keepdims=True)
        rounded = block.astype(BF16)
        norm_ref[t] = rounded[:128]
        norm_ref[2 + t] = rounded[128:]
    spread = spread * (1.0 / 1536)
    for zh in range(2):
        spread_ref[zh] = jnp.broadcast_to(spread[128 * zh : 128 * zh + 128], (128, 128))
    m = moves.slots(8)
    for k in (2, 1, 3):
        z = p.along_z(k)
        moves.push(norm_ref.at[z], norms_ref.at[p.z], p.at_z(z), m + k)
        moves.push(spread_ref.at[lax.div(z, 2)], spreads_ref.at[p.z], p.at_z(z), m + 4 + k)
    norms_ref[p.z] = norm_ref[p.z]
    spreads_ref[p.z] = spread_ref[p.zh]

    for n in range(4):
        arrival((cl_ref if n < 2 else nl_ref).at[2 + n % 2], o + n)()
    arrival(gpas_ref, h)()
    grads = jnp.concatenate([gpa_ref[...], gpas_ref[...]], axis=0)
    head_part = dot(nl_ref[...].reshape(512, 768), grads[:, :640], TN)
    output_part = dot(cl_ref[...].reshape(512, 768), grads[:, 512:], TN)
    tile_lane = lax.broadcasted_iota(jnp.int32, (768, 128), 1)
    middle = jnp.where(tile_lane < 64, head_part[:, 512:], output_part[:, :128])
    parts = jnp.concatenate([head_part[:, :512], middle, output_part[:, 128:]], axis=1)
    for n in range(8):
        for d in range(4):
            row = 96 * n + 24 * d
            hg_ref[d, n] = parts[row : row + 24].astype(BF16)
    for k in (2, 1, 3):
        d = p.along_y(k)
        moves.push(hg_ref.at[d], hgs_ref.at[p.d], p.at(d=d), h + 1 + k)
    hgs_ref[p.d] = hg_ref[p.d]

    for k in (1, 3, 2):
        arrival(bos_ref.at[p.along_z(4 - k)], u + k)()
    total = sec_ref[...].astype(F32)
    projected_out = bos_ref[0].astype(F32)
    for z in range(1, 4):
        projected_out = projected_out + bos_ref[z].astype(F32)
    out_ref[...] = (total + projected_out).astype(BF16)

    for k in (1, 3, 2):
        arrival(norms_ref.at[p.along_z(4 - k)], m + k)()
        arrival(spreads_ref.at[p.along_z(4 - k)], m + 4 + k)()
    grad_normed = norms_ref[0].astype(F32)
    mean = spreads_ref[0]
    for z in range(1, 4):
        grad_normed = grad_normed + norms_ref[z].astype(F32)
        mean = mean + spreads_ref[z]
    inverse = inv_ref[p.zh][:, :1]
    grad_section = cots_ref[p.z].astype(F32) + inverse * grad_normed - inverse * inverse * inverse * total * mean[:, :1]
    grad_pool = (0.5 * grad_section).astype(BF16)
    gp_ref[0] = grad_pool[:, :384]
    gp_ref[1] = grad_pool[:, 384:]
    j = moves.slots(8)
    block = 2 * p.x + p.c
    for k in (4, 5, 2, 3, 6, 7, 1):
        other = lax.rem(block + k, 8)
        x, c = lax.div(other, 2), lax.rem(other, 2)
        moves.push(gp_ref.at[c], gps_ref.at[block], p.at(x=x, c=c), j + k)
    gps_ref[block] = gp_ref[p.c]
    for k in (1, 3, 2):
        arrival(hgs_ref.at[p.along_y(4 - k)], h + 1 + k)()
    rows = hgs_ref[0].astype(F32)
    for d in range(1, 4):
        rows = rows + hgs_ref[d].astype(F32)
    hgo_ref[...] = rows.astype(BF16)

    arrival(x5s_ref, other_x5)()
    for k in (1, 7, 6, 2, 3, 4, 5):
        arrival(gps_ref.at[lax.rem(block + 8 - k, 8)], j + k)()
    here = gps_ref[pl.ds(4 * p.c, 4)].reshape(512, 384)
    there = gps_ref[pl.ds(4 - 4 * p.c, 4)].reshape(512, 384)
    cg_ref[...] = (dot(x5_ref[...], here, NN) + dot(x5s_ref[...], there, NN)).astype(BF16)
    moves.settle()


def main_call(at, edges, cw, wp, cot):
    anywhere = pl.BlockSpec(memory_space=pl.ANY)
    inside = pl.BlockSpec(memory_space=pltpu.VMEM)

    def vmem(*dims, dtype=BF16):
        return pltpu.VMEM(dims, dtype)

    scratch = [
        vmem(4, 2, 320, 128), vmem(16, 384), vmem(16, 384), vmem(5, 4, 80, 768), vmem(2, 4, 2, 96, 768),
        vmem(4, 128, 768), vmem(1600, 512), vmem(1600, 512), vmem(4, 128, 768), vmem(4, 128, 768),
        vmem(128, 768), vmem(4, 128, 768),
        vmem(2, 128, 128, dtype=F32), vmem(4, 128, 768), vmem(4, 128, 768), vmem(4, 128, 768),
        vmem(2, 4, 256, 384), vmem(8, 256, 256, dtype=F32), vmem(8, 256, 256, dtype=F32),
        vmem(8, 256, 256), vmem(8, 256, 256), vmem(4, 256, 384), vmem(4, 256, 384), vmem(4, 256, 384),
        vmem(4, 256, 384),
        vmem(4, 128, 768), vmem(4, 128, 768), vmem(256, 768), vmem(256, 768), vmem(4, 128, 768), vmem(4, 128, 768),
        vmem(2, 128, 128, dtype=F32), vmem(4, 128, 128, dtype=F32),
        vmem(4, 8, 24, 768), vmem(4, 8, 24, 768), vmem(2, 128, 384), vmem(8, 128, 384),
        pltpu.SemaphoreType.DMA((112,)), pltpu.SemaphoreType.DMA((112,)), pltpu.SemaphoreType.DMA((12,)),
    ]
    return pl.pallas_call(
        main_kernel,
        name="main",
        out_shape=(shape(128, 768), shape(8, 24, 768), shape(1600, 384)),
        in_specs=[anywhere] * 5,
        out_specs=(inside,) * 3,
        scratch_shapes=scratch,
        compiler_params=pltpu.CompilerParams(
            collective_id=1, has_side_effects=True, vmem_limit_bytes=60 * 1024 * 1024
        ),
    )(at, edges, cw, wp, cot)


def shape(*dims):
    return jax.ShapeDtypeStruct(dims, BF16)


def local(section_input, conv_weight, head_weight, output_weight, cotangent):
    activity = jax.nn.gelu(section_input[0].astype(F32), approximate=True).astype(BF16)
    bins = activity.reshape(128, 2, 2, 4, 160)
    at = bins.transpose(3, 1, 2, 4, 0).reshape(4, 2, 320, 128)
    edges = jnp.stack([bins[0], bins[127]]).transpose(0, 3, 1, 2, 4).reshape(2, 4, 2, 320)
    edges = jnp.pad(edges, ((0, 0), (0, 0), (0, 14), (0, 64)))
    cw = conv_weight.transpose(1, 0, 2)
    heads = head_weight.reshape(96, 3, 2, 192)
    wp = jnp.stack([heads[:, 1], heads[:, 2], heads[:, 0], output_weight.reshape(96, 2, 192)], axis=2)
    wp = wp.reshape(2, 48, 2, 2, 384).transpose(2, 0, 3, 1, 4).reshape(2, 4, 48, 384)
    block_out, hg_sum, cg = main_call(at, edges, cw, wp, cotangent[0])
    cg = cg.reshape(5, 2, 2, 4, 20, 384).transpose(1, 2, 3, 0, 4, 5).reshape(2, 2, 4, 100, 384)
    hgl, cgl = communicate(
        last_kernel, "last", 8, (shape(2, 4, 24, 768), shape(16, 100, 384)), 24, 4,
        hg_sum.reshape(4, 2, 24, 768), cg,
    )
    conv_grad = jnp.sum(cgl.astype(F32).reshape(2, 2, 4, 5, 20, 384), axis=(0, 2))
    conv_grad = conv_grad.transpose(2, 1, 0, 3).reshape(20, 5, 768)
    both = jnp.sum(hgl.astype(F32), axis=1).reshape(2, 24, 4, 192)
    both = both.transpose(1, 2, 0, 3).reshape(24, 4, 384)
    head_grad = jnp.stack([both[:, 2], both[:, 0], both[:, 1]], axis=1)
    return (block_out[None], conv_grad, head_grad, both[:, 3])


def solution(mesh):
    placed = (
        P("dp", "seq", None),
        P("seq", None, "tensor"),
        P("seq", None, "tensor"),
        P("seq", "tensor"),
        P("dp", "seq", "tensor"),
    )
    return jax.shard_map(
        local,
        mesh=mesh,
        in_specs=placed,
        out_specs=(
            P("dp", "seq", "tensor"),
            P(("seq", "dp"), None, "tensor"),
            P(("seq", "dp"), None, "tensor"),
            P(("seq", "dp"), "tensor"),
        ),
        check_vma=False,
    )
```

time: 677 us -> 152 us (0.22)
  waiting for transfers between devices: 491 us -> 0 us
  Pallas kernels: 0 us -> 130 us
  matrix products: 45 us -> 0 us
  blocking collectives: 38.3 us -> 0 us
  local copies, waits for them, and re-layouts: 55.7 us -> 17.8 us
  starting transfers between devices: 16.1 us -> 0 us
  between operations: 15.8 us -> 0.81 us
  other arithmetic: 12.9 us -> 3.52 us
    all_gather x8 -> x0, waiting for transfers between devices: 307 us -> none  [the longest x1 76.9 us: local(): pieces = lax.all_gather(conv_weight, 'seq', axis=0, tiled=True)]
    pallas_call x0 -> x2, Pallas kernels: none -> 130 us  [the longest x1 107 us: main_call(): pl.pallas_call(main_kernel, name='main', out_shape=(shape(128, 768), shap...]
    reduce_scatter x2 -> x0, waiting for transfers between devices: 84.7 us -> none  [the longest x1 67.8 us: local(): lax.psum_scatter(jnp.concatenate([key_part.reshape(lax.axis_size('seq') *...]
    unnamed x15 -> x0, waiting for transfers between devices: 62.3 us -> none
    dot_general x26 -> x0, matrix products: 42.7 us -> none  [the longest x5 8.6 us: local(): jnp.dot(padded[tap_index:tap_index + positions], pieces[:, tap_index], pr...]
    slice x25 -> x6, local copies, waits for them, and re-layouts: 36.7 us -> 0.22 us  [the longest x3 0.11 us: local(): bins[0]]
    psum x1 -> x0, waiting for transfers between devices: 27.4 us -> none  [local(): lax.psum(normed_partial.astype(jnp.bfloat16), 'tensor').astype(jnp.float32)]
    all_to_all x1 -> x0, blocking collectives: 21.2 us -> none  [local(): lax.all_to_all(activity, 'seq', split_axis=1, concat_axis=0, tiled=True)]
  transfers between devices with their start and end apart: 17 -> 0, of which waited for: 14 -> 0; matrix products, arithmetic and copies ran while one was open for 14% -> 0% of each run, Pallas kernels for 0% -> 0%
where the time goes in v3:
time: 152 us
  Pallas kernels  130 us (86%)
  local copies, waits for them, and re-layouts  17.8 us (12%)
  other arithmetic  3.52 us (2%)
    pallas_call x1, Pallas kernels, main_call(): pl.pallas_call(main_kernel, name='main', out_shape=(shape(128, 768), shap...  107 us
    pallas_call x1, Pallas kernels, communicate(): pl.pallas_call(kernel, name=name, out_shape=outputs, in_specs=[inside if...  22.7 us
    reshape x2, local copies, waits for them, and re-layouts, local(): cg.reshape(5, 2, 2, 4, 20, 384).transpose(1, 2, 3, 0, 4, 5)  3.39 us

profile of v3, /device:TPU:1, one launch (start us, length us, event | category | flops | bytes accessed | tf_op | source)
XLA Modules:
  0.0 152.0 jit_solution(4172851160195565468)
XLA Ops:
  0.6 1.0 stack_reshape.3
  1.6 1.1 reshape.57
  2.8 0.2 slice_bitcast_fusion.2
  3.0 0.8 pad_maximum_fusion
  3.8 0.5 copy.58
  4.3 0.5 reshape.58
  4.8 0.7 copy.59
  5.5 0.4 fusion.15
  6.0 0.1 slice.33
  6.1 0.1 slice.35
  6.2 0.1 reshape.56
  6.3 0.7 pad.4.edge_ref
  7.0 2.0 %reshape.68 = f32[128,2,2,4,160]{4,3,2,1,0:T(4,128)S(1)} reshape(bf16[1,256,1280]{2,1,0:T(8,128)(2,1)S(1)} %copy-done) | data formatting | bytes 1966080 | tf_op jit(solution)/shard_map/convert_element_type | solution.py:606
  9.0 0.9 copy.52
  9.9 0.4 fusion.16
  10.3 0.9 copy.53
  11.2 107.2 %main.1 = (bf16[128,768]{1,0:T(8,128)(2,1)}, bf16[8,24,768]{2,1,0:T(8,128)(2,1)}, bf16[1600,384]{1,0:T(8,128)(2,1)}) custom-call(bf16[4,2,320,128]{3,2,1,0:T(8,128)(2,1)} %bitcast.35, bf16[2,4,16,384]{3,2,1,0:T(8,128)(2,1)} %pad.4.edge_ref, bf16[5,80,768]{2,1,0:T(8,128)(2,1)} %bitcast.40, bf16[2,4,48,384]{3,2,1,0:T(8,128)(2,1)} %bitcast.37, ...), custom_call_target="tpu_custom_call" | custom-call | tf_op jit(solution)/shard_map/main/pallas_call | solution.py:588
  118.5 2.2 %reshape.61 = bf16[5,2,2,4,20,384]{5,4,3,2,1,0:T(8,128)(2,1)S(1)} reshape(bf16[1600,384]{1,0:T(8,128)(2,1)} %get-tuple-element.11) | data formatting | bytes 2457600 | tf_op jit(solution)/shard_map/reshape | solution.py:616
  120.7 0.5 copy.60
  121.2 1.2 copy.61.cg_ref
  122.4 22.7 %last.1 = (bf16[2,4,24,768]{3,2,1,0:T(8,128)(2,1)}, bf16[16,100,384]{2,1,0:T(8,128)(2,1)}) custom-call(bf16[4,2,24,768]{3,2,1,0:T(8,128)(2,1)} %bitcast.41, bf16[2,2,4,100,384]{4,3,2,1,0:T(8,128)(2,1)} %copy.61.cg_ref), custom_call_target="tpu_custom_call" | custom-call | tf_op jit(solution)/shard_map/last/pallas_call | solution.py:85
  145.1 1.0 convert_reduce_fusion
  146.1 0.2 reshape.66
  146.3 0.2 copy.63
  146.4 0.2 reshape.67
  146.6 0.6 slice_bitcast_fusion.3
  147.2 0.7 pad_maximum_fusion.1
  147.9 2.1 %reshape.72 = f32[2,2,4,5,20,384]{5,4,3,2,1,0:T(8,128)S(1)} reshape(bf16[16,100,384]{2,1,0:T(8,128)(2,1)} %get-tuple-element.12) | data formatting | bytes 3686400 | tf_op jit(solution)/shard_map/reshape | solution.py:621
  150.0 0.2 reduce_sum.18
  150.2 0.2 copy.68
  150.4 1.0 reshape.65
  151.4 0.7 copy.70
  (9 shorter events, 0.1 us)
Async XLA Ops:
  3.0 2.5 %copy-start = (bf16[1,256,1280]{2,1,0:T(8,128)(2,1)S(1)}, bf16[1,256,1280]{2,1,0:T(8,128)(2,1)}, u32[]{:S(2)}) copy-start(bf16[1,256,1280]{2,1,0:T(8,128)(2,1)} %param.5) | copy-start | bytes 1966084
  150.2 1.2 copy-start.1

commit v4 on v3

--- a/solution.py
+++ b/solution.py
@@ -79,28 +79,6 @@
             action()
 
 
-def communicate(kernel, name, collective, outputs, remotes, locals_, *operands, aliases=None, vmem=(), scratch=()):
-    anywhere = pl.BlockSpec(memory_space=pl.ANY)
-    inside = pl.BlockSpec(memory_space=pltpu.VMEM)
-    return pl.pallas_call(
-        kernel,
-        name=name,
-        out_shape=outputs,
-        in_specs=[inside if n in vmem else anywhere for n in range(len(operands))],
-        out_specs=tuple([anywhere] * len(outputs)),
-        scratch_shapes=list(scratch)
-        + [
-            pltpu.SemaphoreType.DMA((remotes,)),
-            pltpu.SemaphoreType.DMA((remotes,)),
-            pltpu.SemaphoreType.DMA((locals_,)),
-        ],
-        input_output_aliases=aliases or {},
-        compiler_params=pltpu.CompilerParams(
-            collective_id=collective, has_side_effects=True, vmem_limit_bytes=16 * 1024 * 1024 if vmem else None
-        ),
-    )(*operands)
-
-
 class Moves:
     def __init__(self, place, send, recv, local):
         self.place, self.send, self.recv, self.local = place, send, recv, local
@@ -148,49 +126,6 @@
     return [(None, p.at(d=p.along_y(k))) for k in range(1, 4)]
 
 
-def last_kernel(hg_ref, cg_ref, hgs_ref, cgs_ref, send, recv, local):
-    p = Place()
-    peers = []
-    for zh in range(2):
-        for c in range(2):
-            for k in range(4):
-                here = k == 0
-                target = p.at(zh=zh, c=c, d=p.along_y(k))
-                peers.append((jnp.logical_or(zh != p.zh, c != p.c) if here else None, target))
-    for zh in range(2):
-        for k in range(1, 4):
-            peers.append((None, p.at(zh=zh, x=p.along_x(k), c=p.zh)))
-    barrier = greet(peers)
-    pl.semaphore_wait(barrier, 15 + 6)
-    moves = Moves(p, send, recv, local)
-    b = moves.slots(16)
-    me = 8 * p.zh + 4 * p.c + p.d
-    for k in (8, 12, 4, 2, 10, 14, 6, 1, 3, 9, 11, 13, 15, 5, 7, 0):
-        other = lax.rem(me + k, 16)
-        zh, c, d = lax.div(other, 8), lax.rem(lax.div(other, 4), 2), lax.rem(other, 4)
-        src = cg_ref.at[zh, c, d]
-        if k == 0:
-            moves.keep(src, cgs_ref.at[me])
-        else:
-            moves.push(src, cgs_ref.at[me], p.at(zh=zh, c=c, d=d), b + k)
-            moves.expect(cgs_ref.at[lax.rem(me + 16 - k, 16)], b + k)
-    a = moves.slots(8)
-    for k in range(8):
-        other = lax.rem(2 * p.x + k, 8)
-        x, c = lax.div(other, 2), lax.rem(other, 2)
-        src, dst = hg_ref.at[x, c], hgs_ref.at[p.zh, p.x]
-        alone = jnp.logical_and(jnp.logical_and(x == p.x, c == p.c), p.zh == p.c)
-        if k < 2:
-            moves.push(src, dst, p.at(x=x, zh=p.c, c=c), a + k, a + 4 * p.zh + p.x, jnp.logical_not(alone))
-            moves.keep(src, dst, alone)
-        else:
-            moves.push(src, dst, p.at(x=x, zh=p.c, c=c), a + k, a + 4 * p.zh + p.x)
-    for zh in range(2):
-        for x in range(4):
-            alone = jnp.logical_and(jnp.logical_and(x == p.x, zh == p.zh), p.zh == p.c)
-            moves.expect(hgs_ref.at[zh, x], a + 4 * zh + x, jnp.logical_not(alone))
-    moves.settle()
-
 def dot(a, b, dims):
     return lax.dot_general(a, b, (dims, ((), ())), preferred_element_type=F32)
 
@@ -202,18 +137,21 @@
 
 def main_kernel(
     at_ref, edge_ref, cw_ref, wp_ref, cot_ref,
-    out_ref, hgo_ref, cg_ref,
+    out_ref, conv_ref, head_ref, output_ref,
     xt_ref, low_ref, high_ref, cwf_ref, wf_ref, cots_ref, x5_ref, x5s_ref, part_ref, rs_ref, sec_ref, secs_ref,
     inv_ref, nb_ref, nl_ref, cl_ref, kv_ref, st_ref, dp_ref, p16_ref, ds_ref, dkv_ref, buf_ref, sum_ref, dkvs_ref,
     bo_ref, bos_ref, gpa_ref, gpas_ref, norm_ref, norms_ref, spread_ref, spreads_ref, hg_ref, hgs_ref, gp_ref, gps_ref,
-    send, recv, local,
+    hgo_ref, hgl_ref, cgf_ref, cgm_ref, cg_ref, cgs_ref, send, recv, local,
 ):
     p = Place()
     scale = HEAD_DIM ** (-0.5)
     peers = [(None, {"seq": lax.rem(p.s + k, 16), "tensor": p.t, "dp": p.d}) for k in range(1, 16)]
-    peers += [(None, p.at(t=1 - p.t)), (None, p.at(zh=1 - p.zh, t=1 - p.t))] + y_ring(p)
+    peers += [(None, p.at(t=1 - p.t)), (None, p.at(zh=1 - p.zh, t=1 - p.t))]
+    for zh in range(2):
+        for c in range(2):
+            peers += [(None, p.at(zh=zh, c=c, d=p.along_y(k))) for k in range(1, 4)]
     barrier = greet(peers)
-    pl.semaphore_wait(barrier, 20)
+    pl.semaphore_wait(barrier, 29)
     moves = Moves(p, send, recv, local)
     arrival = moves.arrival
 
@@ -289,14 +227,6 @@
             other = lax.rem(shard + 8 - k, 8)
             quarter_arrivals.append(arrival(quarter(lax.div(other, 4), lax.rem(other, 4), p.c, p.d), w + k))
 
-    cot_first = moves.slots(4)
-    cot_own = pltpu.make_async_copy(cot_ref, cots_ref.at[p.z], local.at[moves.used_local])
-    moves.used_local += 1
-    cot_own.start()
-    cot_arrivals = [cot_own.wait]
-    for k in (2, 1, 3):
-        moves.push(cot_ref, cots_ref.at[p.z], p.at_z(p.along_z(k)), cot_first + k)
-        cot_arrivals.append(arrival(cots_ref.at[p.along_z(4 - k)], cot_first + k))
 
     arrival(from_z, first)()
     moves.push(from_z, from_z, p.sibling, first + 2)
@@ -362,12 +292,6 @@
         d = p.along_y(4 - k)
         arrival(quarters(p.c, d), y + k)()
         moves.push(quarters(p.c, d), quarters(p.c, d), p.sibling, y + 3 + k)
-    for wait in cot_arrivals:
-        wait()
-    o = moves.slots(4)
-    for zh in range(2):
-        cl_ref[zh] = cots_ref[2 * zh + p.c]
-        moves.push(cots_ref.at[2 * zh + 1 - p.c], cl_ref.at[2 + zh], p.sibling, o + zh)
     arrival(quarters(1 - p.c, p.d), y)()
     for k in (1, 3, 2):
         arrival(quarters(1 - p.c, p.along_y(4 - k)), y + 3 + k)()
@@ -382,11 +306,18 @@
         return jnp.concatenate([ref[t], ref[2 + t]], axis=0)
 
     wide_lane = lax.broadcasted_iota(jnp.int32, (256, 256), 1)
-    grad_att = dot(channels(cots_ref, 0), output_rows(0), NN) + dot(channels(cots_ref, 1), output_rows(1), NN)
-    grad_att = jnp.where(wide_lane < 64, 0.0, grad_att).astype(BF16)
 
     for k in (2, 1, 3):
         arrival(secs_ref.at[p.along_z(4 - k)], g + k)()
+    cot_first = moves.slots(4)
+    cot_own = pltpu.make_async_copy(cot_ref, cots_ref.at[p.z], local.at[moves.used_local])
+    moves.used_local += 1
+    cot_own.start()
+    cot_arrivals = [cot_own.wait]
+    for k in (2, 1, 3):
+        moves.push(cot_ref, cots_ref.at[p.z], p.at_z(p.along_z(k)), cot_first + k)
+        cot_arrivals.append(arrival(cots_ref.at[p.along_z(4 - k)], cot_first + k))
+    o = moves.slots(4)
     for zh in range(2):
         left, right = secs_ref[2 * zh].astype(F32), secs_ref[2 * zh + 1].astype(F32)
         squares = jnp.sum(left * left, axis=1, keepdims=True) + jnp.sum(right * right, axis=1, keepdims=True)
@@ -425,6 +356,13 @@
         st_ref[n] = unnormed
         sums = sums + jnp.sum(unnormed, axis=0, keepdims=True)
     share = 1.0 / sums
+    for wait in cot_arrivals:
+        wait()
+    for zh in range(2):
+        cl_ref[zh] = cots_ref[2 * zh + p.c]
+        moves.push(cots_ref.at[2 * zh + 1 - p.c], cl_ref.at[2 + zh], p.sibling, o + zh)
+    grad_att = dot(channels(cots_ref, 0), output_rows(0), NN) + dot(channels(cots_ref, 1), output_rows(1), NN)
+    grad_att = jnp.where(wide_lane < 64, 0.0, grad_att).astype(BF16)
     centre = jnp.zeros((1, 256), F32)
     for n in range(8):
         weights = st_ref[n] * share
@@ -494,7 +432,7 @@
         norm_ref[2 + t] = rounded[128:]
     spread = spread * (1.0 / 1536)
     for zh in range(2):
-        spread_ref[zh] = jnp.broadcast_to(spread[128 * zh : 128 * zh + 128], (128, 128))
+        spread_ref[zh] = jnp.broadcast_to(spread[128 * zh : 128 * zh + 128], (128, 128)).T[:8]
     m = moves.slots(8)
     for k in (2, 1, 3):
         z = p.along_z(k)
@@ -537,8 +475,9 @@
     for z in range(1, 4):
         grad_normed = grad_normed + norms_ref[z].astype(F32)
         mean = mean + spreads_ref[z]
+    mean = jnp.concatenate([mean] * 16, axis=0).T[:, :1]
     inverse = inv_ref[p.zh][:, :1]
-    grad_section = cots_ref[p.z].astype(F32) + inverse * grad_normed - inverse * inverse * inverse * total * mean[:, :1]
+    grad_section = cots_ref[p.z].astype(F32) + inverse * grad_normed - inverse * inverse * inverse * total * mean
     grad_pool = (0.5 * grad_section).astype(BF16)
     gp_ref[0] = grad_pool[:, :384]
     gp_ref[1] = grad_pool[:, 384:]
@@ -554,14 +493,69 @@
     rows = hgs_ref[0].astype(F32)
     for d in range(1, 4):
         rows = rows + hgs_ref[d].astype(F32)
-    hgo_ref[...] = rows.astype(BF16)
+    rows = rows.astype(BF16)
+    f = moves.slots(8)
+    for n in range(8):
+        hgo_ref[n // 2, n % 2] = rows[n]
+    alone = []
+    for k in (2, 3, 4, 5, 6, 7, 0, 1):
+        other = lax.rem(2 * p.x + k, 8)
+        x, c = lax.div(other, 2), lax.rem(other, 2)
+        src, dst = hgo_ref.at[x, c], hgl_ref.at[p.zh, p.x]
+        if k < 2:
+            alone = jnp.logical_and(jnp.logical_and(x == p.x, c == p.c), p.zh == p.c)
+            moves.push(src, dst, p.at(x=x, zh=p.c, c=c), f + k, f + 4 * p.zh + p.x, jnp.logical_not(alone))
+            moves.keep(src, dst, alone)
+        else:
+            moves.push(src, dst, p.at(x=x, zh=p.c, c=c), f + k, f + 4 * p.zh + p.x)
 
     arrival(x5s_ref, other_x5)()
     for k in (1, 7, 6, 2, 3, 4, 5):
         arrival(gps_ref.at[lax.rem(block + 8 - k, 8)], j + k)()
     here = gps_ref[pl.ds(4 * p.c, 4)].reshape(512, 384)
     there = gps_ref[pl.ds(4 - 4 * p.c, 4)].reshape(512, 384)
-    cg_ref[...] = (dot(x5_ref[...], here, NN) + dot(x5s_ref[...], there, NN)).astype(BF16)
+    cgf_ref[...] = dot(x5_ref[...], here, NN) + dot(x5s_ref[...], there, NN)
+    for n in range(16):
+        for tap in range(5):
+            cgm_ref[n % 2, pl.ds(20 * tap, 20), :] = cgf_ref[pl.ds(320 * tap + 20 * n, 20), :]
+        cg_ref[n] = cgm_ref[n % 2].astype(BF16)
+    e = moves.slots(16)
+    me = 8 * p.zh + 4 * p.c + p.d
+    for k in (10, 14, 2, 6, 8, 12, 4, 9, 11, 13, 15, 1, 3, 5, 7):
+        other = lax.rem(me + k, 16)
+        zh, c, d = lax.div(other, 8), lax.rem(lax.div(other, 4), 2), lax.rem(other, 4)
+        moves.push(cg_ref.at[other], cgs_ref.at[me], p.at(zh=zh, c=c, d=d), e + k)
+    cgs_ref[me] = cg_ref[me]
+    for zh in range(2):
+        for x in range(4):
+            alone = jnp.logical_and(jnp.logical_and(x == p.x, zh == p.zh), p.zh == p.c)
+            arrival(hgl_ref.at[zh, x], f + 4 * zh + x, jnp.logical_not(alone))()
+    for when, wait in moves.locals:
+        under(when, wait)
+    moves.locals = []
+    heads = []
+    for zh in range(2):
+        rows = hgl_ref[zh, 0].astype(F32)
+        for x in range(1, 4):
+            rows = rows + hgl_ref[zh, x].astype(F32)
+        heads.append(rows)
+    for n, first in enumerate((384, 0, 192, 576)):
+        piece = jnp.concatenate([rows[:, first : first + 192] for rows in heads], axis=1)
+        if n < 3:
+            head_ref[:, n, :] = piece
+        else:
+            output_ref[...] = piece
+    for k in (1, 2, 3, 4, 5, 6, 7, 8, 9, 10, 11, 12, 13, 14, 15):
+        arrival(cgs_ref.at[lax.rem(me + 16 - k, 16)], e + k)()
+    for c in range(2):
+        total = None
+        for zh in range(2):
+            for d in range(4):
+                part = cgs_ref[8 * zh + 4 * c + d].astype(F32)
+                total = part if total is None else total + part
+        cgm_ref[c] = total
+        for tap in range(5):
+            conv_ref[:, tap, 384 * c : 384 * c + 384] = cgm_ref[c, pl.ds(20 * tap, 20), :]
     moves.settle()
 
 
@@ -581,16 +575,23 @@
         vmem(8, 256, 256), vmem(8, 256, 256), vmem(4, 256, 384), vmem(4, 256, 384), vmem(4, 256, 384),
         vmem(4, 256, 384),
         vmem(4, 128, 768), vmem(4, 128, 768), vmem(256, 768), vmem(256, 768), vmem(4, 128, 768), vmem(4, 128, 768),
-        vmem(2, 128, 128, dtype=F32), vmem(4, 128, 128, dtype=F32),
+        vmem(2, 8, 128, dtype=F32), vmem(4, 8, 128, dtype=F32),
         vmem(4, 8, 24, 768), vmem(4, 8, 24, 768), vmem(2, 128, 384), vmem(8, 128, 384),
-        pltpu.SemaphoreType.DMA((112,)), pltpu.SemaphoreType.DMA((112,)), pltpu.SemaphoreType.DMA((12,)),
+        vmem(4, 2, 24, 768), vmem(2, 4, 24, 768), vmem(1600, 384, dtype=F32), vmem(2, 104, 384, dtype=F32),
+        vmem(16, 104, 384), vmem(16, 104, 384),
+        pltpu.SemaphoreType.DMA((136,)), pltpu.SemaphoreType.DMA((136,)), pltpu.SemaphoreType.DMA((16,)),
     ]
     return pl.pallas_call(
         main_kernel,
         name="main",
-        out_shape=(shape(128, 768), shape(8, 24, 768), shape(1600, 384)),
+        out_shape=(
+            shape(128, 768),
+            jax.ShapeDtypeStruct((20, 5, 768), F32),
+            jax.ShapeDtypeStruct((24, 3, 384), F32),
+            jax.ShapeDtypeStruct((24, 384), F32),
+        ),
         in_specs=[anywhere] * 5,
-        out_specs=(inside,) * 3,
+        out_specs=(inside,) * 4,
         scratch_shapes=scratch,
         compiler_params=pltpu.CompilerParams(
             collective_id=1, has_side_effects=True, vmem_limit_bytes=60 * 1024 * 1024
@@ -612,18 +613,8 @@
     heads = head_weight.reshape(96, 3, 2, 192)
     wp = jnp.stack([heads[:, 1], heads[:, 2], heads[:, 0], output_weight.reshape(96, 2, 192)], axis=2)
     wp = wp.reshape(2, 48, 2, 2, 384).transpose(2, 0, 3, 1, 4).reshape(2, 4, 48, 384)
-    block_out, hg_sum, cg = main_call(at, edges, cw, wp, cotangent[0])
-    cg = cg.reshape(5, 2, 2, 4, 20, 384).transpose(1, 2, 3, 0, 4, 5).reshape(2, 2, 4, 100, 384)
-    hgl, cgl = communicate(
-        last_kernel, "last", 8, (shape(2, 4, 24, 768), shape(16, 100, 384)), 24, 4,
-        hg_sum.reshape(4, 2, 24, 768), cg,
-    )
-    conv_grad = jnp.sum(cgl.astype(F32).reshape(2, 2, 4, 5, 20, 384), axis=(0, 2))
-    conv_grad = conv_grad.transpose(2, 1, 0, 3).reshape(20, 5, 768)
-    both = jnp.sum(hgl.astype(F32), axis=1).reshape(2, 24, 4, 192)
-    both = both.transpose(1, 2, 0, 3).reshape(24, 4, 384)
-    head_grad = jnp.stack([both[:, 2], both[:, 0], both[:, 1]], axis=1)
-    return (block_out[None], conv_grad, head_grad, both[:, 3])
+    block_out, conv_grad, head_grad, output_grad = main_call(at, edges, cw, wp, cotangent[0])
+    return (block_out[None], conv_grad, head_grad, output_grad)
 
 
 def solution(mesh):

time: 152 us -> 140 us (0.921)
  Pallas kernels: 130 us -> 123 us
  local copies, waits for them, and re-layouts: 17.8 us -> 13.7 us
  other arithmetic: 3.52 us -> 1.67 us
    reshape x6 -> x0, local copies, waits for them, and re-layouts: 6.83 us -> none  [the longest x2 3.39 us: local(): cg.reshape(5, 2, 2, 4, 20, 384).transpose(1, 2, 3, 0, 4, 5)]
    pallas_call x2 -> x1, Pallas kernels: 130 us -> 123 us  [main_call(): pl.pallas_call(main_kernel, name='main', out_shape=(shape(128, 768), jax....]
    unnamed x6 -> x12, local copies, waits for them, and re-layouts: 0.85 us -> 5.69 us
where the time goes in v4:
time: 140 us
  Pallas kernels  123 us (88%)
  local copies, waits for them, and re-layouts  13.7 us (10%)
  other arithmetic  1.67 us (1%)
    pallas_call x1, Pallas kernels, main_call(): pl.pallas_call(main_kernel, name='main', out_shape=(shape(128, 768), jax....  123 us
    unnamed x12, local copies, waits for them, and re-layouts  5.69 us
    convert_element_type x2, local copies, waits for them, and re-layouts, local(): section_input[0].astype(F32)  3.96 us

profile of v4, /device:TPU:1, one launch (start us, length us, event | category | flops | bytes accessed | tf_op | source)
XLA Modules:
  0.0 139.6 jit_solution(11454534995816273202)
XLA Ops:
  0.6 3.1 %reshape.36 = f32[128,2,2,4,160]{4,3,2,1,0:T(4,128)S(1)} reshape(bf16[1,256,1280]{2,1,0:T(8,128)(2,1)} %param.5) | data formatting | bytes 1966080 | tf_op jit(solution)/shard_map/convert_element_type | solution.py:607
  3.7 0.9 copy.48
  4.6 0.0 copy-start
  4.6 0.4 fusion.16
  5.1 0.0 copy-start.2
  5.1 0.0 copy-start.1
  5.1 0.9 copy.49
  6.0 0.0 copy-done
  6.0 0.4 fusion.15
  6.4 0.1 slice.24
  6.6 0.1 slice.22
  6.7 0.1 reshape.32
  6.8 0.7 pad.4.edge_ref
  7.4 0.0 copy-done.2
  7.5 0.1 stack_reshape.3
  7.6 0.0 copy-done.1
  7.6 0.2 reshape.33
  7.8 0.2 slice_bitcast_fusion.2
  8.0 0.8 pad_maximum_fusion
  8.7 0.5 copy.54
  9.3 0.5 reshape.34
  9.7 0.7 copy.55
  10.5 123.5 %main.1 = (bf16[128,768]{1,0:T(8,128)(2,1)}, f32[20,5,768]{2,1,0:T(8,128)}, f32[24,3,384]{2,1,0:T(4,128)}, f32[24,384]{1,0:T(8,128)}) custom-call(bf16[4,2,320,128]{3,2,1,0:T(8,128)(2,1)} %bitcast.20, bf16[2,4,16,384]{3,2,1,0:T(8,128)(2,1)} %pad.4.edge_ref, bf16[5,80,768]{2,1,0:T(8,128)(2,1)} %bitcast.23, bf16[2,4,48,384]{3,2,1,0:T(8,128)(2,1)} %bitcast.21, ...), custom_call_target="tpu_custom_call" | custom-call | tf_op jit(solution)/shard_map/main/pallas_call | solution.py:584
  134.0 0.0 copy-start.3
  134.0 1.9 %copy.56 = f32[20,5,768]{2,0,1:T(8,128)} copy(f32[20,5,768]{2,1,0:T(8,128)} %get-tuple-element.29) | data formatting | bytes 614400
  135.8 1.6 %copy.57 = f32[24,3,384]{2,0,1:T(8,128)} copy(f32[24,3,384]{2,1,0:T(4,128)} %get-tuple-element.30) | data formatting | bytes 221184
  137.4 1.6 %copy.61 = bf16[1,128,768]{2,1,0:T(8,128)(2,1)} copy(bf16[1,128,768]{2,1,0:T(8,128)(2,1)} %bitcast.25) | data formatting | bytes 393216
  139.0 0.0 copy-done.3
  139.0 0.6 copy.62
  (4 shorter events, 0.1 us)
Async XLA Ops:
  4.6 1.4 copy-start
  5.1 2.4 %copy-start.2 = (bf16[96,384]{1,0:T(8,128)(2,1)S(1)}, bf16[96,384]{1,0:T(8,128)(2,1)}, u32[]{:S(2)}) copy-start(bf16[96,384]{1,0:T(8,128)(2,1)} %param.8) | copy-start | bytes 221188
  5.1 2.5 %copy-start.1 = (bf16[96,3,384]{2,0,1:T(8,128)(2,1)S(1)}, bf16[96,3,384]{2,0,1:T(8,128)(2,1)}, u32[]{:S(2)}) copy-start(bf16[96,3,384]{2,0,1:T(8,128)(2,1)} %param.7) | copy-start | bytes 663556
  134.0 5.1 %copy-start.3 = (f32[24,384]{1,0:T(8,128)S(1)}, f32[24,384]{1,0:T(8,128)}, u32[]{:S(2)}) copy-start(f32[24,384]{1,0:T(8,128)} %get-tuple-element.44) | copy-start | bytes 110596

commit v5 on v4

--- a/solution.py
+++ b/solution.py
@@ -136,9 +136,9 @@
 
 
 def main_kernel(
-    at_ref, edge_ref, cw_ref, wp_ref, cot_ref,
+    input_ref, cw_ref, hw_ref, ow_ref, cot_ref,
     out_ref, conv_ref, head_ref, output_ref,
-    xt_ref, low_ref, high_ref, cwf_ref, wf_ref, cots_ref, x5_ref, x5s_ref, part_ref, rs_ref, sec_ref, secs_ref,
+    act_ref, at_ref, edge_ref, wp_ref, end_ref, xt_ref, low_ref, high_ref, cwf_ref, wf_ref, cots_ref, x5_ref, x5s_ref, part_ref, rs_ref, sec_ref, secs_ref,
     inv_ref, nb_ref, nl_ref, cl_ref, kv_ref, st_ref, dp_ref, p16_ref, ds_ref, dkv_ref, buf_ref, sum_ref, dkvs_ref,
     bo_ref, bos_ref, gpa_ref, gpas_ref, norm_ref, norms_ref, spread_ref, spreads_ref, hg_ref, hgs_ref, gp_ref, gps_ref,
     hgo_ref, hgl_ref, cgf_ref, cgm_ref, cg_ref, cgs_ref, send, recv, local,
@@ -155,49 +155,25 @@
     moves = Moves(p, send, recv, local)
     arrival = moves.arrival
 
-    first = moves.slots(4)
+    first = moves.slots(12)
+
+    def fifth(zh, c, n):
+        return cwf_ref.at[:, 2 * zh + c, pl.ds(pl.multiple_of(16 * n, 16), 16), :]
+
+    other_half = 1 - p.zh
+    moves.push(cw_ref.at[:, pl.ds(pl.multiple_of(16 * p.d, 16), 16), :], fifth(p.zh, p.c, p.d), p.at(zh=other_half), first)
+    moves.push(cw_ref.at[:, pl.ds(64, 16), :], fifth(p.zh, p.c, 4), p.at(zh=other_half), first + 1)
     mine = cwf_ref.at[:, 2 * p.zh + p.c]
-    moves.push(cw_ref, mine, p.at(zh=1 - p.zh), first)
-    moves.push(cw_ref, mine, p.sibling, first + 1)
+    moves.push(cw_ref, mine, p.sibling, first + 2)
     moves.keep(cw_ref, mine)
-    from_z = cwf_ref.at[:, 2 * (1 - p.zh) + p.c]
-
-    a = moves.slots(4)
-    core = lax.div(p.x, 2)
-    slot = 2 * lax.rem(p.x, 2) + p.c
-    spot = xt_ref.at[slot]
-    for k in (2, 1, 3, 0):
-        x = p.along_x(k)
-        if k == 0:
-            moves.push(at_ref.at[x], spot, p.at(c=core), a, a + slot, core != p.c)
-            moves.keep(at_ref.at[x], spot, core == p.c)
-        else:
-            moves.push(at_ref.at[x], spot, p.at(x=x, c=core), a + k, a + slot)
-    base = 8 * p.zh + 4 * p.c
-    halo = []
-    for up, end_ref in ((True, low_ref), (False, high_ref)):
-        e = moves.slots(4)
-        if up:
-            sends = jnp.logical_and(lax.rem(p.s, 4) == 3, p.s != 15)
-            block = lax.rem(p.s + 1, 16)
-        else:
-            sends = jnp.logical_and(lax.rem(p.s, 4) == 0, p.s != 0)
-            block = lax.rem(p.s + 15, 16)
-        zh, c = lax.div(block, 8), lax.div(lax.rem(block, 8), 4)
-        for k in range(4):
-            x = p.along_x(k)
-            src = edge_ref.at[1 if up else 0, x]
-            target = p.at(x=x, zh=zh, c=c)
-            if k == 0:
-                alone = jnp.logical_and(zh == p.zh, c == p.c)
-                moves.push(src, end_ref, target, e, e, jnp.logical_and(sends, jnp.logical_not(alone)))
-                moves.keep(src, end_ref, jnp.logical_and(sends, alone))
-            else:
-                moves.push(src, end_ref, target, e + k, e, sends)
-        if up:
-            halo.append(arrival(end_ref, e, jnp.logical_and(base != 0, base - 1 != p.s)))
-        else:
-            halo.append(arrival(end_ref, e, jnp.logical_and(base != 12, base + 4 != p.s)))
+
+    for head in range(2):
+        lanes = slice(192 * head, 192 * head + 192)
+        keys, values, queries = (hw_ref[n, :, lanes].astype(F32) for n in (1, 2, 0))
+        pairs = (jnp.concatenate([keys, values], axis=1), jnp.concatenate([queries, ow_ref[:, lanes].astype(F32)], axis=1))
+        for column in range(2):
+            for row in range(2):
+                wp_ref[head, 2 * row + column] = pairs[column][48 * row : 48 * row + 48].astype(BF16)
 
     def quarter(zh, x, c, d):
         rows = pl.ds(pl.multiple_of(48 * lax.div(d, 2), 16), 48)
@@ -227,9 +203,70 @@
             other = lax.rem(shard + 8 - k, 8)
             quarter_arrivals.append(arrival(quarter(lax.div(other, 4), lax.rem(other, 4), p.c, p.d), w + k))
 
-
-    arrival(from_z, first)()
-    moves.push(from_z, from_z, p.sibling, first + 2)
+    for n in range(10):
+        lanes = slice(128 * n, 128 * n + 128)
+        rows = jax.nn.gelu(input_ref[:, lanes].astype(F32), approximate=True).astype(BF16)
+        edge_ref[0, :, lanes] = rows[:16]
+        edge_ref[1, :, lanes] = rows[240:]
+        act_ref[n] = rows.astype(F32)
+        for parity in range(2):
+            turned = act_ref[n, pl.ds(parity, 128, stride=2), :].T.astype(BF16)
+            begin = 128 * n
+            while begin < 128 * n + 128:
+                end = min(128 * n + 128, (begin // 160 + 1) * 160)
+                zh, x = divmod(begin // 160, 4)
+                spot = 160 * zh + begin % 160
+                at_ref[x, parity, spot : spot + end - begin] = turned[begin - 128 * n : end - 128 * n]
+                begin = end
+    a = moves.slots(4)
+    core = lax.div(p.x, 2)
+    slot = 2 * lax.rem(p.x, 2) + p.c
+    spot = xt_ref.at[slot]
+    for k in (2, 1, 3, 0):
+        x = p.along_x(k)
+        if k == 0:
+            moves.push(at_ref.at[x], spot, p.at(c=core), a, a + slot, core != p.c)
+            moves.keep(at_ref.at[x], spot, core == p.c)
+        else:
+            moves.push(at_ref.at[x], spot, p.at(x=x, c=core), a + k, a + slot)
+    base = 8 * p.zh + 4 * p.c
+    halo = []
+    for up, bound_ref in ((True, low_ref), (False, high_ref)):
+        e = moves.slots(4)
+        if up:
+            sends = jnp.logical_and(lax.rem(p.s, 4) == 3, p.s != 15)
+            block = lax.rem(p.s + 1, 16)
+        else:
+            sends = jnp.logical_and(lax.rem(p.s, 4) == 0, p.s != 0)
+            block = lax.rem(p.s + 15, 16)
+        zh, c = lax.div(block, 8), lax.div(lax.rem(block, 8), 4)
+        for k in range(4):
+            x = p.along_x(k)
+            src = edge_ref.at[1 if up else 0]
+            target = p.at(x=x, zh=zh, c=c)
+            if k == 0:
+                alone = jnp.logical_and(zh == p.zh, c == p.c)
+                moves.push(src, bound_ref, target, e, e, jnp.logical_and(sends, jnp.logical_not(alone)))
+                moves.keep(src, bound_ref, jnp.logical_and(sends, alone))
+            else:
+                moves.push(src, bound_ref, target, e + k, e, sends)
+        if up:
+            halo.append(arrival(bound_ref, e, jnp.logical_and(base != 0, base - 1 != p.s)))
+        else:
+            halo.append(arrival(bound_ref, e, jnp.logical_and(base != 12, base + 4 != p.s)))
+
+    moves.arrival(fifth(other_half, p.c, p.d), first)()
+    got = fifth(other_half, p.c, p.d)
+    for k in (2, 1, 3):
+        moves.push(got, got, p.at(d=p.along_y(k)), first + 3 + k)
+    moves.push(got, got, p.sibling, first + 3)
+    got = fifth(other_half, p.c, 4)
+    moves.arrival(got, first + 1)()
+    moves.push(got, got, p.sibling, first + 7)
+    for k in (1, 3, 2):
+        got = fifth(other_half, p.c, p.along_y(4 - k))
+        moves.arrival(got, first + 3 + k)()
+        moves.push(got, got, p.sibling, first + 7 + k)
     for wait in quarter_arrivals:
         wait()
     y = moves.slots(8)
@@ -245,10 +282,16 @@
     for when, wait in moves.locals:
         under(when, wait)
     moves.locals = []
-    pick = (lax.broadcasted_iota(jnp.int32, (16, 128), 0) == lax.broadcasted_iota(jnp.int32, (16, 128), 1)).astype(BF16)
-    zero_rows = jnp.zeros((16, 384), BF16)
-    low = dot(jnp.where(base != 0, low_ref[...], zero_rows), pick, TN)[:320]
-    high = dot(jnp.where(base != 12, high_ref[...], zero_rows), pick, TN)[:320]
+    row = lax.broadcasted_iota(jnp.int32, (16, 128), 0)
+    column = lax.broadcasted_iota(jnp.int32, (16, 128), 1)
+    zero_rows = jnp.zeros((16, 1280), BF16)
+    ends = []
+    for there, bound_ref, shift in ((base != 0, low_ref, 14), (base != 12, high_ref, 0)):
+        pick = (row == column + shift).astype(BF16)
+        end_ref[...] = dot(jnp.where(there, bound_ref[...], zero_rows), pick, TN)
+        lower = pl.multiple_of(160 * p.x, 32)
+        ends.append(jnp.concatenate([end_ref[pl.ds(lower, 160)], end_ref[pl.ds(640 + lower, 160)]], axis=0))
+    low, high = ends
     even = jnp.concatenate([xt_ref[n, 0] for n in range(4)], axis=1).astype(F32)
     odd = jnp.concatenate([xt_ref[n, 1] for n in range(4)], axis=1).astype(F32)
     lane = lax.broadcasted_iota(jnp.int32, (320, 512), 1)
@@ -260,8 +303,11 @@
     ).astype(BF16)
     x5_ref[pl.ds(320, 320), :] = (even + jnp.where(lane == 0, low[:, 1:2], pltpu.roll(odd, 1, 1))).astype(BF16)
     x5_ref[pl.ds(960, 320), :] = (odd + jnp.where(lane == 511, high[:, 0:1], pltpu.roll(even, 511, 1))).astype(BF16)
-    arrival(cwf_ref.at[:, 2 * p.zh + 1 - p.c], first + 1)()
-    arrival(cwf_ref.at[:, 2 * (1 - p.zh) + 1 - p.c], first + 2)()
+    arrival(cwf_ref.at[:, 2 * p.zh + 1 - p.c], first + 2)()
+    arrival(fifth(other_half, 1 - p.c, p.d), first + 3)()
+    arrival(fifth(other_half, 1 - p.c, 4), first + 7)()
+    for k in (1, 3, 2):
+        arrival(fifth(other_half, 1 - p.c, p.along_y(4 - k)), first + 7 + k)()
     b = moves.slots(4)
     for half in range(2):
         conv = dot(x5_ref[:, 256 * half : 256 * half + 256], cwf_ref[...].reshape(1600, 768), TN) * 0.5
@@ -542,7 +588,7 @@
     for n, first in enumerate((384, 0, 192, 576)):
         piece = jnp.concatenate([rows[:, first : first + 192] for rows in heads], axis=1)
         if n < 3:
-            head_ref[:, n, :] = piece
+            head_ref[n] = piece
         else:
             output_ref[...] = piece
     for k in (1, 2, 3, 4, 5, 6, 7, 8, 9, 10, 11, 12, 13, 14, 15):
@@ -555,11 +601,11 @@
                 total = part if total is None else total + part
         cgm_ref[c] = total
         for tap in range(5):
-            conv_ref[:, tap, 384 * c : 384 * c + 384] = cgm_ref[c, pl.ds(20 * tap, 20), :]
+            conv_ref[tap, :, 384 * c : 384 * c + 384] = cgm_ref[c, pl.ds(20 * tap, 20), :]
     moves.settle()
 
 
-def main_call(at, edges, cw, wp, cot):
+def main_call(section_input, cw, hw, ow, cot):
     anywhere = pl.BlockSpec(memory_space=pl.ANY)
     inside = pl.BlockSpec(memory_space=pltpu.VMEM)
 
@@ -567,7 +613,8 @@
         return pltpu.VMEM(dims, dtype)
 
     scratch = [
-        vmem(4, 2, 320, 128), vmem(16, 384), vmem(16, 384), vmem(5, 4, 80, 768), vmem(2, 4, 2, 96, 768),
+        vmem(10, 256, 128, dtype=F32), vmem(4, 2, 320, 128), vmem(2, 16, 1280), vmem(2, 4, 48, 384),
+        vmem(1280, 128, dtype=F32), vmem(4, 2, 320, 128), vmem(16, 1280), vmem(16, 1280), vmem(5, 4, 80, 768), vmem(2, 4, 2, 96, 768),
         vmem(4, 128, 768), vmem(1600, 512), vmem(1600, 512), vmem(4, 128, 768), vmem(4, 128, 768),
         vmem(128, 768), vmem(4, 128, 768),
         vmem(2, 128, 128, dtype=F32), vmem(4, 128, 768), vmem(4, 128, 768), vmem(4, 128, 768),
@@ -579,42 +626,53 @@
         vmem(4, 8, 24, 768), vmem(4, 8, 24, 768), vmem(2, 128, 384), vmem(8, 128, 384),
         vmem(4, 2, 24, 768), vmem(2, 4, 24, 768), vmem(1600, 384, dtype=F32), vmem(2, 104, 384, dtype=F32),
         vmem(16, 104, 384), vmem(16, 104, 384),
-        pltpu.SemaphoreType.DMA((136,)), pltpu.SemaphoreType.DMA((136,)), pltpu.SemaphoreType.DMA((16,)),
+        pltpu.SemaphoreType.DMA((144,)), pltpu.SemaphoreType.DMA((144,)), pltpu.SemaphoreType.DMA((16,)),
     ]
     return pl.pallas_call(
         main_kernel,
         name="main",
         out_shape=(
             shape(128, 768),
-            jax.ShapeDtypeStruct((20, 5, 768), F32),
-            jax.ShapeDtypeStruct((24, 3, 384), F32),
+            jax.ShapeDtypeStruct((5, 20, 768), F32),
+            jax.ShapeDtypeStruct((3, 24, 384), F32),
             jax.ShapeDtypeStruct((24, 384), F32),
         ),
-        in_specs=[anywhere] * 5,
+        in_specs=[inside, anywhere, inside, inside, anywhere],
         out_specs=(inside,) * 4,
         scratch_shapes=scratch,
         compiler_params=pltpu.CompilerParams(
             collective_id=1, has_side_effects=True, vmem_limit_bytes=60 * 1024 * 1024
         ),
-    )(at, edges, cw, wp, cot)
+    )(section_input, cw, hw, ow, cot)
 
 
 def shape(*dims):
     return jax.ShapeDtypeStruct(dims, BF16)
 
 
+def finish_kernel(*refs):
+    for source, target in zip(refs[:4], refs[4:]):
+        target[...] = source[...]
+
+
+def finish(*arrays):
+    inside = pl.BlockSpec(memory_space=pltpu.VMEM)
+    return pl.pallas_call(
+        finish_kernel,
+        name="finish",
+        out_shape=tuple(jax.ShapeDtypeStruct(array.shape, array.dtype) for array in arrays),
+        in_specs=[inside] * 4,
+        out_specs=(inside,) * 4,
+    )(*arrays)
+
+
 def local(section_input, conv_weight, head_weight, output_weight, cotangent):
-    activity = jax.nn.gelu(section_input[0].astype(F32), approximate=True).astype(BF16)
-    bins = activity.reshape(128, 2, 2, 4, 160)
-    at = bins.transpose(3, 1, 2, 4, 0).reshape(4, 2, 320, 128)
-    edges = jnp.stack([bins[0], bins[127]]).transpose(0, 3, 1, 2, 4).reshape(2, 4, 2, 320)
-    edges = jnp.pad(edges, ((0, 0), (0, 0), (0, 14), (0, 64)))
-    cw = conv_weight.transpose(1, 0, 2)
-    heads = head_weight.reshape(96, 3, 2, 192)
-    wp = jnp.stack([heads[:, 1], heads[:, 2], heads[:, 0], output_weight.reshape(96, 2, 192)], axis=2)
-    wp = wp.reshape(2, 48, 2, 2, 384).transpose(2, 0, 3, 1, 4).reshape(2, 4, 48, 384)
-    block_out, conv_grad, head_grad, output_grad = main_call(at, edges, cw, wp, cotangent[0])
-    return (block_out[None], conv_grad, head_grad, output_grad)
+    block_out, conv_grad, head_grad, output_grad = finish(
+        *main_call(
+            section_input[0], conv_weight.transpose(1, 0, 2), head_weight.transpose(1, 0, 2), output_weight, cotangent[0]
+        )
+    )
+    return (block_out[None], conv_grad.transpose(1, 0, 2), head_grad.transpose(1, 0, 2), output_grad)
 
 
 def solution(mesh):

time: 140 us -> 124 us (0.89)
  local copies, waits for them, and re-layouts: 13.7 us -> 0 us
  other arithmetic: 1.67 us -> 0 us
    unnamed x12 -> x0, local copies, waits for them, and re-layouts: 5.69 us -> none
    convert_element_type x2 -> x0, local copies, waits for them, and re-layouts: 3.96 us -> none  [local(): section_input[0].astype(F32)]
    pallas_call x1, Pallas kernels: 123 us -> 121 us  [main_call(): pl.pallas_call(main_kernel, name='main', out_shape=(shape(128, 768), jax....]
    pallas_call x0 -> x1, Pallas kernels: none -> 1.97 us  [finish(): pl.pallas_call(finish_kernel, name='finish', out_shape=tuple((jax.ShapeDt...]
    transpose x2 -> x0, local copies, waits for them, and re-layouts: 1.63 us -> none  [the longest x1 0.89 us: local(): at = bins.transpose(3, 1, 2, 4, 0).reshape(4, 2, 320, 128)]
where the time goes in v5:
time: 124 us
  Pallas kernels  123 us (99%)
    pallas_call x1, Pallas kernels, main_call(): pl.pallas_call(main_kernel, name='main', out_shape=(shape(128, 768), jax....  121 us

profile of v5, /device:TPU:1, one launch (start us, length us, event | category | flops | bytes accessed | tf_op | source)
XLA Modules:
  0.0 123.6 jit_solution(7465736517829975512)
XLA Ops:
  0.6 121.0 %main.1 = (bf16[128,768]{1,0:T(8,128)(2,1)}, f32[5,20,768]{2,1,0:T(8,128)}, f32[3,24,384]{2,1,0:T(8,128)}, f32[24,384]{1,0:T(8,128)}) custom-call(bf16[256,1280]{1,0:T(8,128)(2,1)} %bitcast.7, bf16[5,80,768]{2,1,0:T(8,128)(2,1)} %bitcast.8, bf16[3,96,384]{2,1,0:T(8,128)(2,1)} %bitcast.9, bf16[96,384]{1,0:T(8,128)(2,1)} %ow_ref.1, bf16[128,768]{1,0:T(8,128)(2,1)} %bitcast.10), custom_call_target="tpu_custom_call" | custom-call | tf_op jit(solution)/shard_map/main/pallas_call | solution.py:631
  121.7 2.0 %finish.1 = (bf16[128,768]{1,0:T(8,128)(2,1)}, f32[5,20,768]{2,1,0:T(8,128)}, f32[3,24,384]{2,1,0:T(8,128)}, f32[24,384]{1,0:T(8,128)}) custom-call(bf16[128,768]{1,0:T(8,128)(2,1)} %get-tuple-element.12.refs_0_, f32[5,20,768]{2,1,0:T(8,128)} %get-tuple-element.13.refs_1_, f32[3,24,384]{2,1,0:T(8,128)} %get-tuple-element.14.refs_2_, ...), custom_call_target="tpu_custom_call" | custom-call | tf_op jit(solution)/shard_map/finish/pallas_call | solution.py:660

commit v6 on v5

--- a/solution.py
+++ b/solution.py
@@ -138,10 +138,12 @@
 def main_kernel(
     input_ref, cw_ref, hw_ref, ow_ref, cot_ref,
     out_ref, conv_ref, head_ref, output_ref,
-    act_ref, at_ref, edge_ref, wp_ref, end_ref, xt_ref, low_ref, high_ref, cwf_ref, wf_ref, cots_ref, x5_ref, x5s_ref, part_ref, rs_ref, sec_ref, secs_ref,
-    inv_ref, nb_ref, nl_ref, cl_ref, kv_ref, st_ref, dp_ref, p16_ref, ds_ref, dkv_ref, buf_ref, sum_ref, dkvs_ref,
-    bo_ref, bos_ref, gpa_ref, gpas_ref, norm_ref, norms_ref, spread_ref, spreads_ref, hg_ref, hgs_ref, gp_ref, gps_ref,
-    hgo_ref, hgl_ref, cgf_ref, cgm_ref, cg_ref, cgs_ref, send, recv, local,
+    act_ref, at_ref, edge_ref, wp_ref, end_ref, xt_ref, low_ref, high_ref, cwf_ref, wf_ref, cots_ref,
+    x5_ref, x5t_ref, x5s_ref, part_ref, rs_ref, sec_ref, secs_ref, inv_ref, nb_ref, nl_ref, cl_ref,
+    kv_ref, st_ref, dp_ref, p16_ref, ds_ref, dkv_ref, buf_ref, sum_ref, dkvs_ref, bo_ref, bos_ref,
+    grads_ref, others_ref, norma_ref, normb_ref, normsa_ref, normsb_ref, spread_ref, spreads_ref,
+    hg_ref, hgs_ref, gpa_ref, gpb_ref, gpsa_ref, gpsb_ref, hgo_ref, hgl_ref, cgf_ref, cgm_ref,
+    cga_ref, cgb_ref, cgsa_ref, cgsb_ref, send, recv, local,
 ):
     p = Place()
     scale = HEAD_DIM ** (-0.5)
@@ -167,41 +169,12 @@
     moves.push(cw_ref, mine, p.sibling, first + 2)
     moves.keep(cw_ref, mine)
 
-    for head in range(2):
-        lanes = slice(192 * head, 192 * head + 192)
-        keys, values, queries = (hw_ref[n, :, lanes].astype(F32) for n in (1, 2, 0))
-        pairs = (jnp.concatenate([keys, values], axis=1), jnp.concatenate([queries, ow_ref[:, lanes].astype(F32)], axis=1))
-        for column in range(2):
-            for row in range(2):
-                wp_ref[head, 2 * row + column] = pairs[column][48 * row : 48 * row + 48].astype(BF16)
-
-    def quarter(zh, x, c, d):
-        rows = pl.ds(pl.multiple_of(48 * lax.div(d, 2), 16), 48)
-        columns = pl.ds(pl.multiple_of(384 * lax.rem(d, 2), 128), 384)
-        return wf_ref.at[zh, x, c, rows, columns]
-
-    def quarters(c, d):
-        rows = pl.ds(pl.multiple_of(48 * lax.div(d, 2), 16), 48)
-        columns = pl.ds(pl.multiple_of(384 * lax.rem(d, 2), 128), 384)
-        return wf_ref.at[:, :, c, rows, columns]
-
-    w = moves.slots(8)
-    shard = 4 * p.zh + p.x
-    own_quarter = quarter(p.zh, p.x, p.c, p.d)
-    quarter_arrivals = []
-    for k in range(8):
-        other = lax.rem(shard + k, 8)
-        zh, x = lax.div(other, 4), lax.rem(other, 4)
-        src = wp_ref.at[zh, p.d]
-        if k == 0:
-            copy = pltpu.make_async_copy(src, own_quarter, local.at[moves.used_local])
-            moves.used_local += 1
-            copy.start()
-            quarter_arrivals.append(copy.wait)
-        else:
-            moves.push(src, own_quarter, p.at(x=x, zh=zh), w + k)
-            other = lax.rem(shard + 8 - k, 8)
-            quarter_arrivals.append(arrival(quarter(lax.div(other, 4), lax.rem(other, 4), p.c, p.d), w + k))
+    a = moves.slots(8)
+    core = lax.div(p.x, 2)
+    slot = 2 * lax.rem(p.x, 2) + p.c
+
+    def half_rows(ref, index, half):
+        return ref.at[index, :, pl.ds(160 * half, 160), :]
 
     for n in range(10):
         lanes = slice(128 * n, 128 * n + 128)
@@ -218,17 +191,17 @@
                 spot = 160 * zh + begin % 160
                 at_ref[x, parity, spot : spot + end - begin] = turned[begin - 128 * n : end - 128 * n]
                 begin = end
-    a = moves.slots(4)
-    core = lax.div(p.x, 2)
-    slot = 2 * lax.rem(p.x, 2) + p.c
-    spot = xt_ref.at[slot]
-    for k in (2, 1, 3, 0):
-        x = p.along_x(k)
-        if k == 0:
-            moves.push(at_ref.at[x], spot, p.at(c=core), a, a + slot, core != p.c)
-            moves.keep(at_ref.at[x], spot, core == p.c)
-        else:
-            moves.push(at_ref.at[x], spot, p.at(x=x, c=core), a + k, a + slot)
+        if n % 5 == 4:
+            half = n // 5
+            spot = half_rows(xt_ref, slot, half)
+            for k in (2, 1, 3, 0):
+                x = p.along_x(k)
+                src = half_rows(at_ref, x, half)
+                if k == 0:
+                    moves.push(src, spot, p.at(c=core), a + 4 * half, a + 4 * half + slot, core != p.c)
+                    moves.keep(src, spot, core == p.c)
+                else:
+                    moves.push(src, spot, p.at(x=x, c=core), a + 4 * half + k, a + 4 * half + slot)
     base = 8 * p.zh + 4 * p.c
     halo = []
     for up, bound_ref in ((True, low_ref), (False, high_ref)):
@@ -255,6 +228,42 @@
         else:
             halo.append(arrival(bound_ref, e, jnp.logical_and(base != 12, base + 4 != p.s)))
 
+    for head in range(2):
+        lanes = slice(192 * head, 192 * head + 192)
+        keys, values, queries = (hw_ref[n, :, lanes].astype(F32) for n in (1, 2, 0))
+        pairs = (jnp.concatenate([keys, values], axis=1), jnp.concatenate([queries, ow_ref[:, lanes].astype(F32)], axis=1))
+        for column in range(2):
+            for row in range(2):
+                wp_ref[head, 2 * row + column] = pairs[column][48 * row : 48 * row + 48].astype(BF16)
+
+    def quarter(zh, x, c, d):
+        rows = pl.ds(pl.multiple_of(48 * lax.div(d, 2), 16), 48)
+        columns = pl.ds(pl.multiple_of(384 * lax.rem(d, 2), 128), 384)
+        return wf_ref.at[zh, x, c, rows, columns]
+
+    def quarters(c, d):
+        rows = pl.ds(pl.multiple_of(48 * lax.div(d, 2), 16), 48)
+        columns = pl.ds(pl.multiple_of(384 * lax.rem(d, 2), 128), 384)
+        return wf_ref.at[:, :, c, rows, columns]
+
+    w = moves.slots(8)
+    shard = 4 * p.zh + p.x
+    own_quarter = quarter(p.zh, p.x, p.c, p.d)
+    quarter_arrivals = []
+    for k in range(8):
+        other = lax.rem(shard + k, 8)
+        zh, x = lax.div(other, 4), lax.rem(other, 4)
+        src = wp_ref.at[zh, p.d]
+        if k == 0:
+            copy = pltpu.make_async_copy(src, own_quarter, local.at[moves.used_local])
+            moves.used_local += 1
+            copy.start()
+            quarter_arrivals.append(copy.wait)
+        else:
+            moves.push(src, own_quarter, p.at(x=x, zh=zh), w + k)
+            other = lax.rem(shard + 8 - k, 8)
+            quarter_arrivals.append(arrival(quarter(lax.div(other, 4), lax.rem(other, 4), p.c, p.d), w + k))
+
     moves.arrival(fifth(other_half, p.c, p.d), first)()
     got = fifth(other_half, p.c, p.d)
     for k in (2, 1, 3):
@@ -276,7 +285,8 @@
 
     for n in range(4):
         x, c = 2 * p.c + n // 2, n % 2
-        arrival(xt_ref.at[n], a + n, jnp.logical_or(x != p.x, c != p.c))()
+        for half in range(2):
+            arrival(half_rows(xt_ref, n, half), a + 4 * half + n, jnp.logical_or(x != p.x, c != p.c))()
     for wait in halo:
         wait()
     for when, wait in moves.locals:
@@ -308,31 +318,36 @@
     arrival(fifth(other_half, 1 - p.c, 4), first + 7)()
     for k in (1, 3, 2):
         arrival(fifth(other_half, 1 - p.c, p.along_y(4 - k)), first + 7 + k)()
-    b = moves.slots(4)
-    for half in range(2):
-        conv = dot(x5_ref[:, 256 * half : 256 * half + 256], cwf_ref[...].reshape(1600, 768), TN) * 0.5
-        for n in range(2):
-            slot = 2 * half + n
-            part_ref[slot] = conv[128 * n : 128 * n + 128].astype(BF16)
-            x = 2 * p.c + half
-            alone = jnp.logical_and(x == p.x, n == p.c)
-            moves.push(part_ref.at[slot], rs_ref.at[p.x], p.at(x=x, c=n), b + slot, b + p.x, jnp.logical_not(alone))
-            moves.keep(part_ref.at[slot], rs_ref.at[p.x], alone)
+    x5t_ref[...] = x5_ref[...].T
+    b = moves.slots(8)
+    pieces = ((0, 512), (512, 256))
+    for piece, (lower, width) in enumerate(pieces):
+        lanes = pl.ds(lower, width)
+        conv = dot(x5t_ref[...], cwf_ref[:, :, :, lanes].reshape(1600, width), NN) * 0.5
+        for slot in range(4):
+            part_ref[slot, :, lanes] = conv[128 * slot : 128 * slot + 128].astype(BF16)
+            x, c = 2 * p.c + slot // 2, slot % 2
+            alone = jnp.logical_and(x == p.x, c == p.c)
+            src, dst = part_ref.at[slot, :, lanes], rs_ref.at[p.x, :, lanes]
+            moves.push(src, dst, p.at(x=x, c=c), b + 4 * piece + slot, b + 4 * piece + p.x, jnp.logical_not(alone))
+            moves.keep(src, dst, alone)
     other_x5 = moves.slots(1)
     moves.push(x5_ref, x5s_ref, p.sibling, other_x5)
-    for x in range(4):
-        arrival(rs_ref.at[x], b + x, jnp.logical_or(p.x != x, core != p.c))()
     for when, wait in moves.locals:
         under(when, wait)
     moves.locals = []
-    total = rs_ref[0].astype(F32)
-    for x in range(1, 4):
-        total = total + rs_ref[x].astype(F32)
-    sec_ref[...] = total.astype(BF16)
-    secs_ref[p.z] = total.astype(BF16)
-    g = moves.slots(4)
-    for k in (2, 1, 3):
-        moves.push(sec_ref, secs_ref.at[p.z], p.at_z(p.along_z(k)), g + k)
+    g = moves.slots(8)
+    for piece, (lower, width) in enumerate(pieces):
+        lanes = pl.ds(lower, width)
+        for x in range(4):
+            arrival(rs_ref.at[x, :, lanes], b + 4 * piece + x, jnp.logical_or(p.x != x, core != p.c))()
+        total = rs_ref[0, :, lanes].astype(F32)
+        for x in range(1, 4):
+            total = total + rs_ref[x, :, lanes].astype(F32)
+        sec_ref[:, lanes] = total.astype(BF16)
+        secs_ref[p.z, :, lanes] = total.astype(BF16)
+        for k in (2, 1, 3):
+            moves.push(sec_ref.at[:, lanes], secs_ref.at[p.z, :, lanes], p.at_z(p.along_z(k)), g + 4 * piece + k)
 
     for k in (1, 3, 2):
         d = p.along_y(4 - k)
@@ -354,7 +369,8 @@
     wide_lane = lax.broadcasted_iota(jnp.int32, (256, 256), 1)
 
     for k in (2, 1, 3):
-        arrival(secs_ref.at[p.along_z(4 - k)], g + k)()
+        for piece, (lower, width) in enumerate(pieces):
+            arrival(secs_ref.at[p.along_z(4 - k), :, pl.ds(lower, width)], g + 4 * piece + k)()
     cot_first = moves.slots(4)
     cot_own = pltpu.make_async_copy(cot_ref, cots_ref.at[p.z], local.at[moves.used_local])
     moves.used_local += 1
@@ -446,9 +462,11 @@
     attended = jnp.where(wide_lane < 64, 0.0, attended).astype(BF16)
     grad_query = dot(ds_ref[...].reshape(2048, 256), rows8(kv_ref, 0, 256), TN) * scale
     grad_query = jnp.where(wide_lane < 192, grad_query, 0.0).astype(BF16)
-    gpa_ref[:, 384:512] = grad_query[:, :128]
-    gpa_ref[:, 512:640] = grad_query[:, 128:] + attended[:, :128]
-    gpa_ref[:, 640:] = attended[:, 128:]
+    grads_ref[0, :, :128] = grad_query[:, :128]
+    grads_ref[0, :, 128:256] = grad_query[:, 128:] + attended[:, :128]
+    grads_ref[0, :, 256:] = attended[:, 128:]
+    h = moves.slots(12)
+    moves.push(grads_ref.at[0], others_ref.at[0], p.sibling, h)
     u = moves.slots(4)
     for t in range(2):
         block = dot(attended, output_rows(t), NT).astype(BF16)
@@ -459,51 +477,130 @@
         moves.push(bo_ref.at[z], bos_ref.at[p.z], p.at_z(z), u + k)
     bos_ref[p.z] = bo_ref[p.z]
 
+    def share_rows(part, values):
+        for n in range(8):
+            for d in range(4):
+                row = 96 * n + 24 * d
+                hg_ref[part, d, n] = values[row : row + 24].astype(BF16)
+        for k in (2, 1, 3):
+            d = p.along_y(k)
+            moves.push(hg_ref.at[part, d], hgs_ref.at[part, p.d], p.at(d=d), h + 4 + 4 * part + k)
+        hgs_ref[part, p.d] = hg_ref[part, p.d]
+
+    def all_bins(part):
+        return jnp.concatenate([grads_ref[part], others_ref[part]], axis=0)
+
+    for n in range(4):
+        arrival((cl_ref if n < 2 else nl_ref).at[2 + n % 2], o + n)()
+    arrival(others_ref.at[0], h)()
+    grads = all_bins(0)
+    head_part = dot(nl_ref[...].reshape(512, 768), grads[:, :256], TN)
+    output_part = dot(cl_ref[...].reshape(512, 768), grads[:, 128:], TN)
+    tile_lane = lax.broadcasted_iota(jnp.int32, (768, 128), 1)
+    middle = jnp.where(tile_lane < 64, head_part[:, 128:], output_part[:, :128])
+    share_rows(0, jnp.concatenate([head_part[:, :128], middle, output_part[:, 128:]], axis=1))
+
     for k in (1, 3, 2):
         arrival(dkvs_ref.at[p.along_x(4 - k)], r + 4 + k)()
     total = dkvs_ref[0].astype(F32)
     for x in range(1, 4):
         total = total + dkvs_ref[x].astype(F32)
     grad_kv = total.astype(BF16)
-    gpa_ref[:, :384] = grad_kv
-    h = moves.slots(5)
-    moves.push(gpa_ref, gpas_ref, p.sibling, h)
+    grads_ref[1] = grad_kv
+    moves.push(grads_ref.at[1], others_ref.at[1], p.sibling, h + 1)
     grad_proj = jnp.concatenate([grad_kv, grad_query], axis=1)
     spread = jnp.zeros((256, 1), F32)
     for t in range(2):
         block = dot(grad_proj, kv_rows(t), NT)
         spread = spread + jnp.sum(block * channels(secs_ref, t).astype(F32), axis=1, keepdims=True)
         rounded = block.astype(BF16)
-        norm_ref[t] = rounded[:128]
-        norm_ref[2 + t] = rounded[128:]
+        for zh in range(2):
+            rows = slice(128 * zh, 128 * zh + 128)
+            for c in range(2):
+                norma_ref[2 * zh + t, :, 128 * c : 128 * c + 128] = rounded[rows, 384 * c : 384 * c + 128]
+                normb_ref[2 * zh + t, :, 256 * c : 256 * c + 256] = rounded[rows, 384 * c + 128 : 384 * c + 384]
     spread = spread * (1.0 / 1536)
     for zh in range(2):
         spread_ref[zh] = jnp.broadcast_to(spread[128 * zh : 128 * zh + 128], (128, 128)).T[:8]
-    m = moves.slots(8)
+    m = moves.slots(12)
     for k in (2, 1, 3):
         z = p.along_z(k)
-        moves.push(norm_ref.at[z], norms_ref.at[p.z], p.at_z(z), m + k)
-        moves.push(spread_ref.at[lax.div(z, 2)], spreads_ref.at[p.z], p.at_z(z), m + 4 + k)
-    norms_ref[p.z] = norm_ref[p.z]
+        moves.push(spread_ref.at[lax.div(z, 2)], spreads_ref.at[p.z], p.at_z(z), m + 8 + k)
+        moves.push(norma_ref.at[z], normsa_ref.at[p.z], p.at_z(z), m + k)
+    normsa_ref[p.z] = norma_ref[p.z]
+    normsb_ref[p.z] = normb_ref[p.z]
     spreads_ref[p.z] = spread_ref[p.zh]
-
-    for n in range(4):
-        arrival((cl_ref if n < 2 else nl_ref).at[2 + n % 2], o + n)()
-    arrival(gpas_ref, h)()
-    grads = jnp.concatenate([gpa_ref[...], gpas_ref[...]], axis=0)
-    head_part = dot(nl_ref[...].reshape(512, 768), grads[:, :640], TN)
-    output_part = dot(cl_ref[...].reshape(512, 768), grads[:, 512:], TN)
-    tile_lane = lax.broadcasted_iota(jnp.int32, (768, 128), 1)
-    middle = jnp.where(tile_lane < 64, head_part[:, 512:], output_part[:, :128])
-    parts = jnp.concatenate([head_part[:, :512], middle, output_part[:, 128:]], axis=1)
-    for n in range(8):
-        for d in range(4):
-            row = 96 * n + 24 * d
-            hg_ref[d, n] = parts[row : row + 24].astype(BF16)
+    for k in (1, 3, 2):
+        arrival(normsa_ref.at[p.along_z(4 - k)], m + k)()
+        arrival(spreads_ref.at[p.along_z(4 - k)], m + 8 + k)()
     for k in (2, 1, 3):
-        d = p.along_y(k)
-        moves.push(hg_ref.at[d], hgs_ref.at[p.d], p.at(d=d), h + 1 + k)
-    hgs_ref[p.d] = hg_ref[p.d]
+        z = p.along_z(k)
+        moves.push(normb_ref.at[z], normsb_ref.at[p.z], p.at_z(z), m + 4 + k)
+
+    mean = spreads_ref[0]
+    for z in range(1, 4):
+        mean = mean + spreads_ref[z]
+    mean = jnp.concatenate([mean] * 16, axis=0).T[:, :1]
+    inverse = inv_ref[p.zh][:, :1]
+    factor = inverse * inverse * inverse * mean
+    block = 2 * p.x + p.c
+    j = moves.slots(16)
+
+    def pool(norms, gp, gps, lower, width):
+        for c in range(2):
+            lanes = pl.ds(384 * c + lower, width)
+            here = pl.ds(width * c, width)
+            grad_normed = norms[0, :, here].astype(F32)
+            for z in range(1, 4):
+                grad_normed = grad_normed + norms[z, :, here].astype(F32)
+            grad_section = cots_ref[p.z, :, lanes].astype(F32) + inverse * grad_normed
+            grad_section = grad_section - factor * sec_ref[:, lanes].astype(F32)
+            gp[c] = (0.5 * grad_section).astype(BF16)
+        gps[block] = gp[p.c]
+
+    def pool_sends(gp, gps, first):
+        for k in (4, 5, 2, 3, 6, 7, 1):
+            other = lax.rem(block + k, 8)
+            x, c = lax.div(other, 2), lax.rem(other, 2)
+            moves.push(gp.at[c], gps.at[block], p.at(x=x, c=c), first + k)
+
+    def pool_arrivals(gps, first):
+        for k in (1, 7, 6, 2, 3, 4, 5):
+            arrival(gps.at[lax.rem(block + 8 - k, 8)], first + k)()
+
+    pool(normsa_ref, gpa_ref, gpsa_ref, 0, 128)
+    pool_sends(gpa_ref, gpsa_ref, j)
+    arrival(others_ref.at[1], h + 1)()
+    share_rows(1, dot(nl_ref[...].reshape(512, 768), all_bins(1), TN))
+    for k in (1, 3, 2):
+        arrival(normsb_ref.at[p.along_z(4 - k)], m + 4 + k)()
+    pool(normsb_ref, gpb_ref, gpsb_ref, 128, 256)
+    pool_arrivals(gpsa_ref, j)
+    pool_sends(gpb_ref, gpsb_ref, j + 8)
+
+    arrival(x5s_ref, other_x5)()
+    e = moves.slots(32)
+    me = 8 * p.zh + 4 * p.c + p.d
+
+    def conv_grad(gps, cg, cgs, lower, width, first):
+        here = gps[pl.ds(4 * p.c, 4)].reshape(512, width)
+        there = gps[pl.ds(4 - 4 * p.c, 4)].reshape(512, width)
+        cgf_ref[:, lower : lower + width] = dot(x5_ref[...], here, NN) + dot(x5s_ref[...], there, NN)
+        for n in range(16):
+            for tap in range(5):
+                cgm_ref[n % 2, pl.ds(20 * tap, 20), lower : lower + width] = cgf_ref[
+                    pl.ds(320 * tap + 20 * n, 20), lower : lower + width
+                ]
+            cg[n] = cgm_ref[n % 2, :, lower : lower + width].astype(BF16)
+        for k in (10, 14, 2, 6, 8, 12, 4, 9, 11, 13, 15, 1, 3, 5, 7):
+            other = lax.rem(me + k, 16)
+            zh, c, d = lax.div(other, 8), lax.rem(lax.div(other, 4), 2), lax.rem(other, 4)
+            moves.push(cg.at[other], cgs.at[me], p.at(zh=zh, c=c, d=d), first + k)
+        cgs[me] = cg[me]
+
+    conv_grad(gpsa_ref, cga_ref, cgsa_ref, 0, 128, e)
+    pool_arrivals(gpsb_ref, j + 8)
+    conv_grad(gpsb_ref, cgb_ref, cgsb_ref, 128, 256, e + 16)
 
     for k in (1, 3, 2):
         arrival(bos_ref.at[p.along_z(4 - k)], u + k)()
@@ -513,37 +610,17 @@
         projected_out = projected_out + bos_ref[z].astype(F32)
     out_ref[...] = (total + projected_out).astype(BF16)
 
-    for k in (1, 3, 2):
-        arrival(norms_ref.at[p.along_z(4 - k)], m + k)()
-        arrival(spreads_ref.at[p.along_z(4 - k)], m + 4 + k)()
-    grad_normed = norms_ref[0].astype(F32)
-    mean = spreads_ref[0]
-    for z in range(1, 4):
-        grad_normed = grad_normed + norms_ref[z].astype(F32)
-        mean = mean + spreads_ref[z]
-    mean = jnp.concatenate([mean] * 16, axis=0).T[:, :1]
-    inverse = inv_ref[p.zh][:, :1]
-    grad_section = cots_ref[p.z].astype(F32) + inverse * grad_normed - inverse * inverse * inverse * total * mean
-    grad_pool = (0.5 * grad_section).astype(BF16)
-    gp_ref[0] = grad_pool[:, :384]
-    gp_ref[1] = grad_pool[:, 384:]
-    j = moves.slots(8)
-    block = 2 * p.x + p.c
-    for k in (4, 5, 2, 3, 6, 7, 1):
-        other = lax.rem(block + k, 8)
-        x, c = lax.div(other, 2), lax.rem(other, 2)
-        moves.push(gp_ref.at[c], gps_ref.at[block], p.at(x=x, c=c), j + k)
-    gps_ref[block] = gp_ref[p.c]
-    for k in (1, 3, 2):
-        arrival(hgs_ref.at[p.along_y(4 - k)], h + 1 + k)()
-    rows = hgs_ref[0].astype(F32)
-    for d in range(1, 4):
-        rows = rows + hgs_ref[d].astype(F32)
-    rows = rows.astype(BF16)
     f = moves.slots(8)
-    for n in range(8):
-        hgo_ref[n // 2, n % 2] = rows[n]
-    alone = []
+    for part in range(2):
+        for k in (1, 3, 2):
+            arrival(hgs_ref.at[part, p.along_y(4 - k)], h + 4 + 4 * part + k)()
+        rows = hgs_ref[part, 0].astype(F32)
+        for d in range(1, 4):
+            rows = rows + hgs_ref[part, d].astype(F32)
+        rows = rows.astype(BF16)
+        lanes = pl.ds(384 - 384 * part, 384)
+        for n in range(8):
+            hgo_ref[n // 2, n % 2, :, lanes] = rows[n]
     for k in (2, 3, 4, 5, 6, 7, 0, 1):
         other = lax.rem(2 * p.x + k, 8)
         x, c = lax.div(other, 2), lax.rem(other, 2)
@@ -554,24 +631,6 @@
             moves.keep(src, dst, alone)
         else:
             moves.push(src, dst, p.at(x=x, zh=p.c, c=c), f + k, f + 4 * p.zh + p.x)
-
-    arrival(x5s_ref, other_x5)()
-    for k in (1, 7, 6, 2, 3, 4, 5):
-        arrival(gps_ref.at[lax.rem(block + 8 - k, 8)], j + k)()
-    here = gps_ref[pl.ds(4 * p.c, 4)].reshape(512, 384)
-    there = gps_ref[pl.ds(4 - 4 * p.c, 4)].reshape(512, 384)
-    cgf_ref[...] = dot(x5_ref[...], here, NN) + dot(x5s_ref[...], there, NN)
-    for n in range(16):
-        for tap in range(5):
-            cgm_ref[n % 2, pl.ds(20 * tap, 20), :] = cgf_ref[pl.ds(320 * tap + 20 * n, 20), :]
-        cg_ref[n] = cgm_ref[n % 2].astype(BF16)
-    e = moves.slots(16)
-    me = 8 * p.zh + 4 * p.c + p.d
-    for k in (10, 14, 2, 6, 8, 12, 4, 9, 11, 13, 15, 1, 3, 5, 7):
-        other = lax.rem(me + k, 16)
-        zh, c, d = lax.div(other, 8), lax.rem(lax.div(other, 4), 2), lax.rem(other, 4)
-        moves.push(cg_ref.at[other], cgs_ref.at[me], p.at(zh=zh, c=c, d=d), e + k)
-    cgs_ref[me] = cg_ref[me]
     for zh in range(2):
         for x in range(4):
             alone = jnp.logical_and(jnp.logical_and(x == p.x, zh == p.zh), p.zh == p.c)
@@ -591,17 +650,19 @@
             head_ref[n] = piece
         else:
             output_ref[...] = piece
-    for k in (1, 2, 3, 4, 5, 6, 7, 8, 9, 10, 11, 12, 13, 14, 15):
-        arrival(cgs_ref.at[lax.rem(me + 16 - k, 16)], e + k)()
-    for c in range(2):
-        total = None
-        for zh in range(2):
-            for d in range(4):
-                part = cgs_ref[8 * zh + 4 * c + d].astype(F32)
-                total = part if total is None else total + part
-        cgm_ref[c] = total
-        for tap in range(5):
-            conv_ref[tap, :, 384 * c : 384 * c + 384] = cgm_ref[c, pl.ds(20 * tap, 20), :]
+    for cgs, lower, width, first in ((cgsa_ref, 0, 128, e), (cgsb_ref, 128, 256, e + 16)):
+        for k in range(1, 16):
+            arrival(cgs.at[lax.rem(me + 16 - k, 16)], first + k)()
+        for c in range(2):
+            total = None
+            for zh in range(2):
+                for d in range(4):
+                    part = cgs[8 * zh + 4 * c + d].astype(F32)
+                    total = part if total is None else total + part
+            lanes = slice(lower, lower + width)
+            cgm_ref[c, :, lanes] = total
+            for tap in range(5):
+                conv_ref[tap, :, 384 * c + lower : 384 * c + lower + width] = cgm_ref[c, pl.ds(20 * tap, 20), lanes]
     moves.settle()
 
 
@@ -614,19 +675,22 @@
 
     scratch = [
         vmem(10, 256, 128, dtype=F32), vmem(4, 2, 320, 128), vmem(2, 16, 1280), vmem(2, 4, 48, 384),
-        vmem(1280, 128, dtype=F32), vmem(4, 2, 320, 128), vmem(16, 1280), vmem(16, 1280), vmem(5, 4, 80, 768), vmem(2, 4, 2, 96, 768),
-        vmem(4, 128, 768), vmem(1600, 512), vmem(1600, 512), vmem(4, 128, 768), vmem(4, 128, 768),
-        vmem(128, 768), vmem(4, 128, 768),
-        vmem(2, 128, 128, dtype=F32), vmem(4, 128, 768), vmem(4, 128, 768), vmem(4, 128, 768),
+        vmem(1280, 128, dtype=F32), vmem(4, 2, 320, 128), vmem(16, 1280), vmem(16, 1280),
+        vmem(5, 4, 80, 768), vmem(2, 4, 2, 96, 768), vmem(4, 128, 768),
+        vmem(1600, 512), vmem(512, 1600), vmem(1600, 512), vmem(4, 128, 768), vmem(4, 128, 768),
+        vmem(128, 768), vmem(4, 128, 768), vmem(2, 128, 128, dtype=F32),
+        vmem(4, 128, 768), vmem(4, 128, 768), vmem(4, 128, 768),
         vmem(2, 4, 256, 384), vmem(8, 256, 256, dtype=F32), vmem(8, 256, 256, dtype=F32),
         vmem(8, 256, 256), vmem(8, 256, 256), vmem(4, 256, 384), vmem(4, 256, 384), vmem(4, 256, 384),
-        vmem(4, 256, 384),
-        vmem(4, 128, 768), vmem(4, 128, 768), vmem(256, 768), vmem(256, 768), vmem(4, 128, 768), vmem(4, 128, 768),
+        vmem(4, 256, 384), vmem(4, 128, 768), vmem(4, 128, 768),
+        vmem(2, 256, 384), vmem(2, 256, 384),
+        vmem(4, 128, 256), vmem(4, 128, 512), vmem(4, 128, 256), vmem(4, 128, 512),
         vmem(2, 8, 128, dtype=F32), vmem(4, 8, 128, dtype=F32),
-        vmem(4, 8, 24, 768), vmem(4, 8, 24, 768), vmem(2, 128, 384), vmem(8, 128, 384),
+        vmem(2, 4, 8, 24, 384), vmem(2, 4, 8, 24, 384),
+        vmem(2, 128, 128), vmem(2, 128, 256), vmem(8, 128, 128), vmem(8, 128, 256),
         vmem(4, 2, 24, 768), vmem(2, 4, 24, 768), vmem(1600, 384, dtype=F32), vmem(2, 104, 384, dtype=F32),
-        vmem(16, 104, 384), vmem(16, 104, 384),
-        pltpu.SemaphoreType.DMA((144,)), pltpu.SemaphoreType.DMA((144,)), pltpu.SemaphoreType.DMA((16,)),
+        vmem(16, 104, 128), vmem(16, 104, 256), vmem(16, 104, 128), vmem(16, 104, 256),
+        pltpu.SemaphoreType.DMA((192,)), pltpu.SemaphoreType.DMA((192,)), pltpu.SemaphoreType.DMA((24,)),
     ]
     return pl.pallas_call(
         main_kernel,

time: 124 us -> 118 us (0.952)
  Pallas kernels: 123 us -> 117 us
    pallas_call x1, Pallas kernels: 121 us -> 115 us  [main_call(): pl.pallas_call(main_kernel, name='main', out_shape=(shape(128, 768), jax....]
where the time goes in v6:
time: 118 us
  Pallas kernels  117 us (99%)
    pallas_call x1, Pallas kernels, main_call(): pl.pallas_call(main_kernel, name='main', out_shape=(shape(128, 768), jax....  115 us

profile of v6, /device:TPU:1, one launch (start us, length us, event | category | flops | bytes accessed | tf_op | source)
XLA Modules:
  0.0 117.8 jit_solution(2766428542125585035)
XLA Ops:
  0.6 115.2 %main.1 = (bf16[128,768]{1,0:T(8,128)(2,1)}, f32[5,20,768]{2,1,0:T(8,128)}, f32[3,24,384]{2,1,0:T(8,128)}, f32[24,384]{1,0:T(8,128)}) custom-call(bf16[256,1280]{1,0:T(8,128)(2,1)} %bitcast.7, bf16[5,80,768]{2,1,0:T(8,128)(2,1)} %bitcast.8, bf16[3,96,384]{2,1,0:T(8,128)(2,1)} %bitcast.9, bf16[96,384]{1,0:T(8,128)(2,1)} %ow_ref.1, bf16[128,768]{1,0:T(8,128)(2,1)} %bitcast.10), custom_call_target="tpu_custom_call" | custom-call | tf_op jit(solution)/shard_map/main/pallas_call | solution.py:695
  115.9 2.0 %finish.1 = (bf16[128,768]{1,0:T(8,128)(2,1)}, f32[5,20,768]{2,1,0:T(8,128)}, f32[3,24,384]{2,1,0:T(8,128)}, f32[24,384]{1,0:T(8,128)}) custom-call(bf16[128,768]{1,0:T(8,128)(2,1)} %get-tuple-element.12.refs_0_, f32[5,20,768]{2,1,0:T(8,128)} %get-tuple-element.13.refs_1_, f32[3,24,384]{2,1,0:T(8,128)} %get-tuple-element.14.refs_2_, ...), custom_call_target="tpu_custom_call" | custom-call | tf_op jit(solution)/shard_map/finish/pallas_call | solution.py:724

commit v7 on v6

--- a/solution.py
+++ b/solution.py
@@ -139,11 +139,11 @@
     input_ref, cw_ref, hw_ref, ow_ref, cot_ref,
     out_ref, conv_ref, head_ref, output_ref,
     act_ref, at_ref, edge_ref, wp_ref, end_ref, xt_ref, low_ref, high_ref, cwf_ref, wf_ref, cots_ref,
-    x5_ref, x5t_ref, x5s_ref, part_ref, rs_ref, sec_ref, secs_ref, inv_ref, nb_ref, nl_ref, cl_ref,
+    x5_ref, x5t_ref, x5s_ref, part_ref, rs_ref, sec_ref, secs_ref, inv_ref, nb_ref, nl_ref, nlt_ref, cl_ref,
     kv_ref, st_ref, dp_ref, p16_ref, ds_ref, dkv_ref, buf_ref, sum_ref, dkvs_ref, bo_ref, bos_ref,
     grads_ref, others_ref, norma_ref, normb_ref, normsa_ref, normsb_ref, spread_ref, spreads_ref,
-    hg_ref, hgs_ref, gpa_ref, gpb_ref, gpsa_ref, gpsb_ref, hgo_ref, hgl_ref, cgf_ref, cgm_ref,
-    cga_ref, cgb_ref, cgsa_ref, cgsb_ref, send, recv, local,
+    hg_ref, hgs_ref, gpa_ref, gpb_ref, gpc_ref, gpsa_ref, gpsb_ref, gpsc_ref, hgo_ref, hgl_ref, cgf_ref, cgm_ref,
+    cga_ref, cgb_ref, cgc_ref, cgsa_ref, cgsb_ref, cgsc_ref, send, recv, local,
 ):
     p = Place()
     scale = HEAD_DIM ** (-0.5)
@@ -398,6 +398,9 @@
     for zh in range(2):
         nl_ref[zh] = nb_ref[2 * zh + p.c]
         moves.push(nb_ref.at[2 * zh + 1 - p.c], nl_ref.at[2 + zh], p.sibling, o + 2 + zh)
+    for zh in range(2):
+        arrival(nl_ref.at[2 + zh], o + 2 + zh)()
+    nlt_ref[...] = nl_ref[...].reshape(512, 768).T
     for k in (1, 3, 2):
         spot = kv_ref.at[p.c, p.along_x(4 - k)]
         arrival(spot, q + k)()
@@ -490,11 +493,11 @@
     def all_bins(part):
         return jnp.concatenate([grads_ref[part], others_ref[part]], axis=0)
 
-    for n in range(4):
-        arrival((cl_ref if n < 2 else nl_ref).at[2 + n % 2], o + n)()
+    for zh in range(2):
+        arrival(cl_ref.at[2 + zh], o + zh)()
     arrival(others_ref.at[0], h)()
     grads = all_bins(0)
-    head_part = dot(nl_ref[...].reshape(512, 768), grads[:, :256], TN)
+    head_part = dot(nlt_ref[...], grads[:, :256], NN)
     output_part = dot(cl_ref[...].reshape(512, 768), grads[:, 128:], TN)
     tile_lane = lax.broadcasted_iota(jnp.int32, (768, 128), 1)
     middle = jnp.where(tile_lane < 64, head_part[:, 128:], output_part[:, :128])
@@ -527,15 +530,15 @@
         z = p.along_z(k)
         moves.push(spread_ref.at[lax.div(z, 2)], spreads_ref.at[p.z], p.at_z(z), m + 8 + k)
         moves.push(norma_ref.at[z], normsa_ref.at[p.z], p.at_z(z), m + k)
+    for k in (2, 1, 3):
+        z = p.along_z(k)
+        moves.push(normb_ref.at[z], normsb_ref.at[p.z], p.at_z(z), m + 4 + k)
     normsa_ref[p.z] = norma_ref[p.z]
     normsb_ref[p.z] = normb_ref[p.z]
     spreads_ref[p.z] = spread_ref[p.zh]
     for k in (1, 3, 2):
         arrival(normsa_ref.at[p.along_z(4 - k)], m + k)()
         arrival(spreads_ref.at[p.along_z(4 - k)], m + 8 + k)()
-    for k in (2, 1, 3):
-        z = p.along_z(k)
-        moves.push(normb_ref.at[z], normsb_ref.at[p.z], p.at_z(z), m + 4 + k)
 
     mean = spreads_ref[0]
     for z in range(1, 4):
@@ -544,12 +547,12 @@
     inverse = inv_ref[p.zh][:, :1]
     factor = inverse * inverse * inverse * mean
     block = 2 * p.x + p.c
-    j = moves.slots(16)
-
-    def pool(norms, gp, gps, lower, width):
+    j = moves.slots(24)
+
+    def pool(norms, gp, gps, lower, width, stride, offset):
         for c in range(2):
             lanes = pl.ds(384 * c + lower, width)
-            here = pl.ds(width * c, width)
+            here = pl.ds(stride * c + offset, width)
             grad_normed = norms[0, :, here].astype(F32)
             for z in range(1, 4):
                 grad_normed = grad_normed + norms[z, :, here].astype(F32)
@@ -568,18 +571,20 @@
         for k in (1, 7, 6, 2, 3, 4, 5):
             arrival(gps.at[lax.rem(block + 8 - k, 8)], first + k)()
 
-    pool(normsa_ref, gpa_ref, gpsa_ref, 0, 128)
+    pool(normsa_ref, gpa_ref, gpsa_ref, 0, 128, 128, 0)
     pool_sends(gpa_ref, gpsa_ref, j)
     arrival(others_ref.at[1], h + 1)()
-    share_rows(1, dot(nl_ref[...].reshape(512, 768), all_bins(1), TN))
+    share_rows(1, dot(nlt_ref[...], all_bins(1), NN))
     for k in (1, 3, 2):
         arrival(normsb_ref.at[p.along_z(4 - k)], m + 4 + k)()
-    pool(normsb_ref, gpb_ref, gpsb_ref, 128, 256)
+    pool(normsb_ref, gpb_ref, gpsb_ref, 128, 128, 256, 0)
+    pool_sends(gpb_ref, gpsb_ref, j + 8)
+    pool(normsb_ref, gpc_ref, gpsc_ref, 256, 128, 256, 128)
+    pool_sends(gpc_ref, gpsc_ref, j + 16)
     pool_arrivals(gpsa_ref, j)
-    pool_sends(gpb_ref, gpsb_ref, j + 8)
 
     arrival(x5s_ref, other_x5)()
-    e = moves.slots(32)
+    e = moves.slots(48)
     me = 8 * p.zh + 4 * p.c + p.d
 
     def conv_grad(gps, cg, cgs, lower, width, first):
@@ -600,7 +605,9 @@
 
     conv_grad(gpsa_ref, cga_ref, cgsa_ref, 0, 128, e)
     pool_arrivals(gpsb_ref, j + 8)
-    conv_grad(gpsb_ref, cgb_ref, cgsb_ref, 128, 256, e + 16)
+    conv_grad(gpsb_ref, cgb_ref, cgsb_ref, 128, 128, e + 16)
+    pool_arrivals(gpsc_ref, j + 16)
+    conv_grad(gpsc_ref, cgc_ref, cgsc_ref, 256, 128, e + 32)
 
     for k in (1, 3, 2):
         arrival(bos_ref.at[p.along_z(4 - k)], u + k)()
@@ -650,7 +657,11 @@
             head_ref[n] = piece
         else:
             output_ref[...] = piece
-    for cgs, lower, width, first in ((cgsa_ref, 0, 128, e), (cgsb_ref, 128, 256, e + 16)):
+    for cgs, lower, width, first in (
+        (cgsa_ref, 0, 128, e),
+        (cgsb_ref, 128, 128, e + 16),
+        (cgsc_ref, 256, 128, e + 32),
+    ):
         for k in range(1, 16):
             arrival(cgs.at[lax.rem(me + 16 - k, 16)], first + k)()
         for c in range(2):
@@ -679,7 +690,7 @@
         vmem(5, 4, 80, 768), vmem(2, 4, 2, 96, 768), vmem(4, 128, 768),
         vmem(1600, 512), vmem(512, 1600), vmem(1600, 512), vmem(4, 128, 768), vmem(4, 128, 768),
         vmem(128, 768), vmem(4, 128, 768), vmem(2, 128, 128, dtype=F32),
-        vmem(4, 128, 768), vmem(4, 128, 768), vmem(4, 128, 768),
+        vmem(4, 128, 768), vmem(4, 128, 768), vmem(768, 512), vmem(4, 128, 768),
         vmem(2, 4, 256, 384), vmem(8, 256, 256, dtype=F32), vmem(8, 256, 256, dtype=F32),
         vmem(8, 256, 256), vmem(8, 256, 256), vmem(4, 256, 384), vmem(4, 256, 384), vmem(4, 256, 384),
         vmem(4, 256, 384), vmem(4, 128, 768), vmem(4, 128, 768),
@@ -687,10 +698,12 @@
         vmem(4, 128, 256), vmem(4, 128, 512), vmem(4, 128, 256), vmem(4, 128, 512),
         vmem(2, 8, 128, dtype=F32), vmem(4, 8, 128, dtype=F32),
         vmem(2, 4, 8, 24, 384), vmem(2, 4, 8, 24, 384),
-        vmem(2, 128, 128), vmem(2, 128, 256), vmem(8, 128, 128), vmem(8, 128, 256),
+        vmem(2, 128, 128), vmem(2, 128, 128), vmem(2, 128, 128),
+        vmem(8, 128, 128), vmem(8, 128, 128), vmem(8, 128, 128),
         vmem(4, 2, 24, 768), vmem(2, 4, 24, 768), vmem(1600, 384, dtype=F32), vmem(2, 104, 384, dtype=F32),
-        vmem(16, 104, 128), vmem(16, 104, 256), vmem(16, 104, 128), vmem(16, 104, 256),
-        pltpu.SemaphoreType.DMA((192,)), pltpu.SemaphoreType.DMA((192,)), pltpu.SemaphoreType.DMA((24,)),
+        vmem(16, 104, 128), vmem(16, 104, 128), vmem(16, 104, 128),
+        vmem(16, 104, 128), vmem(16, 104, 128), vmem(16, 104, 128),
+        pltpu.SemaphoreType.DMA((200,)), pltpu.SemaphoreType.DMA((200,)), pltpu.SemaphoreType.DMA((24,)),
     ]
     return pl.pallas_call(
         main_kernel,

time: 118 us -> 114 us (0.966)
  Pallas kernels: 117 us -> 114 us
    pallas_call x1, Pallas kernels: 115 us -> 112 us  [main_call(): pl.pallas_call(main_kernel, name='main', out_shape=(shape(128, 768), jax....]
where the time goes in v7:
time: 114 us
  Pallas kernels  114 us (100%)
    pallas_call x1, Pallas kernels, main_call(): pl.pallas_call(main_kernel, name='main', out_shape=(shape(128, 768), jax....  112 us

profile of v7, /device:TPU:1, one launch (start us, length us, event | category | flops | bytes accessed | tf_op | source)
XLA Modules:
  0.0 114.3 jit_solution(16682308228718532105)
XLA Ops:
  0.6 111.7 %main.1 = (bf16[128,768]{1,0:T(8,128)(2,1)}, f32[5,20,768]{2,1,0:T(8,128)}, f32[3,24,384]{2,1,0:T(8,128)}, f32[24,384]{1,0:T(8,128)}) custom-call(bf16[256,1280]{1,0:T(8,128)(2,1)} %bitcast.7, bf16[5,80,768]{2,1,0:T(8,128)(2,1)} %bitcast.8, bf16[3,96,384]{2,1,0:T(8,128)(2,1)} %bitcast.9, bf16[96,384]{1,0:T(8,128)(2,1)} %ow_ref.1, bf16[128,768]{1,0:T(8,128)(2,1)} %bitcast.10), custom_call_target="tpu_custom_call" | custom-call | tf_op jit(solution)/shard_map/main/pallas_call | solution.py:708
  112.3 2.0 %finish.1 = (bf16[128,768]{1,0:T(8,128)(2,1)}, f32[5,20,768]{2,1,0:T(8,128)}, f32[3,24,384]{2,1,0:T(8,128)}, f32[24,384]{1,0:T(8,128)}) custom-call(bf16[128,768]{1,0:T(8,128)(2,1)} %get-tuple-element.12.refs_0_, f32[5,20,768]{2,1,0:T(8,128)} %get-tuple-element.13.refs_1_, f32[3,24,384]{2,1,0:T(8,128)} %get-tuple-element.14.refs_2_, ...), custom_call_target="tpu_custom_call" | custom-call | tf_op jit(solution)/shard_map/finish/pallas_call | solution.py:737
